TPU v7x, 512 devices: a whole 4x8x8 slice. The times are simulated.
512 devices in a mesh: dp: 128 (over y, z, core), mp: 4 (over x).
Axes of the slice: x: 4, y: 8, z: 8, core: 2. Of those that a mesh axis runs over, the one named last changes fastest.
Arguments:
- query_hidden: bfloat16 [4096, 32, 768], P('dp', None, 'mp'), may hold values from -6 to 6
- query_proj: bfloat16 [768, 128], P('mp'), may hold values from -0.21875 to 0.21875
- passages: bfloat16 [8192, 128, 128], P(('dp', 'mp')), may hold values from -6 to 6
- teacher: float32 [4096, 4, 64], P('dp'), may hold values from -8 to 8
- neg_blocks: int32 [4096, 4], P('dp'), may hold values from 0 to 127, all different within a row; in each aligned block of 32 rows (0 to 31, 32 to 63, ...) at most 2 rows name the same one
Outputs:
- kl_loss: float32 [4096], P('dp')
Inputs may be any that keep to these rules, and one draw needn't show every extreme that they name: `neg_blocks`: each query names 4 different blocks. Among the 32 queries of one dp index no block is named more than 2 times, and some block is named exactly 2 times.
All inputs are finite; a program needn't handle non-finite values.
Results may differ from a plain program's by a relative error of at most 0.0003.
Values may be sent and summed in bfloat16 or wider, within the bound.
No kernel may reach another device: no remote copies, remote signals or barrier semaphores. Data moves between devices by JAX's collectives and lax.ppermute only.
A program may use at most 64 MiB of HBM per device.

v0:
```python
import jax
import jax.numpy as jnp
from jax import lax
from jax.sharding import PartitionSpec as P

softness = 0.1


def unit_rows(values):
    return values * lax.rsqrt(jnp.sum(values * values, axis=-1, keepdims=True) + 1e-06)


def soft_scores(slot_rows, passage_vecs):
    slot_count = slot_rows.shape[0]
    block_size = 16
    padded_count = -(-slot_count // block_size) * block_size
    blocked = slot_rows.reshape(
        padded_count // block_size, block_size, slot_rows.shape[1], slot_rows.shape[2]
    )

    def block_scores(slot_block):
        sims = jnp.einsum(
            "sie,pje->sipj", slot_block, passage_vecs, preferred_element_type=jnp.float32
        )
        softened = softness * jnp.log(jnp.sum(jnp.exp(sims / softness), axis=-1))
        return jnp.sum(softened, axis=1)

    scored = lax.map(block_scores, blocked)
    return scored.reshape(padded_count, -1)


def per_device(query_hidden, query_proj, passages, teacher, neg_blocks):
    partial_sum = jnp.einsum(
        "qth,he->qte", query_hidden, query_proj, preferred_element_type=jnp.float32
    )
    passage_vecs = unit_rows(passages.astype(jnp.float32)).astype(jnp.bfloat16)
    dp_count = lax.axis_size("dp")
    query_count, pick_count = neg_blocks.shape
    embed_width = partial_sum.shape[2]
    row_count = query_count * pick_count
    capacity = max(2, -(-row_count // dp_count))
    slots_all = dp_count * capacity
    owners = neg_blocks.reshape(row_count)
    owner_hits = (owners[:, None] == jnp.arange(dp_count, dtype=jnp.int32)[None, :]).astype(
        jnp.int32
    )
    earlier = jnp.cumsum(owner_hits, axis=0) - owner_hits
    slot_rank = jnp.sum(earlier * owner_hits, axis=1)
    slot_ids = owners * capacity + slot_rank
    matches = (slot_ids[None, :] == jnp.arange(slots_all, dtype=jnp.int32)[:, None]).astype(
        jnp.int32
    )
    row_query = jnp.arange(row_count, dtype=jnp.int32) // pick_count
    source = jnp.sum(matches * row_query[None, :], axis=1)
    filled = jnp.sum(matches, axis=1)
    projected = lax.psum(partial_sum, "mp")
    query_vecs = unit_rows(projected).astype(jnp.bfloat16)
    tokens = query_vecs.shape[1]
    outgoing = query_vecs[source] * filled[:, None, None].astype(jnp.bfloat16)
    outgoing = outgoing.reshape(dp_count, capacity, tokens, embed_width)
    arrived_items = lax.all_to_all(outgoing, "dp", split_axis=0, concat_axis=0, tiled=True)
    dims_items = arrived_items.shape
    flat_items = arrived_items.reshape(dims_items[0] * dims_items[1], dims_items[2], dims_items[3])
    scores = soft_scores(flat_items, passage_vecs).reshape(dims_items[0], dims_items[1], -1)
    returned = lax.all_to_all(scores, "dp", split_axis=0, concat_axis=0, tiled=True)
    home_scores = returned.reshape(slots_all, -1)[slot_ids].reshape(query_count, pick_count, -1)
    teacher_logp = teacher - jnp.log(jnp.sum(jnp.exp(teacher), axis=(1, 2), keepdims=True))
    student = lax.all_gather(home_scores, "mp", axis=2, tiled=True)
    kl_loss = jnp.sum(jnp.exp(teacher_logp) * (teacher_logp - student), axis=(1, 2)) + jnp.log(
        jnp.sum(jnp.exp(student), axis=(1, 2))
    )
    return kl_loss


def solution(mesh):
    in_specs = (
        P("dp", None, "mp"),
        P("mp", None),
        P(("dp", "mp"), None, None),
        P("dp", None, None),
        P("dp", None),
    )
    out_specs = P("dp")
    return jax.shard_map(
        per_device, mesh=mesh, in_specs=in_specs, out_specs=out_specs, check_vma=False
    )
```

profile of v0, /device:TPU:6, one launch (start us, length us, event | category | flops | bytes accessed | tf_op | source)
XLA Modules:
  0.0 229.6 jit_solution(16609151651576874862)
XLA Ops:
  6.5 1.0 copy-done
  7.6 1.9 fusion.7
  9.5 0.8 copy.19
  10.5 0.2 reduce_window_sum.11
  10.6 0.2 select_reduce_fusion.1
  10.8 0.2 convert_reduce_fusion
  11.0 0.2 convert_element_type.30
  11.2 56.0 %all-reduce.2.cloned.1.call-done = f32[32,32,128]{2,1,0:T(8,128)} async-done(((f32[32,32,128]{2,1,0:T(8,128)}), f32[32,32,128]{2,1,0:T(8,128)}) %all-reduce.2.cloned.1.call-update) | async-done | bytes 524304 | tf_op jit(solution)/shard_map/psum | solution.py:56
  67.2 1.2 multiply_reduce_fusion.1
  68.5 1.2 multiply_convert_fusion
  69.7 1.0 gather_fusion
  70.7 1.7 broadcast_multiply_fusion
  72.4 14.6 %all-to-all-start = ((bf16[128,2,32,128]{3,2,1,0:T(8,128)(2,1)}), bf16[128,2,32,128]{3,2,1,0:T(8,128)(2,1)S(1)}, u32[]{:S(2)}, u32[]{:S(2)}) async-start(bf16[128,2,32,128]{3,2,1,0:T(8,128)(2,1)} %broadcast_multiply_fusion), calls=%async_computation | async-start | bytes 4194304 | tf_op jit(solution)/shard_map/all_to_all | solution.py:61
  87.3 0.3 exponential_reduce_fusion.2
  87.6 0.3 fusion.4
  88.0 1.1 fusion.5
  89.1 50.3 %all-to-all-done = bf16[128,2,32,128]{3,2,1,0:T(8,128)(2,1)S(1)} async-done(((bf16[128,2,32,128]{3,2,1,0:T(8,128)(2,1)}), bf16[128,2,32,128]{3,2,1,0:T(8,128)(2,1)S(1)}, u32[]{:S(2)}, u32[]{:S(2)}) %all-to-all-start) | async-done | bytes 2097184 | tf_op jit(solution)/shard_map/all_to_all | solution.py:61
  139.4 49.7 %while.10 = (s32[]{:T(128)}, f32[16,16,16]{2,1,0:T(8,128)}, bf16[16,16,32,128]{3,2,1,0:T(8,128)(2,1)S(1)}, bf16[16,128,128]{2,1,0:T(8,128)(2,1)}, s32[]{:T(128)}) while((s32[]{:T(128)}, f32[16,16,16]{2,1,0:T(8,128)}, bf16[16,16,32,128]{3,2,1,0:T(8,128)(2,1)S(1)}, bf16[16,128,128]{2,1,0:T(8,128)(2,1)}, s32[]{:T(128)}) %tuple.25), condition=%wide.region_11.12_spmd, body=%wide.region_8.11_spmd.sunk | while | flops 270540544 | bytes 731713 | solution.py:28
  139.4 2.4 %exponential_reduce_fusion.4 = f32[16,32,16]{1,2,0:T(8,128)S(1)} fusion(bf16[16,128,128]{2,1,0:T(8,128)(2,1)} %get-tuple-element.78, bf16[16,16,32,128]{3,2,1,0:T(8,128)(2,1)S(1)} %get-tuple-element.77, s32[]{:T(128)} %get-tuple-element.70), kind=kOutput, calls=%fused_computation.2.clone.1 | convolution fusion | flops 270524416 | bytes 688132 | tf_op jit(solution)/shard_map/while/body/eval_jaxpr/sie,pje->sipj/dot_general | solution.py:22
  141.8 0.1 multiply_reduce_fusion.4
  141.9 0.6 bitcast_dynamic-update-slice_fusion.2
  142.5 2.4 %exponential_reduce_fusion.4 = f32[16,32,16]{1,2,0:T(8,128)S(1)} fusion(bf16[16,128,128]{2,1,0:T(8,128)(2,1)} %get-tuple-element.78, bf16[16,16,32,128]{3,2,1,0:T(8,128)(2,1)S(1)} %get-tuple-element.77, s32[]{:T(128)} %get-tuple-element.70), kind=kOutput, calls=%fused_computation.2.clone.1 | convolution fusion | flops 270524416 | bytes 688132 | tf_op jit(solution)/shard_map/while/body/eval_jaxpr/sie,pje->sipj/dot_general | solution.py:22
  144.9 0.1 multiply_reduce_fusion.4
  145.0 0.6 bitcast_dynamic-update-slice_fusion.2
  145.6 2.4 %exponential_reduce_fusion.4 = f32[16,32,16]{1,2,0:T(8,128)S(1)} fusion(bf16[16,128,128]{2,1,0:T(8,128)(2,1)} %get-tuple-element.78, bf16[16,16,32,128]{3,2,1,0:T(8,128)(2,1)S(1)} %get-tuple-element.77, s32[]{:T(128)} %get-tuple-element.70), kind=kOutput, calls=%fused_computation.2.clone.1 | convolution fusion | flops 270524416 | bytes 688132 | tf_op jit(solution)/shard_map/while/body/eval_jaxpr/sie,pje->sipj/dot_general | solution.py:22
  148.0 0.1 multiply_reduce_fusion.4
  148.1 0.6 bitcast_dynamic-update-slice_fusion.2
  148.7 2.4 %exponential_reduce_fusion.4 = f32[16,32,16]{1,2,0:T(8,128)S(1)} fusion(bf16[16,128,128]{2,1,0:T(8,128)(2,1)} %get-tuple-element.78, bf16[16,16,32,128]{3,2,1,0:T(8,128)(2,1)S(1)} %get-tuple-element.77, s32[]{:T(128)} %get-tuple-element.70), kind=kOutput, calls=%fused_computation.2.clone.1 | convolution fusion | flops 270524416 | bytes 688132 | tf_op jit(solution)/shard_map/while/body/eval_jaxpr/sie,pje->sipj/dot_general | solution.py:22
  151.1 0.1 multiply_reduce_fusion.4
  151.2 0.6 bitcast_dynamic-update-slice_fusion.2
  151.8 2.4 %exponential_reduce_fusion.4 = f32[16,32,16]{1,2,0:T(8,128)S(1)} fusion(bf16[16,128,128]{2,1,0:T(8,128)(2,1)} %get-tuple-element.78, bf16[16,16,32,128]{3,2,1,0:T(8,128)(2,1)S(1)} %get-tuple-element.77, s32[]{:T(128)} %get-tuple-element.70), kind=kOutput, calls=%fused_computation.2.clone.1 | convolution fusion | flops 270524416 | bytes 688132 | tf_op jit(solution)/shard_map/while/body/eval_jaxpr/sie,pje->sipj/dot_general | solution.py:22
  154.2 0.1 multiply_reduce_fusion.4
  154.3 0.6 bitcast_dynamic-update-slice_fusion.2
  154.9 2.4 %exponential_reduce_fusion.4 = f32[16,32,16]{1,2,0:T(8,128)S(1)} fusion(bf16[16,128,128]{2,1,0:T(8,128)(2,1)} %get-tuple-element.78, bf16[16,16,32,128]{3,2,1,0:T(8,128)(2,1)S(1)} %get-tuple-element.77, s32[]{:T(128)} %get-tuple-element.70), kind=kOutput, calls=%fused_computation.2.clone.1 | convolution fusion | flops 270524416 | bytes 688132 | tf_op jit(solution)/shard_map/while/body/eval_jaxpr/sie,pje->sipj/dot_general | solution.py:22
  157.3 0.1 multiply_reduce_fusion.4
  157.4 0.6 bitcast_dynamic-update-slice_fusion.2
  158.0 2.4 %exponential_reduce_fusion.4 = f32[16,32,16]{1,2,0:T(8,128)S(1)} fusion(bf16[16,128,128]{2,1,0:T(8,128)(2,1)} %get-tuple-element.78, bf16[16,16,32,128]{3,2,1,0:T(8,128)(2,1)S(1)} %get-tuple-element.77, s32[]{:T(128)} %get-tuple-element.70), kind=kOutput, calls=%fused_computation.2.clone.1 | convolution fusion | flops 270524416 | bytes 688132 | tf_op jit(solution)/shard_map/while/body/eval_jaxpr/sie,pje->sipj/dot_general | solution.py:22
  160.6 0.6 bitcast_dynamic-update-slice_fusion.2
  161.2 2.4 %exponential_reduce_fusion.4 = f32[16,32,16]{1,2,0:T(8,128)S(1)} fusion(bf16[16,128,128]{2,1,0:T(8,128)(2,1)} %get-tuple-element.78, bf16[16,16,32,128]{3,2,1,0:T(8,128)(2,1)S(1)} %get-tuple-element.77, s32[]{:T(128)} %get-tuple-element.70), kind=kOutput, calls=%fused_computation.2.clone.1 | convolution fusion | flops 270524416 | bytes 688132 | tf_op jit(solution)/shard_map/while/body/eval_jaxpr/sie,pje->sipj/dot_general | solution.py:22
  163.7 0.6 bitcast_dynamic-update-slice_fusion.2
  164.3 2.4 %exponential_reduce_fusion.4 = f32[16,32,16]{1,2,0:T(8,128)S(1)} fusion(bf16[16,128,128]{2,1,0:T(8,128)(2,1)} %get-tuple-element.78, bf16[16,16,32,128]{3,2,1,0:T(8,128)(2,1)S(1)} %get-tuple-element.77, s32[]{:T(128)} %get-tuple-element.70), kind=kOutput, calls=%fused_computation.2.clone.1 | convolution fusion | flops 270524416 | bytes 688132 | tf_op jit(solution)/shard_map/while/body/eval_jaxpr/sie,pje->sipj/dot_general | solution.py:22
  166.8 0.6 bitcast_dynamic-update-slice_fusion.2
  167.4 2.4 %exponential_reduce_fusion.4 = f32[16,32,16]{1,2,0:T(8,128)S(1)} fusion(bf16[16,128,128]{2,1,0:T(8,128)(2,1)} %get-tuple-element.78, bf16[16,16,32,128]{3,2,1,0:T(8,128)(2,1)S(1)} %get-tuple-element.77, s32[]{:T(128)} %get-tuple-element.70), kind=kOutput, calls=%fused_computation.2.clone.1 | convolution fusion | flops 270524416 | bytes 688132 | tf_op jit(solution)/shard_map/while/body/eval_jaxpr/sie,pje->sipj/dot_general | solution.py:22
  169.9 0.6 bitcast_dynamic-update-slice_fusion.2
  170.5 2.4 %exponential_reduce_fusion.4 = f32[16,32,16]{1,2,0:T(8,128)S(1)} fusion(bf16[16,128,128]{2,1,0:T(8,128)(2,1)} %get-tuple-element.78, bf16[16,16,32,128]{3,2,1,0:T(8,128)(2,1)S(1)} %get-tuple-element.77, s32[]{:T(128)} %get-tuple-element.70), kind=kOutput, calls=%fused_computation.2.clone.1 | convolution fusion | flops 270524416 | bytes 688132 | tf_op jit(solution)/shard_map/while/body/eval_jaxpr/sie,pje->sipj/dot_general | solution.py:22
  173.0 0.6 bitcast_dynamic-update-slice_fusion.2
  173.6 2.4 %exponential_reduce_fusion.4 = f32[16,32,16]{1,2,0:T(8,128)S(1)} fusion(bf16[16,128,128]{2,1,0:T(8,128)(2,1)} %get-tuple-element.78, bf16[16,16,32,128]{3,2,1,0:T(8,128)(2,1)S(1)} %get-tuple-element.77, s32[]{:T(128)} %get-tuple-element.70), kind=kOutput, calls=%fused_computation.2.clone.1 | convolution fusion | flops 270524416 | bytes 688132 | tf_op jit(solution)/shard_map/while/body/eval_jaxpr/sie,pje->sipj/dot_general | solution.py:22
  176.1 0.6 bitcast_dynamic-update-slice_fusion.2
  176.7 2.4 %exponential_reduce_fusion.4 = f32[16,32,16]{1,2,0:T(8,128)S(1)} fusion(bf16[16,128,128]{2,1,0:T(8,128)(2,1)} %get-tuple-element.78, bf16[16,16,32,128]{3,2,1,0:T(8,128)(2,1)S(1)} %get-tuple-element.77, s32[]{:T(128)} %get-tuple-element.70), kind=kOutput, calls=%fused_computation.2.clone.1 | convolution fusion | flops 270524416 | bytes 688132 | tf_op jit(solution)/shard_map/while/body/eval_jaxpr/sie,pje->sipj/dot_general | solution.py:22
  179.1 0.1 multiply_reduce_fusion.4
  179.2 0.6 bitcast_dynamic-update-slice_fusion.2
  179.8 2.4 %exponential_reduce_fusion.4 = f32[16,32,16]{1,2,0:T(8,128)S(1)} fusion(bf16[16,128,128]{2,1,0:T(8,128)(2,1)} %get-tuple-element.78, bf16[16,16,32,128]{3,2,1,0:T(8,128)(2,1)S(1)} %get-tuple-element.77, s32[]{:T(128)} %get-tuple-element.70), kind=kOutput, calls=%fused_computation.2.clone.1 | convolution fusion | flops 270524416 | bytes 688132 | tf_op jit(solution)/shard_map/while/body/eval_jaxpr/sie,pje->sipj/dot_general | solution.py:22
  182.2 0.1 multiply_reduce_fusion.4
  182.3 0.6 bitcast_dynamic-update-slice_fusion.2
  182.9 2.4 %exponential_reduce_fusion.4 = f32[16,32,16]{1,2,0:T(8,128)S(1)} fusion(bf16[16,128,128]{2,1,0:T(8,128)(2,1)} %get-tuple-element.78, bf16[16,16,32,128]{3,2,1,0:T(8,128)(2,1)S(1)} %get-tuple-element.77, s32[]{:T(128)} %get-tuple-element.70), kind=kOutput, calls=%fused_computation.2.clone.1 | convolution fusion | flops 270524416 | bytes 688132 | tf_op jit(solution)/shard_map/while/body/eval_jaxpr/sie,pje->sipj/dot_general | solution.py:22
  185.4 0.6 bitcast_dynamic-update-slice_fusion.2
  186.0 2.4 %exponential_reduce_fusion.4 = f32[16,32,16]{1,2,0:T(8,128)S(1)} fusion(bf16[16,128,128]{2,1,0:T(8,128)(2,1)} %get-tuple-element.78, bf16[16,16,32,128]{3,2,1,0:T(8,128)(2,1)S(1)} %get-tuple-element.77, s32[]{:T(128)} %get-tuple-element.70), kind=kOutput, calls=%fused_computation.2.clone.1 | convolution fusion | flops 270524416 | bytes 688132 | tf_op jit(solution)/shard_map/while/body/eval_jaxpr/sie,pje->sipj/dot_general | solution.py:22
  188.5 0.6 bitcast_dynamic-update-slice_fusion.2
  189.1 7.5 %all-to-all-start.1 = ((f32[128,2,16]{2,1,0:T(2,128)}), f32[128,2,16]{2,1,0:T(2,128)S(1)}, u32[]{:S(2)}, u32[]{:S(2)}) async-start(f32[128,2,16]{2,1,0:T(2,128)} %bitcast.10), calls=%async_computation.1 | async-start | bytes 262144 | tf_op jit(solution)/shard_map/all_to_all | solution.py:65
  196.7 12.3 %all-to-all-done.1 = f32[128,2,16]{2,1,0:T(2,128)S(1)} async-done(((f32[128,2,16]{2,1,0:T(2,128)}), f32[128,2,16]{2,1,0:T(2,128)S(1)}, u32[]{:S(2)}, u32[]{:S(2)}) %all-to-all-start.1) | async-done | bytes 16416 | tf_op jit(solution)/shard_map/all_to_all | solution.py:65
  209.0 0.6 gather_fusion.1
  209.7 12.2 %all_gather.3 = f32[32,4,64]{0,1,2:T(4,128)S(1)} all-gather(f32[32,4,16]{0,1,2:T(4,128)S(1)} %copy.21), channel_id=1, replica_groups=mesh['dp'=128,'mp'=4] {'mp'}, dimensions={2}, use_global_device_ids=true | all-gather | bytes 40960 | tf_op jit(solution)/shard_map/all_gather | solution.py:68
  222.0 0.2 multiply_reduce_fusion.2
  222.2 0.5 log_add_fusion
  (35 shorter events, 1.7 us)
Async XLA Ops:
  6.5 1.0 copy-start
  6.5 60.7 %all-reduce.2.cloned.1.call-start = ((), (), s32[]{:S(2)}) async-start(), calls=%async_computation.2 | async-start | bytes 1048576 | tf_op jit(solution)/shard_map/psum | solution.py:56
  72.4 14.7 %copy-start.3 = (s32[32,4]{0,1:T(4,128)S(1)}, s32[32,4]{0,1:T(4,128)}, u32[]{:S(2)}) copy-start(s32[32,4]{0,1:T(4,128)} %param.11) | copy-start | bytes 1540
  72.4 14.9 %copy-start.2 = (f32[32,4,64]{2,1,0:T(4,128)S(1)}, f32[32,4,64]{2,1,0:T(4,128)}, u32[]{:S(2)}) copy-start(f32[32,4,64]{2,1,0:T(4,128)} %param.10) | copy-start | bytes 98308
  72.4 15.2 %copy-start.1 = (bf16[16,128,128]{2,1,0:T(8,128)(2,1)S(1)}, bf16[16,128,128]{2,1,0:T(8,128)(2,1)}, u32[]{:S(2)}) copy-start(bf16[16,128,128]{2,1,0:T(8,128)(2,1)} %param.9) | copy-start | bytes 1572868
  72.4 67.0 %all-to-all-start = ((bf16[128,2,32,128]{3,2,1,0:T(8,128)(2,1)}), bf16[128,2,32,128]{3,2,1,0:T(8,128)(2,1)S(1)}, u32[]{:S(2)}, u32[]{:S(2)}) async-start(bf16[128,2,32,128]{3,2,1,0:T(8,128)(2,1)} %broadcast_multiply_fusion), calls=%async_computation | async-start | bytes 4194304 | tf_op jit(solution)/shard_map/all_to_all | solution.py:61
  189.1 19.8 %all-to-all-start.1 = ((f32[128,2,16]{2,1,0:T(2,128)}), f32[128,2,16]{2,1,0:T(2,128)S(1)}, u32[]{:S(2)}, u32[]{:S(2)}) async-start(f32[128,2,16]{2,1,0:T(2,128)} %bitcast.10), calls=%async_computation.1 | async-start | bytes 262144 | tf_op jit(solution)/shard_map/all_to_all | solution.py:65
Sparse Core Ops, SparseCore 0:
  9.7 57.4 all-reduce.1
where the time goes:
time: 231 us; the launch traced here: 230 us
  waiting for transfers between devices  119 us (52%)
  matrix products  39.9 us (17%)
  starting transfers between devices  22.2 us (10%)
  local copies, waits for them, and re-layouts  13.7 us (6%)
  between operations  13.6 us (6%)
  blocking collectives  12.2 us (5%)
  other arithmetic  9.3 us (4%)
    psum x1, waiting for transfers between devices, per_device(): projected = lax.psum(partial_sum, 'mp')  56 us
    all_to_all x1, waiting for transfers between devices, per_device(): lax.all_to_all(outgoing, 'dp', split_axis=0, concat_axis=0, tiled=True)  50.3 us
    dot_general x16, matrix products, block_scores(): jnp.einsum('sie,pje->sipj', slot_block, passage_vecs, preferred_element_t...  38 us
    all_to_all x1, starting transfers between devices, per_device(): lax.all_to_all(outgoing, 'dp', split_axis=0, concat_axis=0, tiled=True)  14.6 us
    all_to_all x1, waiting for transfers between devices, per_device(): lax.all_to_all(scores, 'dp', split_axis=0, concat_axis=0, tiled=True)  12.3 us
    all_gather x1, blocking collectives, per_device(): student = lax.all_gather(home_scores, 'mp', axis=2, tiled=True)  12.2 us
    dynamic_update_slice x16, local copies, waits for them, and re-layouts, soft_scores(): scored = lax.map(block_scores, blocked)  9.63 us
    all_to_all x1, starting transfers between devices, per_device(): lax.all_to_all(scores, 'dp', split_axis=0, concat_axis=0, tiled=True)  7.52 us
  transfers between devices with their start and end apart: 3, of which 3 were waited for; matrix products, arithmetic and copies ran while one was open for 2% of the time, Pallas kernels for 0%

commit v1 on v0

v1 whole, which is shorter than its diff:
```python
import functools
import math

import jax
import jax.numpy as jnp
from jax import lax
from jax.experimental import pallas as pl
from jax.experimental.pallas import tpu as pltpu
from jax.sharding import PartitionSpec as P


SOFTNESS = 0.1
EXP2_SCALE = math.log2(math.e) / SOFTNESS
EPS = 1e-6
VMEM = pl.BlockSpec(memory_space=pltpu.VMEM)
SMEM = pl.BlockSpec(memory_space=pltpu.SMEM)


def unit_rows(values):
    return values * lax.rsqrt(jnp.sum(values * values, axis=-1, keepdims=True) + EPS)


def project_kernel(parts, hidden_ref, proj_ref, out_ref):
    _, queries, share, embed = out_ref.shape
    projected = jnp.dot(hidden_ref[...], proj_ref[...], preferred_element_type=jnp.float32)
    projected = projected.reshape(queries, parts, share, embed)
    for part in range(parts):
        out_ref[part] = projected[:, part]


def passage_kernel(passages_ref, out_ref):
    out_ref[...] = unit_rows(passages_ref[...].astype(jnp.float32)).astype(jnp.bfloat16)


def pack_kernel(source_ref, partial_ref, out_ref, vecs):
    share = partial_ref.shape[2]
    total = partial_ref[0]
    for part in range(1, partial_ref.shape[0]):
        total = total + partial_ref[part]
    vecs[...] = unit_rows(total)
    capacity = out_ref.shape[1] // share

    def place(owner, carry):
        rows = [vecs[source_ref[owner * capacity + rank]] for rank in range(capacity)]
        out_ref[owner] = jnp.concatenate(rows, axis=0).astype(jnp.bfloat16)
        return carry

    lax.fori_loop(0, out_ref.shape[0], place, 0, unroll=8)


def turn_kernel(capacity, slots_ref, out_ref, wide):
    share, width, _ = out_ref.shape
    dp = width // capacity
    wide[...] = slots_ref[...].astype(jnp.float32)
    for token in range(share):
        for rank in range(capacity):
            rows = wide[pl.ds(rank * share + token, dp, stride=capacity * share), :]
            out_ref[token, rank * dp : (rank + 1) * dp] = rows.astype(jnp.bfloat16)


def score_kernel(capacity, *refs):
    slots_ref, *passage_refs, out_ref, sums = refs
    parts = len(passage_refs)
    share, count, _, width = sums.shape
    own = count // parts
    tokens = passage_refs[0].shape[0] // own
    dp = width // capacity
    group = 8
    mine = lax.axis_index("mp")

    def one_token(token, carry):
        vecs = slots_ref[token]
        for part in range(parts):
            for first in range(0, own, group):
                sims = lax.dot_general(
                    passage_refs[part][first * tokens : (first + group) * tokens, :],
                    vecs,
                    (((1,), (1,)), ((), ())),
                    preferred_element_type=jnp.float32,
                )
                raised = jnp.exp2(sims * EXP2_SCALE)
                place = lax.rem(mine + (parts - part), parts) * own + first
                sums[token, pl.ds(place, group)] = jnp.sum(
                    raised.reshape(group, tokens // 8, 8, width), axis=1
                )
        return carry

    lax.fori_loop(0, share, one_token, 0, unroll=2)
    logs = jnp.log(jnp.sum(sums[0], axis=1))
    for token in range(1, share):
        logs = logs + jnp.log(jnp.sum(sums[token], axis=1))
    logs = logs * SOFTNESS
    stacked = jnp.concatenate(
        [logs[:, rank * dp : (rank + 1) * dp] for rank in range(capacity)], axis=0
    )
    out_ref[...] = stacked.T


def home_kernel(owner_ref, rank_ref, scores_ref, out_ref):
    parts, pairs, queries, width = out_ref.shape
    count = width // 2
    lane = lax.broadcasted_iota(jnp.int32, (1, width), 1)

    def one_query(query, carry):
        for pair in range(pairs):
            halves = []
            for half in range(2):
                row = (query * pairs + pair) * 2 + half
                values = scores_ref[pl.ds(owner_ref[row], 1), :]
                turned = pltpu.roll(values, count, 1)
                halves.append(jnp.where(rank_ref[row] == half, values, turned))
            joined = jnp.where(lane < count, halves[0], halves[1])
            for part in range(parts):
                out_ref[part, pair, pl.ds(query, 1), :] = joined
        return carry

    lax.fori_loop(0, queries, one_query, 0, unroll=4)


def loss_kernel(partial_ref, teacher_ref, out_ref):
    pairs = partial_ref.shape[1]
    summed = partial_ref[0]
    for part in range(1, partial_ref.shape[0]):
        summed = summed + partial_ref[part]
    student = jnp.concatenate([summed[pair] for pair in range(pairs)], axis=1)
    teacher = teacher_ref[...]
    teacher_logp = teacher - jnp.log(jnp.sum(jnp.exp(teacher), axis=1, keepdims=True))
    loss = jnp.sum(jnp.exp(teacher_logp) * (teacher_logp - student), axis=1, keepdims=True)
    loss = loss + jnp.log(jnp.sum(jnp.exp(student), axis=1, keepdims=True))
    queries = loss.shape[0]
    out_ref[...] = jnp.broadcast_to(loss, (queries, 128)).T[:1]


def scored_loss(query_hidden, query_proj, passages, teacher, neg_blocks):
    dp = lax.axis_size("dp")
    mp = lax.axis_size("mp")
    queries, tokens, features = query_hidden.shape
    embed = query_proj.shape[1]
    picks = neg_blocks.shape[1]
    rows = queries * picks
    capacity = 2
    share = tokens // mp
    own_count, passage_tokens, _ = passages.shape
    count = own_count * mp

    partial = pl.pallas_call(
        functools.partial(project_kernel, mp),
        out_shape=jax.ShapeDtypeStruct((mp, queries, share, embed), jnp.float32),
        in_specs=[VMEM, VMEM],
        out_specs=VMEM,
        name="project",
    )(query_hidden.reshape(queries * tokens, features), query_proj)
    partial = lax.all_to_all(
        partial.reshape(mp, queries * share, embed), "mp", 0, 0, tiled=True
    ).reshape(mp, queries, share, embed)

    own_vecs = pl.pallas_call(
        passage_kernel,
        out_shape=jax.ShapeDtypeStruct((own_count * passage_tokens, embed), jnp.bfloat16),
        in_specs=[VMEM],
        out_specs=VMEM,
        name="passages",
    )(passages.reshape(own_count * passage_tokens, embed))
    passage_vecs = [own_vecs]
    for shift in range(1, mp):
        ring = [(place, (place + shift) % mp) for place in range(mp)]
        passage_vecs.append(lax.ppermute(own_vecs, "mp", ring))

    owners = neg_blocks.reshape(rows)
    row_ids = jnp.arange(rows, dtype=jnp.int32)
    earlier = (owners[:, None] == owners[None, :]) & (row_ids[None, :] < row_ids[:, None])
    ranks = jnp.sum(earlier.astype(jnp.int32), axis=1)
    slot_ids = owners * capacity + ranks
    slots = jnp.arange(dp * capacity, dtype=jnp.int32)
    source = jnp.sum(
        jnp.where(slots[:, None] == slot_ids[None, :], (row_ids // picks)[None, :], 0), axis=1
    )

    outgoing = pl.pallas_call(
        pack_kernel,
        out_shape=jax.ShapeDtypeStruct((dp, capacity * share, embed), jnp.bfloat16),
        in_specs=[SMEM, VMEM],
        out_specs=VMEM,
        scratch_shapes=[pltpu.VMEM((queries, share, embed), jnp.float32)],
        name="pack",
    )(source, partial)
    arrived = lax.all_to_all(outgoing, "dp", 0, 0, tiled=True)

    turned = pl.pallas_call(
        functools.partial(turn_kernel, capacity),
        out_shape=jax.ShapeDtypeStruct((share, capacity * dp, embed), jnp.bfloat16),
        in_specs=[VMEM],
        out_specs=VMEM,
        scratch_shapes=[pltpu.VMEM((dp * capacity * share, embed), jnp.float32)],
        name="turn",
    )(arrived.reshape(dp * capacity * share, embed))
    scores = pl.pallas_call(
        functools.partial(score_kernel, capacity),
        out_shape=jax.ShapeDtypeStruct((dp, capacity * count), jnp.float32),
        in_specs=[VMEM] * (1 + mp),
        out_specs=VMEM,
        scratch_shapes=[pltpu.VMEM((share, count, 8, dp * capacity), jnp.float32)],
        name="score",
    )(turned, *passage_vecs)
    returned = lax.all_to_all(
        scores.reshape(dp, 1, capacity * count), "dp", 0, 0, tiled=True
    ).reshape(dp, capacity * count)

    home = pl.pallas_call(
        home_kernel,
        out_shape=jax.ShapeDtypeStruct((mp, picks // 2, queries, 2 * count), jnp.float32),
        in_specs=[SMEM, SMEM, VMEM],
        out_specs=VMEM,
        name="home",
    )(owners, ranks, returned)
    home = lax.all_to_all(home, "mp", 0, 0, tiled=True)

    loss = pl.pallas_call(
        loss_kernel,
        out_shape=jax.ShapeDtypeStruct((1, queries), jnp.float32),
        in_specs=[VMEM, VMEM],
        out_specs=VMEM,
        name="loss",
    )(home, teacher.reshape(queries, picks * count))
    return loss.reshape(queries)


def solution(mesh):
    in_specs = (
        P("dp", None, "mp"),
        P("mp", None),
        P(("dp", "mp"), None, None),
        P("dp", None, None),
        P("dp", None),
    )
    return jax.shard_map(
        scored_loss, mesh=mesh, in_specs=in_specs, out_specs=P("dp"), check_vma=False
    )
```

time: 231 us -> 124 us (0.54)
  waiting for transfers between devices: 119 us -> 27 us
  matrix products: 39.9 us -> 0 us
  Pallas kernels: 0 us -> 25.7 us
  starting transfers between devices: 22.2 us -> 37.9 us
  blocking collectives: 12.2 us -> 25.8 us
  between operations: 13.6 us -> 0.07 us
  local copies, waits for them, and re-layouts: 13.7 us -> 4.84 us
  other arithmetic: 9.3 us -> 0.88 us
    psum x1 -> x0, waiting for transfers between devices: 56 us -> none  [per_device(): projected = lax.psum(partial_sum, 'mp')]
    all_to_all x2 -> x3, waiting for transfers between devices: 62.5 us -> 16.5 us  [the longest x1 9.2 us: scored_loss(): arrived = lax.all_to_all(outgoing, 'dp', 0, 0, tiled=True)]
    dot_general x17 -> x0, matrix products: 39.9 us -> none  [the longest x16 38 us: block_scores(): jnp.einsum('sie,pje->sipj', slot_block, passage_vecs, preferred_element_t...]
    all_to_all x0 -> x1, blocking collectives: none -> 25.8 us  [scored_loss(): lax.all_to_all(scores.reshape(dp, 1, capacity * count), 'dp', 0, 0, tiled...]
    pallas_call x0 -> x7, Pallas kernels: none -> 25.7 us  [the longest x1 13 us: scored_loss(): pl.pallas_call(functools.partial(score_kernel, capacity), out_shape=jax.S...]
    all_gather x1 -> x0, blocking collectives: 12.2 us -> none  [per_device(): student = lax.all_gather(home_scores, 'mp', axis=2, tiled=True)]
    ppermute x0 -> x3, waiting for transfers between devices: none -> 10.5 us  [scored_loss(): passage_vecs.append(lax.ppermute(own_vecs, 'mp', ring))]
    dynamic_update_slice x16 -> x0, local copies, waits for them, and re-layouts: 9.63 us -> none  [soft_scores(): scored = lax.map(block_scores, blocked)]
  transfers between devices with their start and end apart: 3 -> 6, of which waited for: 3 -> 5; matrix products, arithmetic and copies ran while one was open for 2% -> 1% of each run, Pallas kernels for 0% -> 4%
where the time goes in v1:
time: 124 us; the launch traced here: 122 us
  starting transfers between devices  37.9 us (31%)
  waiting for transfers between devices  27 us (22%)
  blocking collectives  25.8 us (21%)
  Pallas kernels  25.7 us (21%)
  local copies, waits for them, and re-layouts  4.84 us (4%)
    all_to_all x1, blocking collectives, scored_loss(): lax.all_to_all(scores.reshape(dp, 1, capacity * count), 'dp', 0, 0, tiled...  25.8 us
    all_to_all x1, starting transfers between devices, scored_loss(): arrived = lax.all_to_all(outgoing, 'dp', 0, 0, tiled=True)  14.7 us
    pallas_call x1, Pallas kernels, scored_loss(): pl.pallas_call(functools.partial(score_kernel, capacity), out_shape=jax.S...  13 us
    ppermute x3, waiting for transfers between devices, scored_loss(): passage_vecs.append(lax.ppermute(own_vecs, 'mp', ring))  10.5 us
    all_to_all x1, starting transfers between devices, scored_loss(): lax.all_to_all(partial.reshape(mp, queries * share, embed), 'mp', 0, 0, t...  9.4 us
    ppermute x3, starting transfers between devices, scored_loss(): passage_vecs.append(lax.ppermute(own_vecs, 'mp', ring))  9.2 us
    all_to_all x1, waiting for transfers between devices, scored_loss(): arrived = lax.all_to_all(outgoing, 'dp', 0, 0, tiled=True)  9.2 us
    all_to_all x1, starting transfers between devices, scored_loss(): home = lax.all_to_all(home, 'mp', 0, 0, tiled=True)  4.64 us
  transfers between devices with their start and end apart: 6, of which 5 were waited for; matrix products, arithmetic and copies ran while one was open for 1% of the time, Pallas kernels for 4%

profile of v1, /device:TPU:6, one launch (start us, length us, event | category | flops | bytes accessed | tf_op | source)
XLA Modules:
  0.0 122.1 jit_solution(4613258657771795891)
XLA Ops:
  0.0 2.1 %project.1 = f32[4,32,8,128]{3,2,1,0:T(8,128)} custom-call(bf16[1024,192]{1,0:T(8,128)(2,1)} %bitcast.13, bf16[192,128]{1,0:T(8,128)(2,1)} %proj_ref.1), custom_call_target="tpu_custom_call" | custom-call | tf_op jit(solution)/shard_map/project/pallas_call | solution.py:146
  2.1 0.0 copy-start.9
  2.1 9.4 %all-to-all-start = ((f32[4,256,128]{2,1,0:T(8,128)}), f32[4,256,128]{2,1,0:T(8,128)S(1)}, u32[]{:S(2)}, u32[]{:S(2)}) async-start(f32[4,256,128]{2,1,0:T(8,128)} %bitcast.12), calls=%async_computation | async-start | bytes 1048576 | tf_op jit(solution)/shard_map/all_to_all | solution.py:153
  11.5 0.0 copy-done.9
  11.5 0.1 copy.10
  11.6 0.1 reshape.53.owner_ref
  11.7 0.0 copy-start.7
  11.7 0.2 convert_reduce_fusion.rank_ref
  11.9 0.3 copy-done.7
  12.2 0.0 copy-start.8
  12.2 0.5 copy-done.8
  12.8 0.7 select_reduce_fusion.source_ref
  13.5 4.1 %all-to-all-done = f32[4,256,128]{2,1,0:T(8,128)S(1)} async-done(((f32[4,256,128]{2,1,0:T(8,128)}), f32[4,256,128]{2,1,0:T(8,128)S(1)}, u32[]{:S(2)}, u32[]{:S(2)}) %all-to-all-start) | async-done | bytes 524320 | tf_op jit(solution)/shard_map/all_to_all | solution.py:153
  17.5 0.0 copy-start
  17.5 0.8 copy-done
  18.3 2.3 %pack.1 = bf16[128,16,128]{2,1,0:T(8,128)(2,1)} custom-call(s32[256]{0:T(256)} %select_reduce_fusion.source_ref, f32[4,32,8,128]{3,2,1,0:T(8,128)} %bitcast.10), custom_call_target="tpu_custom_call" | custom-call | tf_op jit(solution)/shard_map/pack/pallas_call | solution.py:179
  20.7 14.7 %all-to-all-start.1 = ((bf16[128,16,128]{2,1,0:T(8,128)(2,1)}), bf16[128,16,128]{2,1,0:T(8,128)(2,1)S(1)}, u32[]{:S(2)}, u32[]{:S(2)}) async-start(bf16[128,16,128]{2,1,0:T(8,128)(2,1)} %pack.1), calls=%async_computation.1 | async-start | bytes 1048576 | tf_op jit(solution)/shard_map/all_to_all | solution.py:187
  35.4 2.2 %passages.1.refs_1_ = bf16[2048,128]{1,0:T(8,128)(2,1)} custom-call(bf16[2048,128]{1,0:T(8,128)(2,1)} %bitcast.14), custom_call_target="tpu_custom_call" | custom-call | tf_op jit(solution)/shard_map/passages/pallas_call | solution.py:157
  37.6 4.0 %collective-permute-start = (bf16[2048,128]{1,0:T(8,128)(2,1)}, bf16[2048,128]{1,0:T(8,128)(2,1)S(1)}, u32[]{:S(2)}, u32[]{:S(2)}) collective-permute-start(bf16[2048,128]{1,0:T(8,128)(2,1)} %passages.1.refs_1_), channel_id=1, source_target_pairs={{0,1},{1,2},{2,3},{3,0},{4,5},{5,6},{6,7},{7,4},{8,9},{9,10},{10,1... | collective-permute-start | bytes 1572872 | tf_op jit(solution)/shard_map/ppermute | solution.py:167
  41.5 1.9 %collective-permute-start.1 = (bf16[2048,128]{1,0:T(8,128)(2,1)}, bf16[2048,128]{1,0:T(8,128)(2,1)S(1)}, u32[]{:S(2)}, u32[]{:S(2)}) collective-permute-start(bf16[2048,128]{1,0:T(8,128)(2,1)} %passages.1.refs_1_), channel_id=1, source_target_pairs={{0,2},{1,3},{2,0},{3,1},{4,6},{5,7},{6,4},{7,5},{8,10},{9,11},{10,... | collective-permute-start | bytes 1572872 | tf_op jit(solution)/shard_map/ppermute | solution.py:167
  43.5 3.3 %collective-permute-start.2 = (bf16[2048,128]{1,0:T(8,128)(2,1)}, bf16[2048,128]{1,0:T(8,128)(2,1)S(1)}, u32[]{:S(2)}, u32[]{:S(2)}) collective-permute-start(bf16[2048,128]{1,0:T(8,128)(2,1)} %passages.1.refs_1_), channel_id=1, source_target_pairs={{0,3},{1,0},{2,1},{3,2},{4,7},{5,4},{6,5},{7,6},{8,11},{9,8},{10,9... | collective-permute-start | bytes 1572872 | tf_op jit(solution)/shard_map/ppermute | solution.py:167
  46.8 9.2 %all-to-all-done.1 = bf16[128,16,128]{2,1,0:T(8,128)(2,1)S(1)} async-done(((bf16[128,16,128]{2,1,0:T(8,128)(2,1)}), bf16[128,16,128]{2,1,0:T(8,128)(2,1)S(1)}, u32[]{:S(2)}, u32[]{:S(2)}) %all-to-all-start.1) | async-done | bytes 524320 | tf_op jit(solution)/shard_map/all_to_all | solution.py:187
  56.0 0.0 copy-start.1
  56.0 0.8 copy-done.1
  56.8 2.2 %turn.1.refs_0_ = bf16[8,256,128]{2,1,0:T(8,128)(2,1)} custom-call(bf16[2048,128]{1,0:T(8,128)(2,1)} %bitcast.11), custom_call_target="tpu_custom_call" | custom-call | tf_op jit(solution)/shard_map/turn/pallas_call | solution.py:189
  59.0 5.0 %collective-permute-done.refs_2_ = bf16[2048,128]{1,0:T(8,128)(2,1)S(1)} collective-permute-done((bf16[2048,128]{1,0:T(8,128)(2,1)}, bf16[2048,128]{1,0:T(8,128)(2,1)S(1)}, u32[]{:S(2)}, u32[]{:S(2)}) %collective-permute-start) | collective-permute-done | bytes 524320 | tf_op jit(solution)/shard_map/ppermute | solution.py:167
  64.1 0.0 copy-start.3
  64.1 0.0 collective-permute-done.1.refs_3_
  64.1 0.0 copy-start.4
  64.1 5.5 %collective-permute-done.2.refs_4_ = bf16[2048,128]{1,0:T(8,128)(2,1)S(1)} collective-permute-done((bf16[2048,128]{1,0:T(8,128)(2,1)}, bf16[2048,128]{1,0:T(8,128)(2,1)S(1)}, u32[]{:S(2)}, u32[]{:S(2)}) %collective-permute-start.2) | collective-permute-done | bytes 524320 | tf_op jit(solution)/shard_map/ppermute | solution.py:167
  69.5 0.0 copy-done.3
  69.5 0.0 copy-done.4
  69.5 0.0 copy-start.5
  69.5 0.8 copy-done.5
  70.3 13.0 %score.1 = f32[128,128]{1,0:T(8,128)} custom-call(bf16[8,256,128]{2,1,0:T(8,128)(2,1)} %turn.1.refs_0_, bf16[2048,128]{1,0:T(8,128)(2,1)} %passages.1.refs_1_, bf16[2048,128]{1,0:T(8,128)(2,1)} %copy-done.3, bf16[2048,128]{1,0:T(8,128)(2,1)} %copy-done.4, bf16[2048,128]{1,0:T(8,128)(2,1)} %copy-done.5), custom_call_target="tpu_custom_call" | custom-call | tf_op jit(solution)/shard_map/score/pallas_call | solution.py:197
  83.3 25.8 %all_to_all.20 = f32[128,1,128]{2,1,0:T(1,128)} all-to-all(f32[128,1,128]{2,1,0:T(1,128)} %bitcast.16), channel_id=1, replica_groups=mesh['dp'=128,'mp'=4] {'dp'}, dimensions={0} | all-to-all | bytes 131072 | tf_op jit(solution)/shard_map/all_to_all | solution.py:205
  109.1 2.2 %home.1 = f32[4,2,32,128]{3,2,1,0:T(8,128)} custom-call(s32[128]{0:T(128)} %copy-done.7, s32[128]{0:T(128)} %copy-done.8, f32[128,128]{1,0:T(8,128)} %bitcast.15), custom_call_target="tpu_custom_call" | custom-call | tf_op jit(solution)/shard_map/home/pallas_call | solution.py:209
  111.3 0.0 copy-start.6
  111.3 4.6 %all-to-all-start.3 = ((f32[4,2,32,128]{3,2,1,0:T(8,128)}), f32[4,2,32,128]{3,2,1,0:T(8,128)S(1)}, u32[]{:S(2)}, u32[]{:S(2)}) async-start(f32[4,2,32,128]{3,2,1,0:T(8,128)} %home.1), calls=%async_computation.3 | async-start | bytes 262144 | tf_op jit(solution)/shard_map/all_to_all | solution.py:216
  115.9 0.0 copy-done.6
  115.9 0.7 reshape.61.teacher_ref
  116.6 3.2 %all-to-all-done.3.partial_ref = f32[4,2,32,128]{3,2,1,0:T(8,128)S(1)} async-done(((f32[4,2,32,128]{3,2,1,0:T(8,128)}), f32[4,2,32,128]{3,2,1,0:T(8,128)S(1)}, u32[]{:S(2)}, u32[]{:S(2)}) %all-to-all-start.3) | async-done | bytes 131104 | tf_op jit(solution)/shard_map/all_to_all | solution.py:216
  119.8 0.0 copy-start.2
  119.8 0.6 copy-done.2
  120.5 1.7 %loss.1 = f32[1,32]{1,0:T(1,128)} custom-call(f32[4,2,32,128]{3,2,1,0:T(8,128)} %copy-done.2, f32[32,256]{1,0:T(8,128)} %reshape.61.teacher_ref), custom_call_target="tpu_custom_call" | custom-call | tf_op jit(solution)/shard_map/loss/pallas_call | solution.py:218
  (1 shorter events, 0.0 us)
Async XLA Ops:
  2.1 9.4 %copy-start.9 = (s32[32,4]{0,1:T(4,128)S(1)}, s32[32,4]{0,1:T(4,128)}, u32[]{:S(2)}) copy-start(s32[32,4]{0,1:T(4,128)} %param.9) | copy-start | bytes 1540
  2.1 15.4 %all-to-all-start = ((f32[4,256,128]{2,1,0:T(8,128)}), f32[4,256,128]{2,1,0:T(8,128)S(1)}, u32[]{:S(2)}, u32[]{:S(2)}) async-start(f32[4,256,128]{2,1,0:T(8,128)} %bitcast.12), calls=%async_computation | async-start | bytes 1048576 | tf_op jit(solution)/shard_map/all_to_all | solution.py:153
  11.7 0.5 copy-start.7
  12.2 0.5 copy-start.8
  17.5 0.8 copy-start
  20.7 35.3 %all-to-all-start.1 = ((bf16[128,16,128]{2,1,0:T(8,128)(2,1)}), bf16[128,16,128]{2,1,0:T(8,128)(2,1)S(1)}, u32[]{:S(2)}, u32[]{:S(2)}) async-start(bf16[128,16,128]{2,1,0:T(8,128)(2,1)} %pack.1), calls=%async_computation.1 | async-start | bytes 1048576 | tf_op jit(solution)/shard_map/all_to_all | solution.py:187
  37.6 26.5 %collective-permute-start = (bf16[2048,128]{1,0:T(8,128)(2,1)}, bf16[2048,128]{1,0:T(8,128)(2,1)S(1)}, u32[]{:S(2)}, u32[]{:S(2)}) collective-permute-start(bf16[2048,128]{1,0:T(8,128)(2,1)} %passages.1.refs_1_), channel_id=1, source_target_pairs={{0,1},{1,2},{2,3},{3,0},{4,5},{5,6},{6,7},{7,4},{8,9},{9,10},{10,1... | collective-permute-start | bytes 1572872 | tf_op jit(solution)/shard_map/ppermute | solution.py:167
  41.5 22.5 %collective-permute-start.1 = (bf16[2048,128]{1,0:T(8,128)(2,1)}, bf16[2048,128]{1,0:T(8,128)(2,1)S(1)}, u32[]{:S(2)}, u32[]{:S(2)}) collective-permute-start(bf16[2048,128]{1,0:T(8,128)(2,1)} %passages.1.refs_1_), channel_id=1, source_target_pairs={{0,2},{1,3},{2,0},{3,1},{4,6},{5,7},{6,4},{7,5},{8,10},{9,11},{10,... | collective-permute-start | bytes 1572872 | tf_op jit(solution)/shard_map/ppermute | solution.py:167
  43.5 26.1 %collective-permute-start.2 = (bf16[2048,128]{1,0:T(8,128)(2,1)}, bf16[2048,128]{1,0:T(8,128)(2,1)S(1)}, u32[]{:S(2)}, u32[]{:S(2)}) collective-permute-start(bf16[2048,128]{1,0:T(8,128)(2,1)} %passages.1.refs_1_), channel_id=1, source_target_pairs={{0,3},{1,0},{2,1},{3,2},{4,7},{5,4},{6,5},{7,6},{8,11},{9,8},{10,9... | collective-permute-start | bytes 1572872 | tf_op jit(solution)/shard_map/ppermute | solution.py:167
  56.0 0.8 copy-start.1
  64.1 5.5 %copy-start.3 = (bf16[2048,128]{1,0:T(8,128)(2,1)}, bf16[2048,128]{1,0:T(8,128)(2,1)S(1)}, u32[]{:S(2)}) copy-start(bf16[2048,128]{1,0:T(8,128)(2,1)S(1)} %collective-permute-done.refs_2_) | copy-start | bytes 1572868
  64.1 5.5 %copy-start.4 = (bf16[2048,128]{1,0:T(8,128)(2,1)}, bf16[2048,128]{1,0:T(8,128)(2,1)S(1)}, u32[]{:S(2)}) copy-start(bf16[2048,128]{1,0:T(8,128)(2,1)S(1)} %collective-permute-done.1.refs_3_) | copy-start | bytes 1572868
  69.5 0.8 copy-start.5
  111.3 4.6 %copy-start.6 = (f32[32,4,64]{2,1,0:T(4,128)S(1)}, f32[32,4,64]{2,1,0:T(4,128)}, u32[]{:S(2)}) copy-start(f32[32,4,64]{2,1,0:T(4,128)} %param.8) | copy-start | bytes 98308
  111.3 8.5 %all-to-all-start.3 = ((f32[4,2,32,128]{3,2,1,0:T(8,128)}), f32[4,2,32,128]{3,2,1,0:T(8,128)S(1)}, u32[]{:S(2)}, u32[]{:S(2)}) async-start(f32[4,2,32,128]{3,2,1,0:T(8,128)} %home.1), calls=%async_computation.3 | async-start | bytes 262144 | tf_op jit(solution)/shard_map/all_to_all | solution.py:216
  119.8 0.7 copy-start.2

commit v2 on v1

--- a/solution.py
+++ b/solution.py
@@ -48,18 +48,8 @@
     lax.fori_loop(0, out_ref.shape[0], place, 0, unroll=8)
 
 
-def turn_kernel(capacity, slots_ref, out_ref, wide):
-    share, width, _ = out_ref.shape
-    dp = width // capacity
-    wide[...] = slots_ref[...].astype(jnp.float32)
-    for token in range(share):
-        for rank in range(capacity):
-            rows = wide[pl.ds(rank * share + token, dp, stride=capacity * share), :]
-            out_ref[token, rank * dp : (rank + 1) * dp] = rows.astype(jnp.bfloat16)
-
-
 def score_kernel(capacity, *refs):
-    slots_ref, *passage_refs, out_ref, sums = refs
+    slots_ref, *passage_refs, out_ref, wide, turned, sums = refs
     parts = len(passage_refs)
     share, count, _, width = sums.shape
     own = count // parts
@@ -67,9 +57,14 @@
     dp = width // capacity
     group = 8
     mine = lax.axis_index("mp")
+    wide[...] = slots_ref[...].astype(jnp.float32)
+    for token in range(share):
+        for rank in range(capacity):
+            rows = wide[pl.ds(rank * share + token, dp, stride=capacity * share), :]
+            turned[token, rank * dp : (rank + 1) * dp] = rows.astype(jnp.bfloat16)
 
     def one_token(token, carry):
-        vecs = slots_ref[token]
+        vecs = turned[token]
         for part in range(parts):
             for first in range(0, own, group):
                 sims = lax.dot_general(
@@ -93,12 +88,20 @@
     stacked = jnp.concatenate(
         [logs[:, rank * dp : (rank + 1) * dp] for rank in range(capacity)], axis=0
     )
-    out_ref[...] = stacked.T
-
-
-def home_kernel(owner_ref, rank_ref, scores_ref, out_ref):
-    parts, pairs, queries, width = out_ref.shape
+    scores = stacked.T
+    for part in range(parts):
+        out_ref[pl.ds(part, dp, stride=parts), :] = scores
+
+
+def loss_kernel(owner_ref, rank_ref, partial_ref, teacher_ref, out_ref, scores, student):
+    pairs, queries, width = student.shape
     count = width // 2
+    dp = scores.shape[0]
+    parts = partial_ref.shape[0] // dp
+    total = partial_ref[pl.ds(0, dp, stride=parts), :]
+    for part in range(1, parts):
+        total = total + partial_ref[pl.ds(part, dp, stride=parts), :]
+    scores[...] = total
     lane = lax.broadcasted_iota(jnp.int32, (1, width), 1)
 
     def one_query(query, carry):
@@ -106,28 +109,18 @@
             halves = []
             for half in range(2):
                 row = (query * pairs + pair) * 2 + half
-                values = scores_ref[pl.ds(owner_ref[row], 1), :]
+                values = scores[pl.ds(owner_ref[row], 1), :]
                 turned = pltpu.roll(values, count, 1)
                 halves.append(jnp.where(rank_ref[row] == half, values, turned))
-            joined = jnp.where(lane < count, halves[0], halves[1])
-            for part in range(parts):
-                out_ref[part, pair, pl.ds(query, 1), :] = joined
+            student[pair, pl.ds(query, 1), :] = jnp.where(lane < count, halves[0], halves[1])
         return carry
 
-    lax.fori_loop(0, queries, one_query, 0, unroll=4)
-
-
-def loss_kernel(partial_ref, teacher_ref, out_ref):
-    pairs = partial_ref.shape[1]
-    summed = partial_ref[0]
-    for part in range(1, partial_ref.shape[0]):
-        summed = summed + partial_ref[part]
-    student = jnp.concatenate([summed[pair] for pair in range(pairs)], axis=1)
+    lax.fori_loop(0, queries, one_query, 0, unroll=8)
+    chosen = jnp.concatenate([student[pair] for pair in range(pairs)], axis=1)
     teacher = teacher_ref[...]
     teacher_logp = teacher - jnp.log(jnp.sum(jnp.exp(teacher), axis=1, keepdims=True))
-    loss = jnp.sum(jnp.exp(teacher_logp) * (teacher_logp - student), axis=1, keepdims=True)
-    loss = loss + jnp.log(jnp.sum(jnp.exp(student), axis=1, keepdims=True))
-    queries = loss.shape[0]
+    loss = jnp.sum(jnp.exp(teacher_logp) * (teacher_logp - chosen), axis=1, keepdims=True)
+    loss = loss + jnp.log(jnp.sum(jnp.exp(chosen), axis=1, keepdims=True))
     out_ref[...] = jnp.broadcast_to(loss, (queries, 128)).T[:1]
 
 
@@ -186,42 +179,33 @@
     )(source, partial)
     arrived = lax.all_to_all(outgoing, "dp", 0, 0, tiled=True)
 
-    turned = pl.pallas_call(
-        functools.partial(turn_kernel, capacity),
-        out_shape=jax.ShapeDtypeStruct((share, capacity * dp, embed), jnp.bfloat16),
-        in_specs=[VMEM],
-        out_specs=VMEM,
-        scratch_shapes=[pltpu.VMEM((dp * capacity * share, embed), jnp.float32)],
-        name="turn",
-    )(arrived.reshape(dp * capacity * share, embed))
     scores = pl.pallas_call(
         functools.partial(score_kernel, capacity),
-        out_shape=jax.ShapeDtypeStruct((dp, capacity * count), jnp.float32),
+        out_shape=jax.ShapeDtypeStruct((dp * mp, capacity * count), jnp.float32),
         in_specs=[VMEM] * (1 + mp),
         out_specs=VMEM,
-        scratch_shapes=[pltpu.VMEM((share, count, 8, dp * capacity), jnp.float32)],
+        scratch_shapes=[
+            pltpu.VMEM((dp * capacity * share, embed), jnp.float32),
+            pltpu.VMEM((share, dp * capacity, embed), jnp.bfloat16),
+            pltpu.VMEM((share, count, 8, dp * capacity), jnp.float32),
+        ],
         name="score",
-    )(turned, *passage_vecs)
+    )(arrived.reshape(dp * capacity * share, embed), *passage_vecs)
     returned = lax.all_to_all(
-        scores.reshape(dp, 1, capacity * count), "dp", 0, 0, tiled=True
-    ).reshape(dp, capacity * count)
-
-    home = pl.pallas_call(
-        home_kernel,
-        out_shape=jax.ShapeDtypeStruct((mp, picks // 2, queries, 2 * count), jnp.float32),
-        in_specs=[SMEM, SMEM, VMEM],
-        out_specs=VMEM,
-        name="home",
-    )(owners, ranks, returned)
-    home = lax.all_to_all(home, "mp", 0, 0, tiled=True)
+        scores.reshape(dp * mp, 1, capacity * count), ("dp", "mp"), 0, 0, tiled=True
+    ).reshape(dp * mp, capacity * count)
 
     loss = pl.pallas_call(
         loss_kernel,
         out_shape=jax.ShapeDtypeStruct((1, queries), jnp.float32),
-        in_specs=[VMEM, VMEM],
-        out_specs=VMEM,
+        in_specs=[SMEM, SMEM, VMEM, VMEM],
+        out_specs=VMEM,
+        scratch_shapes=[
+            pltpu.VMEM((dp, capacity * count), jnp.float32),
+            pltpu.VMEM((picks // 2, queries, 2 * count), jnp.float32),
+        ],
         name="loss",
-    )(home, teacher.reshape(queries, picks * count))
+    )(owners, ranks, returned, teacher.reshape(queries, picks * count))
     return loss.reshape(queries)
 
 

time: 124 us -> 122 us (0.984)
  the two profiles are of different devices: /device:TPU:6 before, /device:TPU:1 now
where the time goes in v2:
time: 122 us; the launch traced here: 121 us
  starting transfers between devices  51.9 us (43%)
  waiting for transfers between devices  42 us (34%)
  Pallas kernels  22.2 us (18%)
  local copies, waits for them, and re-layouts  4.26 us (3%)
    ppermute x3, waiting for transfers between devices, scored_loss(): passage_vecs.append(lax.ppermute(own_vecs, 'mp', ring))  21.5 us
    all_to_all x1, starting transfers between devices, scored_loss(): arrived = lax.all_to_all(outgoing, 'dp', 0, 0, tiled=True)  20.4 us
    all_to_all x1, starting transfers between devices, scored_loss(): lax.all_to_all(scores.reshape(dp * mp, 1, capacity * count), ('dp', 'mp')...  18.1 us
    all_to_all x1, waiting for transfers between devices, scored_loss(): lax.all_to_all(scores.reshape(dp * mp, 1, capacity * count), ('dp', 'mp')...  15.5 us
    pallas_call x1, Pallas kernels, scored_loss(): pl.pallas_call(functools.partial(score_kernel, capacity), out_shape=jax.S...  13.4 us
    ppermute x3, starting transfers between devices, scored_loss(): passage_vecs.append(lax.ppermute(own_vecs, 'mp', ring))  8.4 us
    all_to_all x1, starting transfers between devices, scored_loss(): lax.all_to_all(partial.reshape(mp, queries * share, embed), 'mp', 0, 0, t...  4.96 us
    all_to_all x1, waiting for transfers between devices, scored_loss(): lax.all_to_all(partial.reshape(mp, queries * share, embed), 'mp', 0, 0, t...  4.96 us
  transfers between devices with their start and end apart: 6, of which 5 were waited for; matrix products, arithmetic and copies ran while one was open for 1% of the time, Pallas kernels for 2%

profile of v2, /device:TPU:1, one launch (start us, length us, event | category | flops | bytes accessed | tf_op | source)
XLA Modules:
  0.0 121.4 jit_solution(558249625871052278)
XLA Ops:
  0.0 2.1 %project.1 = f32[4,32,8,128]{3,2,1,0:T(8,128)} custom-call(bf16[1024,192]{1,0:T(8,128)(2,1)} %bitcast.15, bf16[192,128]{1,0:T(8,128)(2,1)} %proj_ref.1), custom_call_target="tpu_custom_call" | custom-call | tf_op jit(solution)/shard_map/project/pallas_call | solution.py:139
  2.1 0.0 copy-start.9
  2.1 5.0 %all-to-all-start = ((f32[4,256,128]{2,1,0:T(8,128)}), f32[4,256,128]{2,1,0:T(8,128)S(1)}, u32[]{:S(2)}, u32[]{:S(2)}) async-start(f32[4,256,128]{2,1,0:T(8,128)} %bitcast.11), calls=%async_computation | async-start | bytes 1048576 | tf_op jit(solution)/shard_map/all_to_all | solution.py:146
  7.1 0.0 copy-done.9
  7.1 0.1 copy.10
  7.2 0.1 reshape.53.owner_ref
  7.3 0.0 copy-start.7
  7.3 0.2 convert_reduce_fusion.rank_ref
  7.5 0.4 copy-done.7
  7.9 0.0 copy-start.8
  7.9 0.5 copy-done.8
  8.4 0.7 select_reduce_fusion.source_ref
  9.1 5.0 %all-to-all-done = f32[4,256,128]{2,1,0:T(8,128)S(1)} async-done(((f32[4,256,128]{2,1,0:T(8,128)}), f32[4,256,128]{2,1,0:T(8,128)S(1)}, u32[]{:S(2)}, u32[]{:S(2)}) %all-to-all-start) | async-done | bytes 524320 | tf_op jit(solution)/shard_map/all_to_all | solution.py:146
  14.0 0.0 copy-start
  14.0 0.8 copy-done
  14.8 2.3 %pack.1 = bf16[128,16,128]{2,1,0:T(8,128)(2,1)} custom-call(s32[256]{0:T(256)} %select_reduce_fusion.source_ref, f32[4,32,8,128]{3,2,1,0:T(8,128)} %bitcast.10), custom_call_target="tpu_custom_call" | custom-call | tf_op jit(solution)/shard_map/pack/pallas_call | solution.py:172
  17.1 20.4 %all-to-all-start.1 = ((bf16[128,16,128]{2,1,0:T(8,128)(2,1)}), bf16[128,16,128]{2,1,0:T(8,128)(2,1)S(1)}, u32[]{:S(2)}, u32[]{:S(2)}) async-start(bf16[128,16,128]{2,1,0:T(8,128)(2,1)} %pack.1), calls=%async_computation.1 | async-start | bytes 1048576 | tf_op jit(solution)/shard_map/all_to_all | solution.py:180
  37.6 2.2 %passages.1.refs_1_ = bf16[2048,128]{1,0:T(8,128)(2,1)} custom-call(bf16[2048,128]{1,0:T(8,128)(2,1)} %bitcast.16), custom_call_target="tpu_custom_call" | custom-call | tf_op jit(solution)/shard_map/passages/pallas_call | solution.py:150
  39.8 2.2 %collective-permute-start = (bf16[2048,128]{1,0:T(8,128)(2,1)}, bf16[2048,128]{1,0:T(8,128)(2,1)S(1)}, u32[]{:S(2)}, u32[]{:S(2)}) collective-permute-start(bf16[2048,128]{1,0:T(8,128)(2,1)} %passages.1.refs_1_), channel_id=1, source_target_pairs={{0,1},{1,2},{2,3},{3,0},{4,5},{5,6},{6,7},{7,4},{8,9},{9,10},{10,1... | collective-permute-start | bytes 1572872 | tf_op jit(solution)/shard_map/ppermute | solution.py:160
  42.0 3.7 %collective-permute-start.1 = (bf16[2048,128]{1,0:T(8,128)(2,1)}, bf16[2048,128]{1,0:T(8,128)(2,1)S(1)}, u32[]{:S(2)}, u32[]{:S(2)}) collective-permute-start(bf16[2048,128]{1,0:T(8,128)(2,1)} %passages.1.refs_1_), channel_id=1, source_target_pairs={{0,2},{1,3},{2,0},{3,1},{4,6},{5,7},{6,4},{7,5},{8,10},{9,11},{10,... | collective-permute-start | bytes 1572872 | tf_op jit(solution)/shard_map/ppermute | solution.py:160
  45.7 2.5 %collective-permute-start.2 = (bf16[2048,128]{1,0:T(8,128)(2,1)}, bf16[2048,128]{1,0:T(8,128)(2,1)S(1)}, u32[]{:S(2)}, u32[]{:S(2)}) collective-permute-start(bf16[2048,128]{1,0:T(8,128)(2,1)} %passages.1.refs_1_), channel_id=1, source_target_pairs={{0,3},{1,0},{2,1},{3,2},{4,7},{5,4},{6,5},{7,6},{8,11},{9,8},{10,9... | collective-permute-start | bytes 1572872 | tf_op jit(solution)/shard_map/ppermute | solution.py:160
  48.2 8.1 %collective-permute-done.refs_2_ = bf16[2048,128]{1,0:T(8,128)(2,1)S(1)} collective-permute-done((bf16[2048,128]{1,0:T(8,128)(2,1)}, bf16[2048,128]{1,0:T(8,128)(2,1)S(1)}, u32[]{:S(2)}, u32[]{:S(2)}) %collective-permute-start) | collective-permute-done | bytes 524320 | tf_op jit(solution)/shard_map/ppermute | solution.py:160
  56.3 0.0 copy-start.3
  56.3 10.1 %collective-permute-done.1.refs_3_ = bf16[2048,128]{1,0:T(8,128)(2,1)S(1)} collective-permute-done((bf16[2048,128]{1,0:T(8,128)(2,1)}, bf16[2048,128]{1,0:T(8,128)(2,1)S(1)}, u32[]{:S(2)}, u32[]{:S(2)}) %collective-permute-start.1) | collective-permute-done | bytes 524320 | tf_op jit(solution)/shard_map/ppermute | solution.py:160
  66.3 0.0 copy-start.4
  66.3 3.4 %collective-permute-done.2.refs_4_ = bf16[2048,128]{1,0:T(8,128)(2,1)S(1)} collective-permute-done((bf16[2048,128]{1,0:T(8,128)(2,1)}, bf16[2048,128]{1,0:T(8,128)(2,1)S(1)}, u32[]{:S(2)}, u32[]{:S(2)}) %collective-permute-start.2) | collective-permute-done | bytes 524320 | tf_op jit(solution)/shard_map/ppermute | solution.py:160
  69.7 0.0 copy-start.5
  69.7 0.0 all-to-all-done.1
  69.7 0.0 copy-start.1
  69.7 0.0 copy-done.3
  69.7 0.0 copy-done.4
  69.7 0.8 copy-done.5
  70.5 0.2 copy-done.1
  70.7 13.4 %score.1 = f32[512,128]{1,0:T(8,128)} custom-call(bf16[2048,128]{1,0:T(8,128)(2,1)} %bitcast.12, bf16[2048,128]{1,0:T(8,128)(2,1)} %passages.1.refs_1_, bf16[2048,128]{1,0:T(8,128)(2,1)} %copy-done.3, bf16[2048,128]{1,0:T(8,128)(2,1)} %copy-done.4, bf16[2048,128]{1,0:T(8,128)(2,1)} %copy-done.5), custom_call_target="tpu_custom_call" | custom-call | tf_op jit(solution)/shard_map/score/pallas_call | solution.py:182
  84.1 0.0 copy-start.6
  84.1 18.1 %all-to-all-start.2 = ((f32[512,1,128]{2,1,0:T(1,128)}), f32[512,1,128]{2,1,0:T(1,128)S(1)}, u32[]{:S(2)}, u32[]{:S(2)}) async-start(f32[512,1,128]{2,1,0:T(1,128)} %bitcast.14), calls=%async_computation.2 | async-start | bytes 524288 | tf_op jit(solution)/shard_map/all_to_all | solution.py:194
  102.3 0.0 copy-done.6
  102.3 0.7 reshape.61.teacher_ref
  103.0 15.5 %all-to-all-done.2 = f32[512,1,128]{2,1,0:T(1,128)S(1)} async-done(((f32[512,1,128]{2,1,0:T(1,128)}), f32[512,1,128]{2,1,0:T(1,128)S(1)}, u32[]{:S(2)}, u32[]{:S(2)}) %all-to-all-start.2) | async-done | bytes 262176 | tf_op jit(solution)/shard_map/all_to_all | solution.py:194
  118.5 0.0 copy-start.2
  118.5 0.7 copy-done.2
  119.2 2.1 %loss.1 = f32[1,32]{1,0:T(1,128)} custom-call(s32[128]{0:T(128)} %copy-done.7, s32[128]{0:T(128)} %copy-done.8, f32[512,128]{1,0:T(8,128)} %bitcast.13, f32[32,256]{1,0:T(8,128)} %reshape.61.teacher_ref), custom_call_target="tpu_custom_call" | custom-call | tf_op jit(solution)/shard_map/loss/pallas_call | solution.py:198
  (1 shorter events, 0.0 us)
Async XLA Ops:
  2.1 5.0 %copy-start.9 = (s32[32,4]{0,1:T(4,128)S(1)}, s32[32,4]{0,1:T(4,128)}, u32[]{:S(2)}) copy-start(s32[32,4]{0,1:T(4,128)} %param.9) | copy-start | bytes 1540
  2.1 11.9 %all-to-all-start = ((f32[4,256,128]{2,1,0:T(8,128)}), f32[4,256,128]{2,1,0:T(8,128)S(1)}, u32[]{:S(2)}, u32[]{:S(2)}) async-start(f32[4,256,128]{2,1,0:T(8,128)} %bitcast.11), calls=%async_computation | async-start | bytes 1048576 | tf_op jit(solution)/shard_map/all_to_all | solution.py:146
  7.3 0.6 copy-start.7
  7.9 0.5 copy-start.8
  14.0 0.8 copy-start
  17.1 52.6 %all-to-all-start.1 = ((bf16[128,16,128]{2,1,0:T(8,128)(2,1)}), bf16[128,16,128]{2,1,0:T(8,128)(2,1)S(1)}, u32[]{:S(2)}, u32[]{:S(2)}) async-start(bf16[128,16,128]{2,1,0:T(8,128)(2,1)} %pack.1), calls=%async_computation.1 | async-start | bytes 1048576 | tf_op jit(solution)/shard_map/all_to_all | solution.py:180
  39.8 16.5 %collective-permute-start = (bf16[2048,128]{1,0:T(8,128)(2,1)}, bf16[2048,128]{1,0:T(8,128)(2,1)S(1)}, u32[]{:S(2)}, u32[]{:S(2)}) collective-permute-start(bf16[2048,128]{1,0:T(8,128)(2,1)} %passages.1.refs_1_), channel_id=1, source_target_pairs={{0,1},{1,2},{2,3},{3,0},{4,5},{5,6},{6,7},{7,4},{8,9},{9,10},{10,1... | collective-permute-start | bytes 1572872 | tf_op jit(solution)/shard_map/ppermute | solution.py:160
  42.0 24.4 %collective-permute-start.1 = (bf16[2048,128]{1,0:T(8,128)(2,1)}, bf16[2048,128]{1,0:T(8,128)(2,1)S(1)}, u32[]{:S(2)}, u32[]{:S(2)}) collective-permute-start(bf16[2048,128]{1,0:T(8,128)(2,1)} %passages.1.refs_1_), channel_id=1, source_target_pairs={{0,2},{1,3},{2,0},{3,1},{4,6},{5,7},{6,4},{7,5},{8,10},{9,11},{10,... | collective-permute-start | bytes 1572872 | tf_op jit(solution)/shard_map/ppermute | solution.py:160
  45.7 24.1 %collective-permute-start.2 = (bf16[2048,128]{1,0:T(8,128)(2,1)}, bf16[2048,128]{1,0:T(8,128)(2,1)S(1)}, u32[]{:S(2)}, u32[]{:S(2)}) collective-permute-start(bf16[2048,128]{1,0:T(8,128)(2,1)} %passages.1.refs_1_), channel_id=1, source_target_pairs={{0,3},{1,0},{2,1},{3,2},{4,7},{5,4},{6,5},{7,6},{8,11},{9,8},{10,9... | collective-permute-start | bytes 1572872 | tf_op jit(solution)/shard_map/ppermute | solution.py:160
  56.3 13.5 %copy-start.3 = (bf16[2048,128]{1,0:T(8,128)(2,1)}, bf16[2048,128]{1,0:T(8,128)(2,1)S(1)}, u32[]{:S(2)}) copy-start(bf16[2048,128]{1,0:T(8,128)(2,1)S(1)} %collective-permute-done.refs_2_) | copy-start | bytes 1572868
  66.3 3.4 %copy-start.4 = (bf16[2048,128]{1,0:T(8,128)(2,1)}, bf16[2048,128]{1,0:T(8,128)(2,1)S(1)}, u32[]{:S(2)}) copy-start(bf16[2048,128]{1,0:T(8,128)(2,1)S(1)} %collective-permute-done.1.refs_3_) | copy-start | bytes 1572868
  69.7 0.8 copy-start.5
  69.7 1.0 copy-start.1
  84.1 18.1 %copy-start.6 = (f32[32,4,64]{2,1,0:T(4,128)S(1)}, f32[32,4,64]{2,1,0:T(4,128)}, u32[]{:S(2)}) copy-start(f32[32,4,64]{2,1,0:T(4,128)} %param.8) | copy-start | bytes 98308
  84.1 34.4 %all-to-all-start.2 = ((f32[512,1,128]{2,1,0:T(1,128)}), f32[512,1,128]{2,1,0:T(1,128)S(1)}, u32[]{:S(2)}, u32[]{:S(2)}) async-start(f32[512,1,128]{2,1,0:T(1,128)} %bitcast.14), calls=%async_computation.2 | async-start | bytes 524288 | tf_op jit(solution)/shard_map/all_to_all | solution.py:194
  118.5 0.7 copy-start.2

commit v3 on v2

--- a/solution.py
+++ b/solution.py
@@ -13,7 +13,16 @@
 EXP2_SCALE = math.log2(math.e) / SOFTNESS
 EPS = 1e-6
 VMEM = pl.BlockSpec(memory_space=pltpu.VMEM)
+LIMIT = pltpu.CompilerParams(vmem_limit_bytes=24 << 20)
 SMEM = pl.BlockSpec(memory_space=pltpu.SMEM)
+
+
+def in_vmem(array):
+    return pltpu.with_memory_space_constraint(array, pltpu.MemorySpace.VMEM)
+
+
+def out_vmem(shape, dtype):
+    return pltpu.MemorySpace.VMEM(shape, dtype)
 
 
 def unit_rows(values):
@@ -32,20 +41,22 @@
     out_ref[...] = unit_rows(passages_ref[...].astype(jnp.float32)).astype(jnp.bfloat16)
 
 
-def pack_kernel(source_ref, partial_ref, out_ref, vecs):
-    share = partial_ref.shape[2]
+def pack_kernel(slot_ref, partial_ref, out_ref, vecs, slots):
+    queries = partial_ref.shape[1]
+    picks = slot_ref.shape[0] // queries
     total = partial_ref[0]
     for part in range(1, partial_ref.shape[0]):
         total = total + partial_ref[part]
     vecs[...] = unit_rows(total)
-    capacity = out_ref.shape[1] // share
-
-    def place(owner, carry):
-        rows = [vecs[source_ref[owner * capacity + rank]] for rank in range(capacity)]
-        out_ref[owner] = jnp.concatenate(rows, axis=0).astype(jnp.bfloat16)
+    slots[...] = jnp.zeros_like(slots)
+
+    def place(query, carry):
+        for pick in range(picks):
+            slots[slot_ref[query * picks + pick]] = vecs[query]
         return carry
 
-    lax.fori_loop(0, out_ref.shape[0], place, 0, unroll=8)
+    lax.fori_loop(0, queries, place, 0, unroll=8)
+    out_ref[...] = slots[...].reshape(out_ref.shape).astype(jnp.bfloat16)
 
 
 def score_kernel(capacity, *refs):
@@ -80,7 +91,7 @@
                 )
         return carry
 
-    lax.fori_loop(0, share, one_token, 0, unroll=2)
+    lax.fori_loop(0, share, one_token, 0, unroll=True)
     logs = jnp.log(jnp.sum(sums[0], axis=1))
     for token in range(1, share):
         logs = logs + jnp.log(jnp.sum(sums[token], axis=1))
@@ -93,7 +104,7 @@
         out_ref[pl.ds(part, dp, stride=parts), :] = scores
 
 
-def loss_kernel(owner_ref, rank_ref, partial_ref, teacher_ref, out_ref, scores, student):
+def loss_kernel(slot_ref, partial_ref, teacher_ref, out_ref, scores, student):
     pairs, queries, width = student.shape
     count = width // 2
     dp = scores.shape[0]
@@ -108,10 +119,10 @@
         for pair in range(pairs):
             halves = []
             for half in range(2):
-                row = (query * pairs + pair) * 2 + half
-                values = scores[pl.ds(owner_ref[row], 1), :]
+                slot = slot_ref[(query * pairs + pair) * 2 + half]
+                values = scores[pl.ds(slot // 2, 1), :]
                 turned = pltpu.roll(values, count, 1)
-                halves.append(jnp.where(rank_ref[row] == half, values, turned))
+                halves.append(jnp.where(slot % 2 == half, values, turned))
             student[pair, pl.ds(query, 1), :] = jnp.where(lane < count, halves[0], halves[1])
         return carry
 
@@ -138,9 +149,10 @@
 
     partial = pl.pallas_call(
         functools.partial(project_kernel, mp),
-        out_shape=jax.ShapeDtypeStruct((mp, queries, share, embed), jnp.float32),
+        out_shape=out_vmem((mp, queries, share, embed), jnp.float32),
         in_specs=[VMEM, VMEM],
         out_specs=VMEM,
+        compiler_params=LIMIT,
         name="project",
     )(query_hidden.reshape(queries * tokens, features), query_proj)
     partial = lax.all_to_all(
@@ -149,9 +161,10 @@
 
     own_vecs = pl.pallas_call(
         passage_kernel,
-        out_shape=jax.ShapeDtypeStruct((own_count * passage_tokens, embed), jnp.bfloat16),
+        out_shape=out_vmem((own_count * passage_tokens, embed), jnp.bfloat16),
         in_specs=[VMEM],
         out_specs=VMEM,
+        compiler_params=LIMIT,
         name="passages",
     )(passages.reshape(own_count * passage_tokens, embed))
     passage_vecs = [own_vecs]
@@ -164,24 +177,23 @@
     earlier = (owners[:, None] == owners[None, :]) & (row_ids[None, :] < row_ids[:, None])
     ranks = jnp.sum(earlier.astype(jnp.int32), axis=1)
     slot_ids = owners * capacity + ranks
-    slots = jnp.arange(dp * capacity, dtype=jnp.int32)
-    source = jnp.sum(
-        jnp.where(slots[:, None] == slot_ids[None, :], (row_ids // picks)[None, :], 0), axis=1
-    )
-
     outgoing = pl.pallas_call(
         pack_kernel,
-        out_shape=jax.ShapeDtypeStruct((dp, capacity * share, embed), jnp.bfloat16),
+        out_shape=out_vmem((dp, capacity * share, embed), jnp.bfloat16),
         in_specs=[SMEM, VMEM],
         out_specs=VMEM,
-        scratch_shapes=[pltpu.VMEM((queries, share, embed), jnp.float32)],
+        scratch_shapes=[
+            pltpu.VMEM((queries, share, embed), jnp.float32),
+            pltpu.VMEM((dp * capacity, share, embed), jnp.float32),
+        ],
+        compiler_params=LIMIT,
         name="pack",
-    )(source, partial)
+    )(slot_ids, in_vmem(partial))
     arrived = lax.all_to_all(outgoing, "dp", 0, 0, tiled=True)
 
     scores = pl.pallas_call(
         functools.partial(score_kernel, capacity),
-        out_shape=jax.ShapeDtypeStruct((dp * mp, capacity * count), jnp.float32),
+        out_shape=out_vmem((dp * mp, capacity * count), jnp.float32),
         in_specs=[VMEM] * (1 + mp),
         out_specs=VMEM,
         scratch_shapes=[
@@ -189,8 +201,9 @@
             pltpu.VMEM((share, dp * capacity, embed), jnp.bfloat16),
             pltpu.VMEM((share, count, 8, dp * capacity), jnp.float32),
         ],
+        compiler_params=LIMIT,
         name="score",
-    )(arrived.reshape(dp * capacity * share, embed), *passage_vecs)
+    )(in_vmem(arrived.reshape(dp * capacity * share, embed)), *[in_vmem(v) for v in passage_vecs])
     returned = lax.all_to_all(
         scores.reshape(dp * mp, 1, capacity * count), ("dp", "mp"), 0, 0, tiled=True
     ).reshape(dp * mp, capacity * count)
@@ -198,14 +211,15 @@
     loss = pl.pallas_call(
         loss_kernel,
         out_shape=jax.ShapeDtypeStruct((1, queries), jnp.float32),
-        in_specs=[SMEM, SMEM, VMEM, VMEM],
+        in_specs=[SMEM, VMEM, VMEM],
         out_specs=VMEM,
         scratch_shapes=[
             pltpu.VMEM((dp, capacity * count), jnp.float32),
             pltpu.VMEM((picks // 2, queries, 2 * count), jnp.float32),
         ],
+        compiler_params=LIMIT,
         name="loss",
-    )(owners, ranks, returned, teacher.reshape(queries, picks * count))
+    )(slot_ids, in_vmem(returned), teacher.reshape(queries, picks * count))
     return loss.reshape(queries)
 
 

time: 122 us -> 115 us (0.943)
  Pallas kernels: 22.2 us -> 16.4 us
  local copies, waits for them, and re-layouts: 4.26 us -> 2.15 us
  waiting for transfers between devices: 42 us -> 43.7 us
    pallas_call x4, Pallas kernels: 20.1 us -> 14.1 us  [the longest x1 11 us: scored_loss(): pl.pallas_call(functools.partial(score_kernel, capacity), out_shape=out_v...]
    all_to_all x1, waiting for transfers between devices: 4.96 us -> 6.54 us  [scored_loss(): lax.all_to_all(partial.reshape(mp, queries * share, embed), 'mp', 0, 0, t...]
    unnamed x21 -> x11, local copies, waits for them, and re-layouts: 3.45 us -> 1.94 us
  transfers between devices with their start and end apart: 6 -> 6, of which waited for: 5 -> 5; matrix products, arithmetic and copies ran while one was open for 1% -> 0% of each run, Pallas kernels for 2% -> 0%
where the time goes in v3:
time: 115 us
  starting transfers between devices  52.3 us (45%)
  waiting for transfers between devices  43.7 us (38%)
  Pallas kernels  16.4 us (14%)
  local copies, waits for them, and re-layouts  2.15 us (2%)
    ppermute x3, waiting for transfers between devices, scored_loss(): passage_vecs.append(lax.ppermute(own_vecs, 'mp', ring))  21 us
    all_to_all x1, starting transfers between devices, scored_loss(): arrived = lax.all_to_all(outgoing, 'dp', 0, 0, tiled=True)  20.5 us
    all_to_all x1, starting transfers between devices, scored_loss(): lax.all_to_all(scores.reshape(dp * mp, 1, capacity * count), ('dp', 'mp')...  18.2 us
    all_to_all x1, waiting for transfers between devices, scored_loss(): lax.all_to_all(scores.reshape(dp * mp, 1, capacity * count), ('dp', 'mp')...  16.1 us
    pallas_call x1, Pallas kernels, scored_loss(): pl.pallas_call(functools.partial(score_kernel, capacity), out_shape=out_v...  11 us
    ppermute x3, starting transfers between devices, scored_loss(): passage_vecs.append(lax.ppermute(own_vecs, 'mp', ring))  8.6 us
    all_to_all x1, waiting for transfers between devices, scored_loss(): lax.all_to_all(partial.reshape(mp, queries * share, embed), 'mp', 0, 0, t...  6.54 us
    all_to_all x1, starting transfers between devices, scored_loss(): lax.all_to_all(partial.reshape(mp, queries * share, embed), 'mp', 0, 0, t...  4.97 us
  transfers between devices with their start and end apart: 6, of which 5 were waited for; matrix products, arithmetic and copies ran while one was open for 0% of the time, Pallas kernels for 0%

profile of v3, /device:TPU:1, one launch (start us, length us, event | category | flops | bytes accessed | tf_op | source)
XLA Modules:
  0.0 114.9 jit_solution(1901492567415157099)
XLA Ops:
  0.0 0.0 copy-start
  0.0 1.0 copy-done
  1.0 0.0 copy-start.2
  1.0 0.8 copy-done.2
  1.8 1.1 project.1
  2.9 0.0 copy-start.4
  2.9 5.0 %all-to-all-start = ((f32[4,256,128]{2,1,0:T(8,128)}), f32[4,256,128]{2,1,0:T(8,128)S(1)}, u32[]{:S(2)}, u32[]{:S(2)}) async-start(f32[4,256,128]{2,1,0:T(8,128)} %bitcast.1), calls=%async_computation | async-start | bytes 1048576 | tf_op jit(solution)/shard_map/all_to_all | solution.py:158
  7.9 0.0 copy-done.4
  7.9 0.1 copy.10
  8.0 0.1 reshape.32
  8.1 0.2 convert_reduce_fusion
  8.3 6.5 %all-to-all-done = f32[4,256,128]{2,1,0:T(8,128)S(1)} async-done(((f32[4,256,128]{2,1,0:T(8,128)}), f32[4,256,128]{2,1,0:T(8,128)S(1)}, u32[]{:S(2)}, u32[]{:S(2)}) %all-to-all-start) | async-done | bytes 524320 | tf_op jit(solution)/shard_map/all_to_all | solution.py:158
  14.8 1.7 %pack.1 = bf16[128,16,128]{2,1,0:T(8,128)(2,1)} custom-call(s32[128]{0:T(128)S(1)} %multiply_add_fusion.slot_ref, f32[4,32,8,128]{3,2,1,0:T(8,128)S(1)} %bitcast.10), custom_call_target="tpu_custom_call" | custom-call | tf_op jit(solution)/shard_map/pack/pallas_call | solution.py:180
  16.5 0.0 copy-start.1
  16.5 20.5 %all-to-all-start.1 = ((bf16[128,16,128]{2,1,0:T(8,128)(2,1)}), bf16[128,16,128]{2,1,0:T(8,128)(2,1)S(1)}, u32[]{:S(2)}, u32[]{:S(2)}) async-start(bf16[128,16,128]{2,1,0:T(8,128)(2,1)} %pack.1), calls=%async_computation.1 | async-start | bytes 1048576 | tf_op jit(solution)/shard_map/all_to_all | solution.py:192
  37.0 0.0 copy-done.1
  37.0 0.4 passages.1.refs_1_
  37.4 2.2 %collective-permute-start = (bf16[2048,128]{1,0:T(8,128)(2,1)S(1)}, bf16[2048,128]{1,0:T(8,128)(2,1)S(1)}, u32[]{:S(2)}, u32[]{:S(2)}) collective-permute-start(bf16[2048,128]{1,0:T(8,128)(2,1)S(1)} %passages.1.refs_1_), channel_id=1, source_target_pairs={{0,1},{1,2},{2,3},{3,0},{4,5},{5,6},{6,7},{7,4},{8,9},{9,10},{10,1... | collective-permute-start | bytes 1572872 | tf_op jit(solution)/shard_map/ppermute | solution.py:173
  39.6 3.7 %collective-permute-start.1 = (bf16[2048,128]{1,0:T(8,128)(2,1)S(1)}, bf16[2048,128]{1,0:T(8,128)(2,1)S(1)}, u32[]{:S(2)}, u32[]{:S(2)}) collective-permute-start(bf16[2048,128]{1,0:T(8,128)(2,1)S(1)} %passages.1.refs_1_), channel_id=1, source_target_pairs={{0,2},{1,3},{2,0},{3,1},{4,6},{5,7},{6,4},{7,5},{8,10},{9,11},{10,... | collective-permute-start | bytes 1572872 | tf_op jit(solution)/shard_map/ppermute | solution.py:173
  43.3 2.7 %collective-permute-start.2 = (bf16[2048,128]{1,0:T(8,128)(2,1)S(1)}, bf16[2048,128]{1,0:T(8,128)(2,1)S(1)}, u32[]{:S(2)}, u32[]{:S(2)}) collective-permute-start(bf16[2048,128]{1,0:T(8,128)(2,1)S(1)} %passages.1.refs_1_), channel_id=1, source_target_pairs={{0,3},{1,0},{2,1},{3,2},{4,7},{5,4},{6,5},{7,6},{8,11},{9,8},{10,9... | collective-permute-start | bytes 1572872 | tf_op jit(solution)/shard_map/ppermute | solution.py:173
  46.0 7.7 %collective-permute-done.refs_2_ = bf16[2048,128]{1,0:T(8,128)(2,1)S(1)} collective-permute-done((bf16[2048,128]{1,0:T(8,128)(2,1)S(1)}, bf16[2048,128]{1,0:T(8,128)(2,1)S(1)}, u32[]{:S(2)}, u32[]{:S(2)}) %collective-permute-start) | collective-permute-done | bytes 524320 | tf_op jit(solution)/shard_map/ppermute | solution.py:173
  53.7 10.1 %collective-permute-done.1.refs_3_ = bf16[2048,128]{1,0:T(8,128)(2,1)S(1)} collective-permute-done((bf16[2048,128]{1,0:T(8,128)(2,1)S(1)}, bf16[2048,128]{1,0:T(8,128)(2,1)S(1)}, u32[]{:S(2)}, u32[]{:S(2)}) %collective-permute-start.1) | collective-permute-done | bytes 524320 | tf_op jit(solution)/shard_map/ppermute | solution.py:173
  63.8 3.3 %collective-permute-done.2.refs_4_ = bf16[2048,128]{1,0:T(8,128)(2,1)S(1)} collective-permute-done((bf16[2048,128]{1,0:T(8,128)(2,1)S(1)}, bf16[2048,128]{1,0:T(8,128)(2,1)S(1)}, u32[]{:S(2)}, u32[]{:S(2)}) %collective-permute-start.2) | collective-permute-done | bytes 524320 | tf_op jit(solution)/shard_map/ppermute | solution.py:173
  67.1 0.0 all-to-all-done.1
  67.1 11.0 %score.1 = f32[512,128]{1,0:T(8,128)} custom-call(bf16[2048,128]{1,0:T(8,128)(2,1)S(1)} %bitcast.11, bf16[2048,128]{1,0:T(8,128)(2,1)S(1)} %passages.1.refs_1_, bf16[2048,128]{1,0:T(8,128)(2,1)S(1)} %collective-permute-done.refs_2_, bf16[2048,128]{1,0:T(8,128)(2,1)S(1)} %collective-permute-done.1.refs_3_, bf16[2048,128]{1,0:T(8,128)(2,1)S(1)} %collective-permute-done.2.refs_4_), custom_call_target="tpu_custom_call" | custom-call | tf_op jit(solution)/shard_map/score/pallas_call | solution.py:194
  78.1 0.0 copy-start.3
  78.1 18.2 %all-to-all-start.2 = ((f32[512,1,128]{2,1,0:T(1,128)}), f32[512,1,128]{2,1,0:T(1,128)S(1)}, u32[]{:S(2)}, u32[]{:S(2)}) async-start(f32[512,1,128]{2,1,0:T(1,128)} %bitcast.6), calls=%async_computation.2 | async-start | bytes 524288 | tf_op jit(solution)/shard_map/all_to_all | solution.py:207
  96.3 0.0 copy-done.3
  96.3 0.1 reshape.40.teacher_ref
  96.4 16.1 %all-to-all-done.2 = f32[512,1,128]{2,1,0:T(1,128)S(1)} async-done(((f32[512,1,128]{2,1,0:T(1,128)}), f32[512,1,128]{2,1,0:T(1,128)S(1)}, u32[]{:S(2)}, u32[]{:S(2)}) %all-to-all-start.2) | async-done | bytes 262176 | tf_op jit(solution)/shard_map/all_to_all | solution.py:207
  112.6 2.3 %loss.1 = f32[1,32]{1,0:T(1,128)} custom-call(s32[128]{0:T(128)S(1)} %multiply_add_fusion.slot_ref, f32[512,128]{1,0:T(8,128)S(1)} %bitcast.12, f32[32,256]{1,0:T(8,128)S(1)} %reshape.40.teacher_ref), custom_call_target="tpu_custom_call" | custom-call | tf_op jit(solution)/shard_map/loss/pallas_call | solution.py:211
  (1 shorter events, 0.0 us)
Async XLA Ops:
  0.0 1.0 copy-start
  1.0 0.8 copy-start.2
  2.9 5.0 %copy-start.4 = (s32[32,4]{0,1:T(4,128)S(1)}, s32[32,4]{0,1:T(4,128)}, u32[]{:S(2)}) copy-start(s32[32,4]{0,1:T(4,128)} %param.9) | copy-start | bytes 1540
  2.9 11.9 %all-to-all-start = ((f32[4,256,128]{2,1,0:T(8,128)}), f32[4,256,128]{2,1,0:T(8,128)S(1)}, u32[]{:S(2)}, u32[]{:S(2)}) async-start(f32[4,256,128]{2,1,0:T(8,128)} %bitcast.1), calls=%async_computation | async-start | bytes 1048576 | tf_op jit(solution)/shard_map/all_to_all | solution.py:158
  16.5 20.5 %copy-start.1 = (bf16[16,128,128]{2,1,0:T(8,128)(2,1)S(1)}, bf16[16,128,128]{2,1,0:T(8,128)(2,1)}, u32[]{:S(2)}) copy-start(bf16[16,128,128]{2,1,0:T(8,128)(2,1)} %param.7) | copy-start | bytes 1572868
  16.5 50.6 %all-to-all-start.1 = ((bf16[128,16,128]{2,1,0:T(8,128)(2,1)}), bf16[128,16,128]{2,1,0:T(8,128)(2,1)S(1)}, u32[]{:S(2)}, u32[]{:S(2)}) async-start(bf16[128,16,128]{2,1,0:T(8,128)(2,1)} %pack.1), calls=%async_computation.1 | async-start | bytes 1048576 | tf_op jit(solution)/shard_map/all_to_all | solution.py:192
  37.4 16.3 %collective-permute-start = (bf16[2048,128]{1,0:T(8,128)(2,1)S(1)}, bf16[2048,128]{1,0:T(8,128)(2,1)S(1)}, u32[]{:S(2)}, u32[]{:S(2)}) collective-permute-start(bf16[2048,128]{1,0:T(8,128)(2,1)S(1)} %passages.1.refs_1_), channel_id=1, source_target_pairs={{0,1},{1,2},{2,3},{3,0},{4,5},{5,6},{6,7},{7,4},{8,9},{9,10},{10,1... | collective-permute-start | bytes 1572872 | tf_op jit(solution)/shard_map/ppermute | solution.py:173
  39.6 24.2 %collective-permute-start.1 = (bf16[2048,128]{1,0:T(8,128)(2,1)S(1)}, bf16[2048,128]{1,0:T(8,128)(2,1)S(1)}, u32[]{:S(2)}, u32[]{:S(2)}) collective-permute-start(bf16[2048,128]{1,0:T(8,128)(2,1)S(1)} %passages.1.refs_1_), channel_id=1, source_target_pairs={{0,2},{1,3},{2,0},{3,1},{4,6},{5,7},{6,4},{7,5},{8,10},{9,11},{10,... | collective-permute-start | bytes 1572872 | tf_op jit(solution)/shard_map/ppermute | solution.py:173
  43.3 23.8 %collective-permute-start.2 = (bf16[2048,128]{1,0:T(8,128)(2,1)S(1)}, bf16[2048,128]{1,0:T(8,128)(2,1)S(1)}, u32[]{:S(2)}, u32[]{:S(2)}) collective-permute-start(bf16[2048,128]{1,0:T(8,128)(2,1)S(1)} %passages.1.refs_1_), channel_id=1, source_target_pairs={{0,3},{1,0},{2,1},{3,2},{4,7},{5,4},{6,5},{7,6},{8,11},{9,8},{10,9... | collective-permute-start | bytes 1572872 | tf_op jit(solution)/shard_map/ppermute | solution.py:173
  78.1 18.3 %copy-start.3 = (f32[32,4,64]{2,1,0:T(4,128)S(1)}, f32[32,4,64]{2,1,0:T(4,128)}, u32[]{:S(2)}) copy-start(f32[32,4,64]{2,1,0:T(4,128)} %param.8) | copy-start | bytes 98308
  78.1 34.5 %all-to-all-start.2 = ((f32[512,1,128]{2,1,0:T(1,128)}), f32[512,1,128]{2,1,0:T(1,128)S(1)}, u32[]{:S(2)}, u32[]{:S(2)}) async-start(f32[512,1,128]{2,1,0:T(1,128)} %bitcast.6), calls=%async_computation.2 | async-start | bytes 524288 | tf_op jit(solution)/shard_map/all_to_all | solution.py:207

commit v4 on v3

--- a/solution.py
+++ b/solution.py
@@ -152,7 +152,6 @@
         out_shape=out_vmem((mp, queries, share, embed), jnp.float32),
         in_specs=[VMEM, VMEM],
         out_specs=VMEM,
-        compiler_params=LIMIT,
         name="project",
     )(query_hidden.reshape(queries * tokens, features), query_proj)
     partial = lax.all_to_all(
@@ -167,10 +166,12 @@
         compiler_params=LIMIT,
         name="passages",
     )(passages.reshape(own_count * passage_tokens, embed))
-    passage_vecs = [own_vecs]
-    for shift in range(1, mp):
-        ring = [(place, (place + shift) % mp) for place in range(mp)]
-        passage_vecs.append(lax.ppermute(own_vecs, "mp", ring))
+    up = [(place, (place + 1) % mp) for place in range(mp)]
+    down = [(place, (place + mp - 1) % mp) for place in range(mp)]
+    below = lax.ppermute(own_vecs, "mp", up)
+    above = lax.ppermute(own_vecs, "mp", down)
+    opposite = lax.ppermute(below, "mp", up)
+    passage_vecs = [own_vecs, below, opposite, above]
 
     owners = neg_blocks.reshape(rows)
     row_ids = jnp.arange(rows, dtype=jnp.int32)

time: 115 us -> 102 us (0.89)
  waiting for transfers between devices: 43.7 us -> 33 us
  starting transfers between devices: 52.3 us -> 50.4 us
  local copies, waits for them, and re-layouts: 2.15 us -> 0.31 us
    ppermute x3, waiting for transfers between devices: 21 us -> 12.1 us  [the longest x1 8.99 us: scored_loss(): above = lax.ppermute(own_vecs, 'mp', down)]
    all_to_all x1, waiting for transfers between devices: 6.54 us -> 2.89 us  [scored_loss(): lax.all_to_all(partial.reshape(mp, queries * share, embed), 'mp', 0, 0, t...]
    all_to_all x1, starting transfers between devices: 18.2 us -> 14.9 us  [scored_loss(): lax.all_to_all(scores.reshape(dp * mp, 1, capacity * count), ('dp', 'mp')...]
    unnamed x11 -> x7, local copies, waits for them, and re-layouts: 1.94 us -> 0.1 us
    all_to_all x1, waiting for transfers between devices: 0.01 us -> 1.79 us  [scored_loss(): arrived = lax.all_to_all(outgoing, 'dp', 0, 0, tiled=True)]
    all_to_all x1, starting transfers between devices: 20.5 us -> 21.7 us  [scored_loss(): arrived = lax.all_to_all(outgoing, 'dp', 0, 0, tiled=True)]
  transfers between devices with their start and end apart: 6 -> 6, of which waited for: 5 -> 5; matrix products, arithmetic and copies ran while one was open for 0% -> 0% of each run, Pallas kernels for 0% -> 2%
where the time goes in v4:
time: 102 us; the launch traced here: 101 us
  starting transfers between devices  50.4 us (49%)
  waiting for transfers between devices  33 us (32%)
  Pallas kernels  17.4 us (17%)
    all_to_all x1, starting transfers between devices, scored_loss(): arrived = lax.all_to_all(outgoing, 'dp', 0, 0, tiled=True)  21.7 us
    all_to_all x1, waiting for transfers between devices, scored_loss(): lax.all_to_all(scores.reshape(dp * mp, 1, capacity * count), ('dp', 'mp')...  16.1 us
    all_to_all x1, starting transfers between devices, scored_loss(): lax.all_to_all(scores.reshape(dp * mp, 1, capacity * count), ('dp', 'mp')...  14.9 us
    pallas_call x1, Pallas kernels, scored_loss(): pl.pallas_call(functools.partial(score_kernel, capacity), out_shape=out_v...  11 us
    ppermute x1, waiting for transfers between devices, scored_loss(): above = lax.ppermute(own_vecs, 'mp', down)  8.99 us
    all_to_all x1, starting transfers between devices, scored_loss(): lax.all_to_all(partial.reshape(mp, queries * share, embed), 'mp', 0, 0, t...  4.97 us
    ppermute x1, starting transfers between devices, scored_loss(): opposite = lax.ppermute(below, 'mp', up)  3.54 us
    ppermute x1, starting transfers between devices, scored_loss(): below = lax.ppermute(own_vecs, 'mp', up)  3.37 us
  transfers between devices with their start and end apart: 6, of which 5 were waited for; matrix products, arithmetic and copies ran while one was open for 0% of the time, Pallas kernels for 2%

profile of v4, /device:TPU:1, one launch (start us, length us, event | category | flops | bytes accessed | tf_op | source)
XLA Modules:
  0.0 101.4 jit_solution(13662795458348863959)
XLA Ops:
  0.0 2.1 %project.1 = f32[4,32,8,128]{3,2,1,0:T(8,128)} custom-call(bf16[1024,192]{1,0:T(8,128)(2,1)} %bitcast.14, bf16[192,128]{1,0:T(8,128)(2,1)} %proj_ref.1), custom_call_target="tpu_custom_call" | custom-call | tf_op jit(solution)/shard_map/project/pallas_call | solution.py:150
  2.1 0.0 copy-start
  2.1 5.0 %all-to-all-start = ((f32[4,256,128]{2,1,0:T(8,128)}), f32[4,256,128]{2,1,0:T(8,128)S(1)}, u32[]{:S(2)}, u32[]{:S(2)}) async-start(f32[4,256,128]{2,1,0:T(8,128)} %bitcast.1), calls=%async_computation | async-start | bytes 1048576 | tf_op jit(solution)/shard_map/all_to_all | solution.py:157
  7.1 0.0 copy-done
  7.1 0.0 copy-start.2
  7.1 0.4 passages.1.refs_1_
  7.5 3.4 %collective-permute-start = (bf16[2048,128]{1,0:T(8,128)(2,1)S(1)}, bf16[2048,128]{1,0:T(8,128)(2,1)S(1)}, u32[]{:S(2)}, u32[]{:S(2)}) collective-permute-start(bf16[2048,128]{1,0:T(8,128)(2,1)S(1)} %passages.1.refs_1_), channel_id=1, source_target_pairs={{0,1},{1,2},{2,3},{3,0},{4,5},{5,6},{6,7},{7,4},{8,9},{9,10},{10,1... | collective-permute-start | bytes 1572872 | tf_op jit(solution)/shard_map/ppermute | solution.py:171
  10.8 0.0 copy-done.2
  10.8 0.1 copy.10
  10.9 0.1 reshape.32
  11.0 0.2 convert_reduce_fusion
  11.2 2.9 %all-to-all-done = f32[4,256,128]{2,1,0:T(8,128)S(1)} async-done(((f32[4,256,128]{2,1,0:T(8,128)}), f32[4,256,128]{2,1,0:T(8,128)S(1)}, u32[]{:S(2)}, u32[]{:S(2)}) %all-to-all-start) | async-done | bytes 524320 | tf_op jit(solution)/shard_map/all_to_all | solution.py:157
  14.1 1.7 %pack.1 = bf16[128,16,128]{2,1,0:T(8,128)(2,1)} custom-call(s32[128]{0:T(128)S(1)} %multiply_add_fusion.slot_ref, f32[4,32,8,128]{3,2,1,0:T(8,128)S(1)} %bitcast.10), custom_call_target="tpu_custom_call" | custom-call | tf_op jit(solution)/shard_map/pack/pallas_call | solution.py:181
  15.8 21.7 %all-to-all-start.1 = ((bf16[128,16,128]{2,1,0:T(8,128)(2,1)}), bf16[128,16,128]{2,1,0:T(8,128)(2,1)S(1)}, u32[]{:S(2)}, u32[]{:S(2)}) async-start(bf16[128,16,128]{2,1,0:T(8,128)(2,1)} %pack.1), calls=%async_computation.1 | async-start | bytes 1048576 | tf_op jit(solution)/shard_map/all_to_all | solution.py:193
  37.5 1.9 %collective-permute-start.2 = (bf16[2048,128]{1,0:T(8,128)(2,1)S(1)}, bf16[2048,128]{1,0:T(8,128)(2,1)S(1)}, u32[]{:S(2)}, u32[]{:S(2)}) collective-permute-start(bf16[2048,128]{1,0:T(8,128)(2,1)S(1)} %passages.1.refs_1_), channel_id=1, source_target_pairs={{0,3},{1,0},{2,1},{3,2},{4,7},{5,4},{6,5},{7,6},{8,11},{9,8},{10,9... | collective-permute-start | bytes 1572872 | tf_op jit(solution)/shard_map/ppermute | solution.py:172
  39.5 0.0 collective-permute-done.refs_2_
  39.5 3.5 %collective-permute-start.1 = (bf16[2048,128]{1,0:T(8,128)(2,1)S(1)}, bf16[2048,128]{1,0:T(8,128)(2,1)S(1)}, u32[]{:S(2)}, u32[]{:S(2)}) collective-permute-start(bf16[2048,128]{1,0:T(8,128)(2,1)S(1)} %collective-permute-done.refs_2_), channel_id=1, source_target_pairs={{0,1},{1,2},{2,3},{3,0},{4,5},{5,6},{6,7},{7,4},{8,9},{9,10},{10,1... | collective-permute-start | bytes 1572872 | tf_op jit(solution)/shard_map/ppermute | solution.py:173
  43.0 9.0 %collective-permute-done.2.refs_4_ = bf16[2048,128]{1,0:T(8,128)(2,1)S(1)} collective-permute-done((bf16[2048,128]{1,0:T(8,128)(2,1)S(1)}, bf16[2048,128]{1,0:T(8,128)(2,1)S(1)}, u32[]{:S(2)}, u32[]{:S(2)}) %collective-permute-start.2) | collective-permute-done | bytes 524320 | tf_op jit(solution)/shard_map/ppermute | solution.py:172
  52.0 3.1 %collective-permute-done.1.refs_3_ = bf16[2048,128]{1,0:T(8,128)(2,1)S(1)} collective-permute-done((bf16[2048,128]{1,0:T(8,128)(2,1)S(1)}, bf16[2048,128]{1,0:T(8,128)(2,1)S(1)}, u32[]{:S(2)}, u32[]{:S(2)}) %collective-permute-start.1) | collective-permute-done | bytes 524320 | tf_op jit(solution)/shard_map/ppermute | solution.py:173
  55.2 1.8 %all-to-all-done.1 = bf16[128,16,128]{2,1,0:T(8,128)(2,1)S(1)} async-done(((bf16[128,16,128]{2,1,0:T(8,128)(2,1)}), bf16[128,16,128]{2,1,0:T(8,128)(2,1)S(1)}, u32[]{:S(2)}, u32[]{:S(2)}) %all-to-all-start.1) | async-done | bytes 524320 | tf_op jit(solution)/shard_map/all_to_all | solution.py:193
  57.0 11.0 %score.1 = f32[512,128]{1,0:T(8,128)} custom-call(bf16[2048,128]{1,0:T(8,128)(2,1)S(1)} %bitcast.11, bf16[2048,128]{1,0:T(8,128)(2,1)S(1)} %passages.1.refs_1_, bf16[2048,128]{1,0:T(8,128)(2,1)S(1)} %collective-permute-done.refs_2_, bf16[2048,128]{1,0:T(8,128)(2,1)S(1)} %collective-permute-done.1.refs_3_, bf16[2048,128]{1,0:T(8,128)(2,1)S(1)} %collective-permute-done.2.refs_4_), custom_call_target="tpu_custom_call" | custom-call | tf_op jit(solution)/shard_map/score/pallas_call | solution.py:195
  68.0 0.0 copy-start.1
  68.0 14.9 %all-to-all-start.2 = ((f32[512,1,128]{2,1,0:T(1,128)}), f32[512,1,128]{2,1,0:T(1,128)S(1)}, u32[]{:S(2)}, u32[]{:S(2)}) async-start(f32[512,1,128]{2,1,0:T(1,128)} %bitcast.6), calls=%async_computation.2 | async-start | bytes 524288 | tf_op jit(solution)/shard_map/all_to_all | solution.py:208
  82.8 0.0 copy-done.1
  82.9 0.1 reshape.40.teacher_ref
  83.0 16.1 %all-to-all-done.2 = f32[512,1,128]{2,1,0:T(1,128)S(1)} async-done(((f32[512,1,128]{2,1,0:T(1,128)}), f32[512,1,128]{2,1,0:T(1,128)S(1)}, u32[]{:S(2)}, u32[]{:S(2)}) %all-to-all-start.2) | async-done | bytes 262176 | tf_op jit(solution)/shard_map/all_to_all | solution.py:208
  99.1 2.3 %loss.1 = f32[1,32]{1,0:T(1,128)} custom-call(s32[128]{0:T(128)S(1)} %multiply_add_fusion.slot_ref, f32[512,128]{1,0:T(8,128)S(1)} %bitcast.12, f32[32,256]{1,0:T(8,128)S(1)} %reshape.40.teacher_ref), custom_call_target="tpu_custom_call" | custom-call | tf_op jit(solution)/shard_map/loss/pallas_call | solution.py:212
  (1 shorter events, 0.0 us)
Async XLA Ops:
  2.1 5.0 %copy-start = (bf16[16,128,128]{2,1,0:T(8,128)(2,1)S(1)}, bf16[16,128,128]{2,1,0:T(8,128)(2,1)}, u32[]{:S(2)}) copy-start(bf16[16,128,128]{2,1,0:T(8,128)(2,1)} %param.7) | copy-start | bytes 1572868
  2.1 12.0 %all-to-all-start = ((f32[4,256,128]{2,1,0:T(8,128)}), f32[4,256,128]{2,1,0:T(8,128)S(1)}, u32[]{:S(2)}, u32[]{:S(2)}) async-start(f32[4,256,128]{2,1,0:T(8,128)} %bitcast.1), calls=%async_computation | async-start | bytes 1048576 | tf_op jit(solution)/shard_map/all_to_all | solution.py:157
  7.1 3.7 %copy-start.2 = (s32[32,4]{0,1:T(4,128)S(1)}, s32[32,4]{0,1:T(4,128)}, u32[]{:S(2)}) copy-start(s32[32,4]{0,1:T(4,128)} %param.9) | copy-start | bytes 1540
  7.5 32.0 %collective-permute-start = (bf16[2048,128]{1,0:T(8,128)(2,1)S(1)}, bf16[2048,128]{1,0:T(8,128)(2,1)S(1)}, u32[]{:S(2)}, u32[]{:S(2)}) collective-permute-start(bf16[2048,128]{1,0:T(8,128)(2,1)S(1)} %passages.1.refs_1_), channel_id=1, source_target_pairs={{0,1},{1,2},{2,3},{3,0},{4,5},{5,6},{6,7},{7,4},{8,9},{9,10},{10,1... | collective-permute-start | bytes 1572872 | tf_op jit(solution)/shard_map/ppermute | solution.py:171
  15.8 41.2 %all-to-all-start.1 = ((bf16[128,16,128]{2,1,0:T(8,128)(2,1)}), bf16[128,16,128]{2,1,0:T(8,128)(2,1)S(1)}, u32[]{:S(2)}, u32[]{:S(2)}) async-start(bf16[128,16,128]{2,1,0:T(8,128)(2,1)} %pack.1), calls=%async_computation.1 | async-start | bytes 1048576 | tf_op jit(solution)/shard_map/all_to_all | solution.py:193
  37.5 14.5 %collective-permute-start.2 = (bf16[2048,128]{1,0:T(8,128)(2,1)S(1)}, bf16[2048,128]{1,0:T(8,128)(2,1)S(1)}, u32[]{:S(2)}, u32[]{:S(2)}) collective-permute-start(bf16[2048,128]{1,0:T(8,128)(2,1)S(1)} %passages.1.refs_1_), channel_id=1, source_target_pairs={{0,3},{1,0},{2,1},{3,2},{4,7},{5,4},{6,5},{7,6},{8,11},{9,8},{10,9... | collective-permute-start | bytes 1572872 | tf_op jit(solution)/shard_map/ppermute | solution.py:172
  39.5 15.7 %collective-permute-start.1 = (bf16[2048,128]{1,0:T(8,128)(2,1)S(1)}, bf16[2048,128]{1,0:T(8,128)(2,1)S(1)}, u32[]{:S(2)}, u32[]{:S(2)}) collective-permute-start(bf16[2048,128]{1,0:T(8,128)(2,1)S(1)} %collective-permute-done.refs_2_), channel_id=1, source_target_pairs={{0,1},{1,2},{2,3},{3,0},{4,5},{5,6},{6,7},{7,4},{8,9},{9,10},{10,1... | collective-permute-start | bytes 1572872 | tf_op jit(solution)/shard_map/ppermute | solution.py:173
  68.0 14.9 %copy-start.1 = (f32[32,4,64]{2,1,0:T(4,128)S(1)}, f32[32,4,64]{2,1,0:T(4,128)}, u32[]{:S(2)}) copy-start(f32[32,4,64]{2,1,0:T(4,128)} %param.8) | copy-start | bytes 98308
  68.0 31.1 %all-to-all-start.2 = ((f32[512,1,128]{2,1,0:T(1,128)}), f32[512,1,128]{2,1,0:T(1,128)S(1)}, u32[]{:S(2)}, u32[]{:S(2)}) async-start(f32[512,1,128]{2,1,0:T(1,128)} %bitcast.6), calls=%async_computation.2 | async-start | bytes 524288 | tf_op jit(solution)/shard_map/all_to_all | solution.py:208

commit v5 on v4

v5 whole, which is shorter than its diff:
```python
import functools
import math

import jax
import jax.numpy as jnp
from jax import lax
from jax.experimental import pallas as pl
from jax.experimental.pallas import tpu as pltpu
from jax.sharding import PartitionSpec as P


SOFTNESS = 0.1
EXP2_SCALE = math.log2(math.e) / SOFTNESS
EPS = 1e-6
VMEM = pl.BlockSpec(memory_space=pltpu.VMEM)
LIMIT = pltpu.CompilerParams(vmem_limit_bytes=24 << 20)
SMEM = pl.BlockSpec(memory_space=pltpu.SMEM)


def in_vmem(array):
    return pltpu.with_memory_space_constraint(array, pltpu.MemorySpace.VMEM)


def out_vmem(shape, dtype):
    return pltpu.MemorySpace.VMEM(shape, dtype)


def unit_rows(values):
    return values * lax.rsqrt(jnp.sum(values * values, axis=-1, keepdims=True) + EPS)


def project_kernel(hidden_ref, proj_ref, out_ref):
    parts, queries, share, embed = out_ref.shape
    projected = jnp.dot(hidden_ref[...], proj_ref[...], preferred_element_type=jnp.float32)
    projected = projected.reshape(queries, parts, share, embed)
    for part in range(parts):
        out_ref[part] = projected[:, part].astype(out_ref.dtype)


def passage_kernel(passages_ref, out_ref):
    out_ref[...] = unit_rows(passages_ref[...].astype(jnp.float32)).astype(jnp.bfloat16)


def pack_kernel(slot_ref, partial_ref, out_ref, vecs, slots):
    queries = partial_ref.shape[1]
    picks = slot_ref.shape[0] // queries
    total = partial_ref[0].astype(jnp.float32)
    for part in range(1, partial_ref.shape[0]):
        total = total + partial_ref[part].astype(jnp.float32)
    vecs[...] = unit_rows(total)
    slots[...] = jnp.zeros_like(slots)

    def place(query, carry):
        for pick in range(picks):
            slots[slot_ref[query * picks + pick]] = vecs[query]
        return carry

    lax.fori_loop(0, queries, place, 0, unroll=8)
    out_ref[...] = slots[...].reshape(out_ref.shape).astype(jnp.bfloat16)


def soft_sums(turned, passage_refs, sums):
    share, count, _, width = sums.shape
    own = count // len(passage_refs)
    tokens = passage_refs[0].shape[0] // own
    group = 8

    def one_token(token, carry):
        vecs = turned[token]
        for part, passage_ref in enumerate(passage_refs):
            for first in range(0, own, group):
                sims = lax.dot_general(
                    passage_ref[first * tokens : (first + group) * tokens, :],
                    vecs,
                    (((1,), (1,)), ((), ())),
                    preferred_element_type=jnp.float32,
                )
                raised = jnp.exp2(sims * EXP2_SCALE)
                place = part * own + first
                sums[token, place : place + group] = jnp.sum(
                    raised.reshape(group, tokens // 8, 8, width), axis=1
                )
        return carry

    lax.fori_loop(0, share, one_token, 0, unroll=True)
    logs = jnp.log(jnp.sum(sums[0], axis=1))
    for token in range(1, share):
        logs = logs + jnp.log(jnp.sum(sums[token], axis=1))
    return logs * SOFTNESS


def near_kernel(capacity, slots_ref, own_ref, below_ref, turned_ref, out_ref, wide, sums):
    share, width, _ = turned_ref.shape
    dp = width // capacity
    wide[...] = slots_ref[...].astype(jnp.float32)
    for token in range(share):
        for rank in range(capacity):
            rows = wide[pl.ds(rank * share + token, dp, stride=capacity * share), :]
            turned_ref[token, rank * dp : (rank + 1) * dp] = rows.astype(jnp.bfloat16)
    out_ref[...] = soft_sums(turned_ref, [own_ref, below_ref], sums)


def far_kernel(capacity, turned_ref, opposite_ref, above_ref, near_ref, out_ref, ordered, sums):
    parts = 4
    count, width = ordered.shape
    own = count // parts
    dp = width // capacity
    far = soft_sums(turned_ref, [opposite_ref, above_ref], sums)
    mine = lax.axis_index("mp")
    blocks = [near_ref[:own], near_ref[own:], far[:own], far[own:]]
    for below, block in enumerate(blocks):
        place = pl.multiple_of(lax.rem(mine + (parts - below), parts) * own, own)
        ordered[pl.ds(place, own), :] = block
    scores = jnp.concatenate(
        [ordered[:, rank * dp : (rank + 1) * dp] for rank in range(capacity)], axis=0
    ).T
    for part in range(parts):
        out_ref[pl.ds(part, dp, stride=parts), :] = scores


def loss_kernel(slot_ref, partial_ref, teacher_ref, out_ref, student):
    rows, count = student.shape
    queries = out_ref.shape[1]
    picks = rows // queries
    capacity = partial_ref.shape[1] // count
    dp = 128
    parts = partial_ref.shape[0] // dp
    total = partial_ref[pl.ds(0, dp, stride=parts), :]
    for part in range(1, parts):
        total = total + partial_ref[pl.ds(part, dp, stride=parts), :]
    table = jnp.concatenate(
        [total[:, rank * count : (rank + 1) * count] for rank in range(capacity)], axis=0
    )
    slots = slot_ref[...]
    places = lax.rem(slots, capacity) * dp + lax.div(slots, capacity)
    chosen = lax.broadcasted_iota(jnp.int32, (capacity * dp, rows), 0) == places
    student[...] = lax.dot_general(
        chosen.astype(jnp.float32),
        table,
        (((0,), (0,)), ((), ())),
        precision=lax.Precision.HIGHEST,
        preferred_element_type=jnp.float32,
    )
    teachers = [teacher_ref[pl.ds(pick, queries, stride=picks), :] for pick in range(picks)]
    students = [student[pl.ds(pick, queries, stride=picks), :] for pick in range(picks)]
    raised = sum(jnp.exp(scores) for scores in teachers)
    log_total = jnp.log(jnp.sum(raised, axis=1, keepdims=True))
    terms = 0.0
    for scores, guesses in zip(teachers, students):
        logp = scores - log_total
        terms = terms + jnp.exp(logp) * (logp - guesses)
    raised = sum(jnp.exp(guesses) for guesses in students)
    loss = jnp.sum(terms, axis=1, keepdims=True) + jnp.log(
        jnp.sum(raised, axis=1, keepdims=True)
    )
    out_ref[...] = jnp.broadcast_to(loss, (queries, 128)).T[:1]


def scored_loss(query_hidden, query_proj, passages, teacher, neg_blocks):
    dp = lax.axis_size("dp")
    mp = lax.axis_size("mp")
    queries, tokens, features = query_hidden.shape
    embed = query_proj.shape[1]
    picks = neg_blocks.shape[1]
    rows = queries * picks
    capacity = 2
    share = tokens // mp
    own_count, passage_tokens, _ = passages.shape
    count = own_count * mp

    steps = 4
    partial = pl.pallas_call(
        project_kernel,
        grid=(steps,),
        out_shape=jax.ShapeDtypeStruct((mp, queries, share, embed), jnp.bfloat16),
        in_specs=[
            pl.BlockSpec((queries * tokens // steps, features), lambda step: (step, 0)),
            pl.BlockSpec((features, embed), lambda step: (0, 0)),
        ],
        out_specs=pl.BlockSpec((mp, queries // steps, share, embed), lambda step: (0, step, 0, 0)),
        name="project",
    )(query_hidden.reshape(queries * tokens, features), query_proj)
    partial = lax.all_to_all(
        partial.reshape(mp, queries * share, embed), "mp", 0, 0, tiled=True
    ).reshape(mp, queries, share, embed)

    own_vecs = pl.pallas_call(
        passage_kernel,
        out_shape=out_vmem((own_count * passage_tokens, embed), jnp.bfloat16),
        in_specs=[VMEM],
        out_specs=VMEM,
        compiler_params=LIMIT,
        name="passages",
    )(passages.reshape(own_count * passage_tokens, embed))
    up = [(place, (place + 1) % mp) for place in range(mp)]
    down = [(place, (place + mp - 1) % mp) for place in range(mp)]
    below = lax.ppermute(own_vecs, "mp", up)
    above = lax.ppermute(own_vecs, "mp", down)
    opposite = lax.ppermute(below, "mp", up)

    owners = neg_blocks.reshape(rows)
    row_ids = jnp.arange(rows, dtype=jnp.int32)
    earlier = (owners[:, None] == owners[None, :]) & (row_ids[None, :] < row_ids[:, None])
    ranks = jnp.sum(earlier.astype(jnp.int32), axis=1)
    slot_ids = owners * capacity + ranks
    outgoing = pl.pallas_call(
        pack_kernel,
        out_shape=out_vmem((dp, capacity * share, embed), jnp.bfloat16),
        in_specs=[SMEM, VMEM],
        out_specs=VMEM,
        scratch_shapes=[
            pltpu.VMEM((queries, share, embed), jnp.float32),
            pltpu.VMEM((dp * capacity, share, embed), jnp.float32),
        ],
        compiler_params=LIMIT,
        name="pack",
    )(slot_ids, in_vmem(partial))
    arrived = lax.all_to_all(outgoing, "dp", 0, 0, tiled=True)

    turned, near = pl.pallas_call(
        functools.partial(near_kernel, capacity),
        out_shape=[
            out_vmem((share, capacity * dp, embed), jnp.bfloat16),
            out_vmem((count // 2, capacity * dp), jnp.float32),
        ],
        in_specs=[VMEM] * 3,
        out_specs=[VMEM] * 2,
        scratch_shapes=[
            pltpu.VMEM((dp * capacity * share, embed), jnp.float32),
            pltpu.VMEM((share, count // 2, 8, dp * capacity), jnp.float32),
        ],
        compiler_params=LIMIT,
        name="score_near",
    )(in_vmem(arrived.reshape(dp * capacity * share, embed)), in_vmem(own_vecs), in_vmem(below))
    scores = pl.pallas_call(
        functools.partial(far_kernel, capacity),
        out_shape=jax.ShapeDtypeStruct((dp * mp, capacity * count), jnp.float32),
        in_specs=[VMEM] * 4,
        out_specs=VMEM,
        scratch_shapes=[
            pltpu.VMEM((count, capacity * dp), jnp.float32),
            pltpu.VMEM((share, count // 2, 8, dp * capacity), jnp.float32),
        ],
        compiler_params=LIMIT,
        name="score_far",
    )(in_vmem(turned), in_vmem(opposite), in_vmem(above), in_vmem(near))
    returned = lax.all_to_all(
        scores.reshape(dp * mp, 1, capacity * count), ("dp", "mp"), 0, 0, tiled=True
    ).reshape(dp * mp, capacity * count)

    loss = pl.pallas_call(
        loss_kernel,
        out_shape=jax.ShapeDtypeStruct((1, queries), jnp.float32),
        in_specs=[VMEM] * 3,
        out_specs=VMEM,
        scratch_shapes=[pltpu.VMEM((rows, count), jnp.float32)],
        compiler_params=LIMIT,
        name="loss",
    )(slot_ids.reshape(1, rows), in_vmem(returned), teacher.reshape(rows, count))
    return loss.reshape(queries)


def solution(mesh):
    in_specs = (
        P("dp", None, "mp"),
        P("mp", None),
        P(("dp", "mp"), None, None),
        P("dp", None, None),
        P("dp", None),
    )
    return jax.shard_map(
        scored_loss, mesh=mesh, in_specs=in_specs, out_specs=P("dp"), check_vma=False
    )
```

time: 102 us -> 101 us (level)
  starting transfers between devices: 50.4 us -> 42.9 us
  waiting for transfers between devices: 33 us -> 38.4 us
  local copies, waits for them, and re-layouts: 0.31 us -> 1.43 us
    all_to_all x1, waiting for transfers between devices: 1.79 us -> 13.9 us  [scored_loss(): arrived = lax.all_to_all(outgoing, 'dp', 0, 0, tiled=True)]
    ppermute x1, waiting for transfers between devices: 8.99 us -> 0.01 us  [scored_loss(): above = lax.ppermute(own_vecs, 'mp', down)]
    all_to_all x1, waiting for transfers between devices: 2.89 us -> 8.29 us  [scored_loss(): lax.all_to_all(partial.reshape(mp, queries * share, embed), 'mp', 0, 0, t...]
    all_to_all x1, starting transfers between devices: 14.9 us -> 10.6 us  [scored_loss(): lax.all_to_all(scores.reshape(dp * mp, 1, capacity * count), ('dp', 'mp')...]
    ppermute x1, waiting for transfers between devices: 3.15 us -> 0.01 us  [scored_loss(): opposite = lax.ppermute(below, 'mp', up)]
    all_to_all x1, starting transfers between devices: 21.7 us -> 19 us  [scored_loss(): arrived = lax.all_to_all(outgoing, 'dp', 0, 0, tiled=True)]
    pallas_call x2 -> x3, Pallas kernels: 13.1 us -> 14.5 us  [the longest x1 5.7 us: scored_loss(): pl.pallas_call(functools.partial(far_kernel, capacity), out_shape=jax.Sha...]
    pallas_call x1, Pallas kernels: 2.29 us -> 1.03 us  [scored_loss(): pl.pallas_call(loss_kernel, out_shape=jax.ShapeDtypeStruct((1, queries),...]
  transfers between devices with their start and end apart: 6 -> 6, of which waited for: 5 -> 3; matrix products, arithmetic and copies ran while one was open for 0% -> 1% of each run, Pallas kernels for 2% -> 10%
where the time goes in v5:
time: 101 us
  starting transfers between devices  42.9 us (42%)
  waiting for transfers between devices  38.4 us (38%)
  Pallas kernels  17.6 us (17%)
  local copies, waits for them, and re-layouts  1.43 us (1%)
    all_to_all x1, starting transfers between devices, scored_loss(): arrived = lax.all_to_all(outgoing, 'dp', 0, 0, tiled=True)  19 us
    all_to_all x1, waiting for transfers between devices, scored_loss(): lax.all_to_all(scores.reshape(dp * mp, 1, capacity * count), ('dp', 'mp')...  16.2 us
    all_to_all x1, waiting for transfers between devices, scored_loss(): arrived = lax.all_to_all(outgoing, 'dp', 0, 0, tiled=True)  13.9 us
    all_to_all x1, starting transfers between devices, scored_loss(): lax.all_to_all(scores.reshape(dp * mp, 1, capacity * count), ('dp', 'mp')...  10.6 us
    all_to_all x1, waiting for transfers between devices, scored_loss(): lax.all_to_all(partial.reshape(mp, queries * share, embed), 'mp', 0, 0, t...  8.29 us
    pallas_call x1, Pallas kernels, scored_loss(): pl.pallas_call(functools.partial(far_kernel, capacity), out_shape=jax.Sha...  5.7 us
    pallas_call x1, Pallas kernels, scored_loss(): pl.pallas_call(functools.partial(near_kernel, capacity), out_shape=[out_v...  5.33 us
    ppermute x1, starting transfers between devices, scored_loss(): below = lax.ppermute(own_vecs, 'mp', up)  3.94 us
  transfers between devices with their start and end apart: 6, of which 3 were waited for; matrix products, arithmetic and copies ran while one was open for 1% of the time, Pallas kernels for 10%

profile of v5, /device:TPU:1, one launch (start us, length us, event | category | flops | bytes accessed | tf_op | source)
XLA Modules:
  0.0 100.6 jit_solution(14071277644002809574)
XLA Ops:
  0.0 0.0 copy-start
  0.0 1.0 %copy-done = bf16[16,128,128]{2,1,0:T(8,128)(2,1)S(1)} copy-done((bf16[16,128,128]{2,1,0:T(8,128)(2,1)S(1)}, bf16[16,128,128]{2,1,0:T(8,128)(2,1)}, u32[]{:S(2)}) %copy-start) | copy-done | bytes 524312
  1.0 0.4 passages.1.own_ref
  1.4 3.9 %collective-permute-start = (bf16[2048,128]{1,0:T(8,128)(2,1)S(1)}, bf16[2048,128]{1,0:T(8,128)(2,1)S(1)}, u32[]{:S(2)}, u32[]{:S(2)}) collective-permute-start(bf16[2048,128]{1,0:T(8,128)(2,1)S(1)} %passages.1.own_ref), channel_id=1, source_target_pairs={{0,1},{1,2},{2,3},{3,0},{4,5},{5,6},{6,7},{7,4},{8,9},{9,10},{10,1... | collective-permute-start | bytes 1572872 | tf_op jit(solution)/shard_map/ppermute | solution.py:197
  5.3 3.5 %project.1 = bf16[4,32,8,128]{3,2,1,0:T(8,128)(2,1)} custom-call(bf16[1024,192]{1,0:T(8,128)(2,1)} %bitcast.19, bf16[192,128]{1,0:T(8,128)(2,1)} %proj_ref.1), custom_call_target="tpu_custom_call" | custom-call | tf_op jit(solution)/shard_map/project/pallas_call | solution.py:172
  8.8 0.0 copy-start.2
  8.8 3.9 %all-to-all-start = ((bf16[4,256,128]{2,1,0:T(8,128)(2,1)}), bf16[4,256,128]{2,1,0:T(8,128)(2,1)S(1)}, u32[]{:S(2)}, u32[]{:S(2)}) async-start(bf16[4,256,128]{2,1,0:T(8,128)(2,1)} %bitcast.18), calls=%async_computation | async-start | bytes 524288 | tf_op jit(solution)/shard_map/all_to_all | solution.py:183
  12.7 0.0 copy-done.2
  12.7 0.1 copy.14
  12.8 0.1 eq.15
  12.9 0.2 convert_reduce_fusion
  13.1 8.3 %all-to-all-done = bf16[4,256,128]{2,1,0:T(8,128)(2,1)S(1)} async-done(((bf16[4,256,128]{2,1,0:T(8,128)(2,1)}), bf16[4,256,128]{2,1,0:T(8,128)(2,1)S(1)}, u32[]{:S(2)}, u32[]{:S(2)}) %all-to-all-start) | async-done | bytes 262176 | tf_op jit(solution)/shard_map/all_to_all | solution.py:183
  21.4 1.7 %pack.1 = bf16[128,16,128]{2,1,0:T(8,128)(2,1)} custom-call(s32[128]{0:T(128)S(1)} %multiply_add_fusion.slot_ref, bf16[4,32,8,128]{3,2,1,0:T(8,128)(2,1)S(1)} %bitcast.15), custom_call_target="tpu_custom_call" | custom-call | tf_op jit(solution)/shard_map/pack/pallas_call | solution.py:206
  23.0 19.0 %all-to-all-start.1 = ((bf16[128,16,128]{2,1,0:T(8,128)(2,1)}), bf16[128,16,128]{2,1,0:T(8,128)(2,1)S(1)}, u32[]{:S(2)}, u32[]{:S(2)}) async-start(bf16[128,16,128]{2,1,0:T(8,128)(2,1)} %pack.1), calls=%async_computation.1 | async-start | bytes 1048576 | tf_op jit(solution)/shard_map/all_to_all | solution.py:218
  42.0 1.9 %collective-permute-start.2 = (bf16[2048,128]{1,0:T(8,128)(2,1)S(1)}, bf16[2048,128]{1,0:T(8,128)(2,1)S(1)}, u32[]{:S(2)}, u32[]{:S(2)}) collective-permute-start(bf16[2048,128]{1,0:T(8,128)(2,1)S(1)} %passages.1.own_ref), channel_id=1, source_target_pairs={{0,3},{1,0},{2,1},{3,2},{4,7},{5,4},{6,5},{7,6},{8,11},{9,8},{10,9... | collective-permute-start | bytes 1572872 | tf_op jit(solution)/shard_map/ppermute | solution.py:198
  44.0 0.0 collective-permute-done.below_ref
  44.0 3.5 %collective-permute-start.1 = (bf16[2048,128]{1,0:T(8,128)(2,1)S(1)}, bf16[2048,128]{1,0:T(8,128)(2,1)S(1)}, u32[]{:S(2)}, u32[]{:S(2)}) collective-permute-start(bf16[2048,128]{1,0:T(8,128)(2,1)S(1)} %collective-permute-done.below_ref), channel_id=1, source_target_pairs={{0,1},{1,2},{2,3},{3,0},{4,5},{5,6},{6,7},{7,4},{8,9},{9,10},{10,1... | collective-permute-start | bytes 1572872 | tf_op jit(solution)/shard_map/ppermute | solution.py:199
  47.5 13.9 %all-to-all-done.1 = bf16[128,16,128]{2,1,0:T(8,128)(2,1)S(1)} async-done(((bf16[128,16,128]{2,1,0:T(8,128)(2,1)}), bf16[128,16,128]{2,1,0:T(8,128)(2,1)S(1)}, u32[]{:S(2)}, u32[]{:S(2)}) %all-to-all-start.1) | async-done | bytes 524320 | tf_op jit(solution)/shard_map/all_to_all | solution.py:218
  61.5 5.3 %score_near.1 = (bf16[8,256,128]{2,1,0:T(8,128)(2,1)S(1)}, f32[32,256]{1,0:T(8,128)S(1)}) custom-call(bf16[2048,128]{1,0:T(8,128)(2,1)S(1)} %bitcast.13, bf16[2048,128]{1,0:T(8,128)(2,1)S(1)} %passages.1.own_ref, bf16[2048,128]{1,0:T(8,128)(2,1)S(1)} %collective-permute-done.below_ref), custom_call_target="tpu_custom_call" | custom-call | tf_op jit(solution)/shard_map/score_near/pallas_call | solution.py:220
  66.8 0.0 collective-permute-done.2.above_ref
  66.8 0.0 collective-permute-done.1.opposite_ref
  66.8 5.7 %score_far.1 = f32[512,128]{1,0:T(8,128)} custom-call(bf16[8,256,128]{2,1,0:T(8,128)(2,1)S(1)} %get-tuple-element.7.turned_ref, bf16[2048,128]{1,0:T(8,128)(2,1)S(1)} %collective-permute-done.1.opposite_ref, bf16[2048,128]{1,0:T(8,128)(2,1)S(1)} %collective-permute-done.2.above_ref, f32[32,256]{1,0:T(8,128)S(1)} %get-tuple-element.8.near_ref), custom_call_target="tpu_custom_call" | custom-call | tf_op jit(solution)/shard_map/score_far/pallas_call | solution.py:235
  72.5 0.0 copy-start.1
  72.5 10.6 %all-to-all-start.2 = ((f32[512,1,128]{2,1,0:T(1,128)}), f32[512,1,128]{2,1,0:T(1,128)S(1)}, u32[]{:S(2)}, u32[]{:S(2)}) async-start(f32[512,1,128]{2,1,0:T(1,128)} %bitcast.7), calls=%async_computation.2 | async-start | bytes 524288 | tf_op jit(solution)/shard_map/all_to_all | solution.py:247
  83.1 0.1 copy.13
  83.2 0.1 mul.22
  83.4 16.2 %all-to-all-done.2 = f32[512,1,128]{2,1,0:T(1,128)S(1)} async-done(((f32[512,1,128]{2,1,0:T(1,128)}), f32[512,1,128]{2,1,0:T(1,128)S(1)}, u32[]{:S(2)}, u32[]{:S(2)}) %all-to-all-start.2) | async-done | bytes 262176 | tf_op jit(solution)/shard_map/all_to_all | solution.py:247
  99.5 0.0 copy-done.1
  99.5 1.0 %loss.1 = f32[1,32]{1,0:T(1,128)} custom-call(s32[1,128]{1,0:T(1,128)S(1)} %bitcast_add_fusion.slot_ref, f32[512,128]{1,0:T(8,128)S(1)} %bitcast.14, f32[128,64]{1,0:T(8,128)S(1)} %bitcast.17), custom_call_target="tpu_custom_call" | custom-call | tf_op jit(solution)/shard_map/loss/pallas_call | solution.py:251
  (3 shorter events, 0.0 us)
Async XLA Ops:
  0.0 1.0 %copy-start = (bf16[16,128,128]{2,1,0:T(8,128)(2,1)S(1)}, bf16[16,128,128]{2,1,0:T(8,128)(2,1)}, u32[]{:S(2)}) copy-start(bf16[16,128,128]{2,1,0:T(8,128)(2,1)} %param.7) | copy-start | bytes 1572868
  1.4 42.6 %collective-permute-start = (bf16[2048,128]{1,0:T(8,128)(2,1)S(1)}, bf16[2048,128]{1,0:T(8,128)(2,1)S(1)}, u32[]{:S(2)}, u32[]{:S(2)}) collective-permute-start(bf16[2048,128]{1,0:T(8,128)(2,1)S(1)} %passages.1.own_ref), channel_id=1, source_target_pairs={{0,1},{1,2},{2,3},{3,0},{4,5},{5,6},{6,7},{7,4},{8,9},{9,10},{10,1... | collective-permute-start | bytes 1572872 | tf_op jit(solution)/shard_map/ppermute | solution.py:197
  8.8 3.9 %copy-start.2 = (s32[32,4]{0,1:T(4,128)S(1)}, s32[32,4]{0,1:T(4,128)}, u32[]{:S(2)}) copy-start(s32[32,4]{0,1:T(4,128)} %param.9) | copy-start | bytes 1540
  8.8 12.5 %all-to-all-start = ((bf16[4,256,128]{2,1,0:T(8,128)(2,1)}), bf16[4,256,128]{2,1,0:T(8,128)(2,1)S(1)}, u32[]{:S(2)}, u32[]{:S(2)}) async-start(bf16[4,256,128]{2,1,0:T(8,128)(2,1)} %bitcast.18), calls=%async_computation | async-start | bytes 524288 | tf_op jit(solution)/shard_map/all_to_all | solution.py:183
  23.0 38.4 %all-to-all-start.1 = ((bf16[128,16,128]{2,1,0:T(8,128)(2,1)}), bf16[128,16,128]{2,1,0:T(8,128)(2,1)S(1)}, u32[]{:S(2)}, u32[]{:S(2)}) async-start(bf16[128,16,128]{2,1,0:T(8,128)(2,1)} %pack.1), calls=%async_computation.1 | async-start | bytes 1048576 | tf_op jit(solution)/shard_map/all_to_all | solution.py:218
  42.0 24.8 %collective-permute-start.2 = (bf16[2048,128]{1,0:T(8,128)(2,1)S(1)}, bf16[2048,128]{1,0:T(8,128)(2,1)S(1)}, u32[]{:S(2)}, u32[]{:S(2)}) collective-permute-start(bf16[2048,128]{1,0:T(8,128)(2,1)S(1)} %passages.1.own_ref), channel_id=1, source_target_pairs={{0,3},{1,0},{2,1},{3,2},{4,7},{5,4},{6,5},{7,6},{8,11},{9,8},{10,9... | collective-permute-start | bytes 1572872 | tf_op jit(solution)/shard_map/ppermute | solution.py:198
  44.0 22.8 %collective-permute-start.1 = (bf16[2048,128]{1,0:T(8,128)(2,1)S(1)}, bf16[2048,128]{1,0:T(8,128)(2,1)S(1)}, u32[]{:S(2)}, u32[]{:S(2)}) collective-permute-start(bf16[2048,128]{1,0:T(8,128)(2,1)S(1)} %collective-permute-done.below_ref), channel_id=1, source_target_pairs={{0,1},{1,2},{2,3},{3,0},{4,5},{5,6},{6,7},{7,4},{8,9},{9,10},{10,1... | collective-permute-start | bytes 1572872 | tf_op jit(solution)/shard_map/ppermute | solution.py:199
  72.5 27.0 %copy-start.1 = (f32[32,4,64]{2,1,0:T(4,128)S(1)}, f32[32,4,64]{2,1,0:T(4,128)}, u32[]{:S(2)}) copy-start(f32[32,4,64]{2,1,0:T(4,128)} %param.8) | copy-start | bytes 98308
  72.5 27.0 %all-to-all-start.2 = ((f32[512,1,128]{2,1,0:T(1,128)}), f32[512,1,128]{2,1,0:T(1,128)S(1)}, u32[]{:S(2)}, u32[]{:S(2)}) async-start(f32[512,1,128]{2,1,0:T(1,128)} %bitcast.7), calls=%async_computation.2 | async-start | bytes 524288 | tf_op jit(solution)/shard_map/all_to_all | solution.py:247

commit v6 on v5

--- a/solution.py
+++ b/solution.py
@@ -168,16 +168,11 @@
     own_count, passage_tokens, _ = passages.shape
     count = own_count * mp
 
-    steps = 4
     partial = pl.pallas_call(
         project_kernel,
-        grid=(steps,),
         out_shape=jax.ShapeDtypeStruct((mp, queries, share, embed), jnp.bfloat16),
-        in_specs=[
-            pl.BlockSpec((queries * tokens // steps, features), lambda step: (step, 0)),
-            pl.BlockSpec((features, embed), lambda step: (0, 0)),
-        ],
-        out_specs=pl.BlockSpec((mp, queries // steps, share, embed), lambda step: (0, step, 0, 0)),
+        in_specs=[VMEM, VMEM],
+        out_specs=VMEM,
         name="project",
     )(query_hidden.reshape(queries * tokens, features), query_proj)
     partial = lax.all_to_all(

time: 101 us -> 101 us (level)
  Pallas kernels: 17.6 us -> 16.1 us
  waiting for transfers between devices: 38.4 us -> 39.9 us
    all_to_all x1, waiting for transfers between devices: 8.29 us -> 9.74 us  [scored_loss(): lax.all_to_all(partial.reshape(mp, queries * share, embed), 'mp', 0, 0, t...]
    pallas_call x1, Pallas kernels: 3.48 us -> 2.04 us  [scored_loss(): pl.pallas_call(project_kernel, out_shape=jax.ShapeDtypeStruct((mp, querie...]
  transfers between devices with their start and end apart: 6 -> 6, of which waited for: 3 -> 3; matrix products, arithmetic and copies ran while one was open for 1% -> 1% of each run, Pallas kernels for 10% -> 9%
where the time goes in v6:
time: 101 us
  starting transfers between devices  42.8 us (42%)
  waiting for transfers between devices  39.9 us (40%)
  Pallas kernels  16.1 us (16%)
  local copies, waits for them, and re-layouts  1.43 us (1%)
    all_to_all x1, starting transfers between devices, scored_loss(): arrived = lax.all_to_all(outgoing, 'dp', 0, 0, tiled=True)  19 us
    all_to_all x1, waiting for transfers between devices, scored_loss(): lax.all_to_all(scores.reshape(dp * mp, 1, capacity * count), ('dp', 'mp')...  16.2 us
    all_to_all x1, waiting for transfers between devices, scored_loss(): arrived = lax.all_to_all(outgoing, 'dp', 0, 0, tiled=True)  13.9 us
    all_to_all x1, starting transfers between devices, scored_loss(): lax.all_to_all(scores.reshape(dp * mp, 1, capacity * count), ('dp', 'mp')...  10.6 us
    all_to_all x1, waiting for transfers between devices, scored_loss(): lax.all_to_all(partial.reshape(mp, queries * share, embed), 'mp', 0, 0, t...  9.74 us
    pallas_call x1, Pallas kernels, scored_loss(): pl.pallas_call(functools.partial(far_kernel, capacity), out_shape=jax.Sha...  5.7 us
    pallas_call x1, Pallas kernels, scored_loss(): pl.pallas_call(functools.partial(near_kernel, capacity), out_shape=[out_v...  5.33 us
    ppermute x1, starting transfers between devices, scored_loss(): below = lax.ppermute(own_vecs, 'mp', up)  3.94 us
  transfers between devices with their start and end apart: 6, of which 3 were waited for; matrix products, arithmetic and copies ran while one was open for 1% of the time, Pallas kernels for 9%

profile of v6, /device:TPU:1, one launch (start us, length us, event | category | flops | bytes accessed | tf_op | source)
XLA Modules:
  0.0 100.6 jit_solution(2282731910772889739)
XLA Ops:
  0.0 0.0 copy-start
  0.0 1.0 %copy-done = bf16[16,128,128]{2,1,0:T(8,128)(2,1)S(1)} copy-done((bf16[16,128,128]{2,1,0:T(8,128)(2,1)S(1)}, bf16[16,128,128]{2,1,0:T(8,128)(2,1)}, u32[]{:S(2)}) %copy-start) | copy-done | bytes 524312
  1.0 0.4 passages.1.own_ref
  1.4 3.9 %collective-permute-start = (bf16[2048,128]{1,0:T(8,128)(2,1)S(1)}, bf16[2048,128]{1,0:T(8,128)(2,1)S(1)}, u32[]{:S(2)}, u32[]{:S(2)}) collective-permute-start(bf16[2048,128]{1,0:T(8,128)(2,1)S(1)} %passages.1.own_ref), channel_id=1, source_target_pairs={{0,1},{1,2},{2,3},{3,0},{4,5},{5,6},{6,7},{7,4},{8,9},{9,10},{10,1... | collective-permute-start | bytes 1572872 | tf_op jit(solution)/shard_map/ppermute | solution.py:192
  5.3 2.0 %project.1 = bf16[4,32,8,128]{3,2,1,0:T(8,128)(2,1)} custom-call(bf16[1024,192]{1,0:T(8,128)(2,1)} %bitcast.19, bf16[192,128]{1,0:T(8,128)(2,1)} %proj_ref.1), custom_call_target="tpu_custom_call" | custom-call | tf_op jit(solution)/shard_map/project/pallas_call | solution.py:171
  7.4 0.0 copy-start.2
  7.4 3.9 %all-to-all-start = ((bf16[4,256,128]{2,1,0:T(8,128)(2,1)}), bf16[4,256,128]{2,1,0:T(8,128)(2,1)S(1)}, u32[]{:S(2)}, u32[]{:S(2)}) async-start(bf16[4,256,128]{2,1,0:T(8,128)(2,1)} %bitcast.18), calls=%async_computation | async-start | bytes 524288 | tf_op jit(solution)/shard_map/all_to_all | solution.py:178
  11.2 0.0 copy-done.2
  11.3 0.1 copy.14
  11.3 0.1 eq.15
  11.4 0.2 convert_reduce_fusion
  11.6 9.7 %all-to-all-done = bf16[4,256,128]{2,1,0:T(8,128)(2,1)S(1)} async-done(((bf16[4,256,128]{2,1,0:T(8,128)(2,1)}), bf16[4,256,128]{2,1,0:T(8,128)(2,1)S(1)}, u32[]{:S(2)}, u32[]{:S(2)}) %all-to-all-start) | async-done | bytes 262176 | tf_op jit(solution)/shard_map/all_to_all | solution.py:178
  21.4 1.7 %pack.1 = bf16[128,16,128]{2,1,0:T(8,128)(2,1)} custom-call(s32[128]{0:T(128)S(1)} %multiply_add_fusion.slot_ref, bf16[4,32,8,128]{3,2,1,0:T(8,128)(2,1)S(1)} %bitcast.15), custom_call_target="tpu_custom_call" | custom-call | tf_op jit(solution)/shard_map/pack/pallas_call | solution.py:201
  23.1 19.0 %all-to-all-start.1 = ((bf16[128,16,128]{2,1,0:T(8,128)(2,1)}), bf16[128,16,128]{2,1,0:T(8,128)(2,1)S(1)}, u32[]{:S(2)}, u32[]{:S(2)}) async-start(bf16[128,16,128]{2,1,0:T(8,128)(2,1)} %pack.1), calls=%async_computation.1 | async-start | bytes 1048576 | tf_op jit(solution)/shard_map/all_to_all | solution.py:213
  42.0 1.9 %collective-permute-start.2 = (bf16[2048,128]{1,0:T(8,128)(2,1)S(1)}, bf16[2048,128]{1,0:T(8,128)(2,1)S(1)}, u32[]{:S(2)}, u32[]{:S(2)}) collective-permute-start(bf16[2048,128]{1,0:T(8,128)(2,1)S(1)} %passages.1.own_ref), channel_id=1, source_target_pairs={{0,3},{1,0},{2,1},{3,2},{4,7},{5,4},{6,5},{7,6},{8,11},{9,8},{10,9... | collective-permute-start | bytes 1572872 | tf_op jit(solution)/shard_map/ppermute | solution.py:193
  44.0 0.0 collective-permute-done.below_ref
  44.0 3.5 %collective-permute-start.1 = (bf16[2048,128]{1,0:T(8,128)(2,1)S(1)}, bf16[2048,128]{1,0:T(8,128)(2,1)S(1)}, u32[]{:S(2)}, u32[]{:S(2)}) collective-permute-start(bf16[2048,128]{1,0:T(8,128)(2,1)S(1)} %collective-permute-done.below_ref), channel_id=1, source_target_pairs={{0,1},{1,2},{2,3},{3,0},{4,5},{5,6},{6,7},{7,4},{8,9},{9,10},{10,1... | collective-permute-start | bytes 1572872 | tf_op jit(solution)/shard_map/ppermute | solution.py:194
  47.5 13.9 %all-to-all-done.1 = bf16[128,16,128]{2,1,0:T(8,128)(2,1)S(1)} async-done(((bf16[128,16,128]{2,1,0:T(8,128)(2,1)}), bf16[128,16,128]{2,1,0:T(8,128)(2,1)S(1)}, u32[]{:S(2)}, u32[]{:S(2)}) %all-to-all-start.1) | async-done | bytes 524320 | tf_op jit(solution)/shard_map/all_to_all | solution.py:213
  61.5 5.3 %score_near.1 = (bf16[8,256,128]{2,1,0:T(8,128)(2,1)S(1)}, f32[32,256]{1,0:T(8,128)S(1)}) custom-call(bf16[2048,128]{1,0:T(8,128)(2,1)S(1)} %bitcast.13, bf16[2048,128]{1,0:T(8,128)(2,1)S(1)} %passages.1.own_ref, bf16[2048,128]{1,0:T(8,128)(2,1)S(1)} %collective-permute-done.below_ref), custom_call_target="tpu_custom_call" | custom-call | tf_op jit(solution)/shard_map/score_near/pallas_call | solution.py:215
  66.8 0.0 collective-permute-done.2.above_ref
  66.8 0.0 collective-permute-done.1.opposite_ref
  66.8 5.7 %score_far.1 = f32[512,128]{1,0:T(8,128)} custom-call(bf16[8,256,128]{2,1,0:T(8,128)(2,1)S(1)} %get-tuple-element.7.turned_ref, bf16[2048,128]{1,0:T(8,128)(2,1)S(1)} %collective-permute-done.1.opposite_ref, bf16[2048,128]{1,0:T(8,128)(2,1)S(1)} %collective-permute-done.2.above_ref, f32[32,256]{1,0:T(8,128)S(1)} %get-tuple-element.8.near_ref), custom_call_target="tpu_custom_call" | custom-call | tf_op jit(solution)/shard_map/score_far/pallas_call | solution.py:230
  72.5 0.0 copy-start.1
  72.5 10.6 %all-to-all-start.2 = ((f32[512,1,128]{2,1,0:T(1,128)}), f32[512,1,128]{2,1,0:T(1,128)S(1)}, u32[]{:S(2)}, u32[]{:S(2)}) async-start(f32[512,1,128]{2,1,0:T(1,128)} %bitcast.7), calls=%async_computation.2 | async-start | bytes 524288 | tf_op jit(solution)/shard_map/all_to_all | solution.py:242
  83.1 0.1 copy.13
  83.2 0.1 mul.22
  83.4 16.2 %all-to-all-done.2 = f32[512,1,128]{2,1,0:T(1,128)S(1)} async-done(((f32[512,1,128]{2,1,0:T(1,128)}), f32[512,1,128]{2,1,0:T(1,128)S(1)}, u32[]{:S(2)}, u32[]{:S(2)}) %all-to-all-start.2) | async-done | bytes 262176 | tf_op jit(solution)/shard_map/all_to_all | solution.py:242
  99.5 0.0 copy-done.1
  99.5 1.0 %loss.1 = f32[1,32]{1,0:T(1,128)} custom-call(s32[1,128]{1,0:T(1,128)S(1)} %bitcast_add_fusion.slot_ref, f32[512,128]{1,0:T(8,128)S(1)} %bitcast.14, f32[128,64]{1,0:T(8,128)S(1)} %bitcast.17), custom_call_target="tpu_custom_call" | custom-call | tf_op jit(solution)/shard_map/loss/pallas_call | solution.py:246
  (3 shorter events, 0.0 us)
Async XLA Ops:
  0.0 1.0 %copy-start = (bf16[16,128,128]{2,1,0:T(8,128)(2,1)S(1)}, bf16[16,128,128]{2,1,0:T(8,128)(2,1)}, u32[]{:S(2)}) copy-start(bf16[16,128,128]{2,1,0:T(8,128)(2,1)} %param.7) | copy-start | bytes 1572868
  1.4 42.6 %collective-permute-start = (bf16[2048,128]{1,0:T(8,128)(2,1)S(1)}, bf16[2048,128]{1,0:T(8,128)(2,1)S(1)}, u32[]{:S(2)}, u32[]{:S(2)}) collective-permute-start(bf16[2048,128]{1,0:T(8,128)(2,1)S(1)} %passages.1.own_ref), channel_id=1, source_target_pairs={{0,1},{1,2},{2,3},{3,0},{4,5},{5,6},{6,7},{7,4},{8,9},{9,10},{10,1... | collective-permute-start | bytes 1572872 | tf_op jit(solution)/shard_map/ppermute | solution.py:192
  7.4 3.9 %copy-start.2 = (s32[32,4]{0,1:T(4,128)S(1)}, s32[32,4]{0,1:T(4,128)}, u32[]{:S(2)}) copy-start(s32[32,4]{0,1:T(4,128)} %param.9) | copy-start | bytes 1540
  7.4 14.0 %all-to-all-start = ((bf16[4,256,128]{2,1,0:T(8,128)(2,1)}), bf16[4,256,128]{2,1,0:T(8,128)(2,1)S(1)}, u32[]{:S(2)}, u32[]{:S(2)}) async-start(bf16[4,256,128]{2,1,0:T(8,128)(2,1)} %bitcast.18), calls=%async_computation | async-start | bytes 524288 | tf_op jit(solution)/shard_map/all_to_all | solution.py:178
  23.1 38.4 %all-to-all-start.1 = ((bf16[128,16,128]{2,1,0:T(8,128)(2,1)}), bf16[128,16,128]{2,1,0:T(8,128)(2,1)S(1)}, u32[]{:S(2)}, u32[]{:S(2)}) async-start(bf16[128,16,128]{2,1,0:T(8,128)(2,1)} %pack.1), calls=%async_computation.1 | async-start | bytes 1048576 | tf_op jit(solution)/shard_map/all_to_all | solution.py:213
  42.0 24.8 %collective-permute-start.2 = (bf16[2048,128]{1,0:T(8,128)(2,1)S(1)}, bf16[2048,128]{1,0:T(8,128)(2,1)S(1)}, u32[]{:S(2)}, u32[]{:S(2)}) collective-permute-start(bf16[2048,128]{1,0:T(8,128)(2,1)S(1)} %passages.1.own_ref), channel_id=1, source_target_pairs={{0,3},{1,0},{2,1},{3,2},{4,7},{5,4},{6,5},{7,6},{8,11},{9,8},{10,9... | collective-permute-start | bytes 1572872 | tf_op jit(solution)/shard_map/ppermute | solution.py:193
  44.0 22.8 %collective-permute-start.1 = (bf16[2048,128]{1,0:T(8,128)(2,1)S(1)}, bf16[2048,128]{1,0:T(8,128)(2,1)S(1)}, u32[]{:S(2)}, u32[]{:S(2)}) collective-permute-start(bf16[2048,128]{1,0:T(8,128)(2,1)S(1)} %collective-permute-done.below_ref), channel_id=1, source_target_pairs={{0,1},{1,2},{2,3},{3,0},{4,5},{5,6},{6,7},{7,4},{8,9},{9,10},{10,1... | collective-permute-start | bytes 1572872 | tf_op jit(solution)/shard_map/ppermute | solution.py:194
  72.5 27.0 %copy-start.1 = (f32[32,4,64]{2,1,0:T(4,128)S(1)}, f32[32,4,64]{2,1,0:T(4,128)}, u32[]{:S(2)}) copy-start(f32[32,4,64]{2,1,0:T(4,128)} %param.8) | copy-start | bytes 98308
  72.5 27.0 %all-to-all-start.2 = ((f32[512,1,128]{2,1,0:T(1,128)}), f32[512,1,128]{2,1,0:T(1,128)S(1)}, u32[]{:S(2)}, u32[]{:S(2)}) async-start(f32[512,1,128]{2,1,0:T(1,128)} %bitcast.7), calls=%async_computation.2 | async-start | bytes 524288 | tf_op jit(solution)/shard_map/all_to_all | solution.py:242

commit v7 on v6

--- a/solution.py
+++ b/solution.py
@@ -14,6 +14,7 @@
 EPS = 1e-6
 VMEM = pl.BlockSpec(memory_space=pltpu.VMEM)
 LIMIT = pltpu.CompilerParams(vmem_limit_bytes=24 << 20)
+ANY = pl.BlockSpec(memory_space=pl.ANY)
 SMEM = pl.BlockSpec(memory_space=pltpu.SMEM)
 
 
@@ -29,19 +30,48 @@
     return values * lax.rsqrt(jnp.sum(values * values, axis=-1, keepdims=True) + EPS)
 
 
-def project_kernel(hidden_ref, proj_ref, out_ref):
+def project_kernel(hidden_ref, proj_ref, out_ref, hidden, proj, projected, arrivals, leaves, ready):
     parts, queries, share, embed = out_ref.shape
-    projected = jnp.dot(hidden_ref[...], proj_ref[...], preferred_element_type=jnp.float32)
-    projected = projected.reshape(queries, parts, share, embed)
-    for part in range(parts):
-        out_ref[part] = projected[:, part].astype(out_ref.dtype)
+    steps = arrivals.shape[0]
+    rows = hidden.shape[0] // steps
+    some = queries // steps
+
+    def arrival(step):
+        block = pl.ds(step * rows, rows)
+        return pltpu.make_async_copy(hidden_ref.at[block], hidden.at[block], arrivals.at[step])
+
+    def leave(step):
+        block = pl.ds(step * some, some)
+        return pltpu.make_async_copy(
+            projected.at[:, block], out_ref.at[:, block], leaves.at[step]
+        )
+
+    whole = pltpu.make_async_copy(proj_ref, proj, ready)
+    whole.start()
+    for step in range(steps):
+        arrival(step).start()
+    whole.wait()
+    for step in range(steps):
+        arrival(step).wait()
+        block = jnp.dot(
+            hidden[step * rows : (step + 1) * rows],
+            proj[...],
+            preferred_element_type=jnp.float32,
+        ).reshape(some, parts, share, embed)
+        for part in range(parts):
+            projected[part, step * some : (step + 1) * some] = block[:, part].astype(
+                projected.dtype
+            )
+        leave(step).start()
+    for step in range(steps):
+        leave(step).wait()
 
 
 def passage_kernel(passages_ref, out_ref):
     out_ref[...] = unit_rows(passages_ref[...].astype(jnp.float32)).astype(jnp.bfloat16)
 
 
-def pack_kernel(slot_ref, partial_ref, out_ref, vecs, slots):
+def pack_kernel(slot_ref, partial_ref, out_ref, vecs, slots, packed, leaves):
     queries = partial_ref.shape[1]
     picks = slot_ref.shape[0] // queries
     total = partial_ref[0].astype(jnp.float32)
@@ -56,7 +86,23 @@
         return carry
 
     lax.fori_loop(0, queries, place, 0, unroll=8)
-    out_ref[...] = slots[...].reshape(out_ref.shape).astype(jnp.bfloat16)
+    steps = leaves.shape[0]
+    owners = packed.shape[0] // steps
+    per_step = slots.shape[0] // steps
+
+    def leave(step):
+        block = pl.ds(step * owners, owners)
+        return pltpu.make_async_copy(packed.at[block], out_ref.at[block], leaves.at[step])
+
+    for step in range(steps):
+        packed[step * owners : (step + 1) * owners] = (
+            slots[step * per_step : (step + 1) * per_step]
+            .reshape(owners, *packed.shape[1:])
+            .astype(jnp.bfloat16)
+        )
+        leave(step).start()
+    for step in range(steps):
+        leave(step).wait()
 
 
 def soft_sums(turned, passage_refs, sums):
@@ -171,8 +217,16 @@
     partial = pl.pallas_call(
         project_kernel,
         out_shape=jax.ShapeDtypeStruct((mp, queries, share, embed), jnp.bfloat16),
-        in_specs=[VMEM, VMEM],
-        out_specs=VMEM,
+        in_specs=[ANY, ANY],
+        out_specs=ANY,
+        scratch_shapes=[
+            pltpu.VMEM((queries * tokens, features), jnp.bfloat16),
+            pltpu.VMEM((features, embed), jnp.bfloat16),
+            pltpu.VMEM((mp, queries, share, embed), jnp.bfloat16),
+            pltpu.SemaphoreType.DMA((4,)),
+            pltpu.SemaphoreType.DMA((4,)),
+            pltpu.SemaphoreType.DMA,
+        ],
         name="project",
     )(query_hidden.reshape(queries * tokens, features), query_proj)
     partial = lax.all_to_all(
@@ -202,10 +256,12 @@
         pack_kernel,
         out_shape=out_vmem((dp, capacity * share, embed), jnp.bfloat16),
         in_specs=[SMEM, VMEM],
-        out_specs=VMEM,
+        out_specs=ANY,
         scratch_shapes=[
             pltpu.VMEM((queries, share, embed), jnp.float32),
             pltpu.VMEM((dp * capacity, share, embed), jnp.float32),
+            pltpu.VMEM((dp, capacity * share, embed), jnp.bfloat16),
+            pltpu.SemaphoreType.DMA((4,)),
         ],
         compiler_params=LIMIT,
         name="pack",

time: 101 us -> 101 us (level)
  no operation moved by 1% of the time
where the time goes in v7:
time: 101 us
  starting transfers between devices  42.8 us (42%)
  waiting for transfers between devices  39.5 us (39%)
  Pallas kernels  16.6 us (16%)
  local copies, waits for them, and re-layouts  1.43 us (1%)
    all_to_all x1, starting transfers between devices, scored_loss(): arrived = lax.all_to_all(outgoing, 'dp', 0, 0, tiled=True)  19 us
    all_to_all x1, waiting for transfers between devices, scored_loss(): lax.all_to_all(scores.reshape(dp * mp, 1, capacity * count), ('dp', 'mp')...  16.2 us
    all_to_all x1, waiting for transfers between devices, scored_loss(): arrived = lax.all_to_all(outgoing, 'dp', 0, 0, tiled=True)  13.9 us
    all_to_all x1, starting transfers between devices, scored_loss(): lax.all_to_all(scores.reshape(dp * mp, 1, capacity * count), ('dp', 'mp')...  10.6 us
    all_to_all x1, waiting for transfers between devices, scored_loss(): lax.all_to_all(partial.reshape(mp, queries * share, embed), 'mp', 0, 0, t...  9.33 us
    pallas_call x1, Pallas kernels, scored_loss(): pl.pallas_call(functools.partial(far_kernel, capacity), out_shape=jax.Sha...  5.7 us
    pallas_call x1, Pallas kernels, scored_loss(): pl.pallas_call(functools.partial(near_kernel, capacity), out_shape=[out_v...  5.33 us
    ppermute x1, starting transfers between devices, scored_loss(): below = lax.ppermute(own_vecs, 'mp', up)  3.94 us
  transfers between devices with their start and end apart: 6, of which 3 were waited for; matrix products, arithmetic and copies ran while one was open for 1% of the time, Pallas kernels for 9%

profile of v7, /device:TPU:1, one launch (start us, length us, event | category | flops | bytes accessed | tf_op | source)
XLA Modules:
  0.0 100.6 jit_solution(7653432618124598893)
XLA Ops:
  0.0 0.0 copy-start
  0.0 1.0 %copy-done = bf16[16,128,128]{2,1,0:T(8,128)(2,1)S(1)} copy-done((bf16[16,128,128]{2,1,0:T(8,128)(2,1)S(1)}, bf16[16,128,128]{2,1,0:T(8,128)(2,1)}, u32[]{:S(2)}) %copy-start) | copy-done | bytes 524312
  1.0 0.4 passages.1.own_ref
  1.4 3.9 %collective-permute-start = (bf16[2048,128]{1,0:T(8,128)(2,1)S(1)}, bf16[2048,128]{1,0:T(8,128)(2,1)S(1)}, u32[]{:S(2)}, u32[]{:S(2)}) collective-permute-start(bf16[2048,128]{1,0:T(8,128)(2,1)S(1)} %passages.1.own_ref), channel_id=1, source_target_pairs={{0,1},{1,2},{2,3},{3,0},{4,5},{5,6},{6,7},{7,4},{8,9},{9,10},{10,1... | collective-permute-start | bytes 1572872 | tf_op jit(solution)/shard_map/ppermute | solution.py:246
  5.3 2.5 %project.1 = bf16[4,32,8,128]{3,2,1,0:T(8,128)(2,1)} custom-call(bf16[1024,192]{1,0:T(8,128)(2,1)} %bitcast.19, bf16[192,128]{1,0:T(8,128)(2,1)} %proj_ref.1), custom_call_target="tpu_custom_call" | custom-call | tf_op jit(solution)/shard_map/project/pallas_call | solution.py:217
  7.9 0.0 copy-start.2
  7.9 3.7 %all-to-all-start = ((bf16[4,256,128]{2,1,0:T(8,128)(2,1)}), bf16[4,256,128]{2,1,0:T(8,128)(2,1)S(1)}, u32[]{:S(2)}, u32[]{:S(2)}) async-start(bf16[4,256,128]{2,1,0:T(8,128)(2,1)} %bitcast.18), calls=%async_computation | async-start | bytes 524288 | tf_op jit(solution)/shard_map/all_to_all | solution.py:232
  11.6 0.0 copy-done.2
  11.6 0.1 copy.14
  11.7 0.1 eq.15
  11.8 0.2 convert_reduce_fusion
  12.0 9.3 %all-to-all-done = bf16[4,256,128]{2,1,0:T(8,128)(2,1)S(1)} async-done(((bf16[4,256,128]{2,1,0:T(8,128)(2,1)}), bf16[4,256,128]{2,1,0:T(8,128)(2,1)S(1)}, u32[]{:S(2)}, u32[]{:S(2)}) %all-to-all-start) | async-done | bytes 262176 | tf_op jit(solution)/shard_map/all_to_all | solution.py:232
  21.4 1.7 %pack.1 = bf16[128,16,128]{2,1,0:T(8,128)(2,1)} custom-call(s32[128]{0:T(128)S(1)} %multiply_add_fusion.slot_ref, bf16[4,32,8,128]{3,2,1,0:T(8,128)(2,1)S(1)} %bitcast.15), custom_call_target="tpu_custom_call" | custom-call | tf_op jit(solution)/shard_map/pack/pallas_call | solution.py:255
  23.0 19.0 %all-to-all-start.1 = ((bf16[128,16,128]{2,1,0:T(8,128)(2,1)}), bf16[128,16,128]{2,1,0:T(8,128)(2,1)S(1)}, u32[]{:S(2)}, u32[]{:S(2)}) async-start(bf16[128,16,128]{2,1,0:T(8,128)(2,1)} %pack.1), calls=%async_computation.1 | async-start | bytes 1048576 | tf_op jit(solution)/shard_map/all_to_all | solution.py:269
  42.1 1.9 %collective-permute-start.2 = (bf16[2048,128]{1,0:T(8,128)(2,1)S(1)}, bf16[2048,128]{1,0:T(8,128)(2,1)S(1)}, u32[]{:S(2)}, u32[]{:S(2)}) collective-permute-start(bf16[2048,128]{1,0:T(8,128)(2,1)S(1)} %passages.1.own_ref), channel_id=1, source_target_pairs={{0,3},{1,0},{2,1},{3,2},{4,7},{5,4},{6,5},{7,6},{8,11},{9,8},{10,9... | collective-permute-start | bytes 1572872 | tf_op jit(solution)/shard_map/ppermute | solution.py:247
  44.0 0.0 collective-permute-done.below_ref
  44.0 3.5 %collective-permute-start.1 = (bf16[2048,128]{1,0:T(8,128)(2,1)S(1)}, bf16[2048,128]{1,0:T(8,128)(2,1)S(1)}, u32[]{:S(2)}, u32[]{:S(2)}) collective-permute-start(bf16[2048,128]{1,0:T(8,128)(2,1)S(1)} %collective-permute-done.below_ref), channel_id=1, source_target_pairs={{0,1},{1,2},{2,3},{3,0},{4,5},{5,6},{6,7},{7,4},{8,9},{9,10},{10,1... | collective-permute-start | bytes 1572872 | tf_op jit(solution)/shard_map/ppermute | solution.py:248
  47.6 13.9 %all-to-all-done.1 = bf16[128,16,128]{2,1,0:T(8,128)(2,1)S(1)} async-done(((bf16[128,16,128]{2,1,0:T(8,128)(2,1)}), bf16[128,16,128]{2,1,0:T(8,128)(2,1)S(1)}, u32[]{:S(2)}, u32[]{:S(2)}) %all-to-all-start.1) | async-done | bytes 524320 | tf_op jit(solution)/shard_map/all_to_all | solution.py:269
  61.5 5.3 %score_near.1 = (bf16[8,256,128]{2,1,0:T(8,128)(2,1)S(1)}, f32[32,256]{1,0:T(8,128)S(1)}) custom-call(bf16[2048,128]{1,0:T(8,128)(2,1)S(1)} %bitcast.13, bf16[2048,128]{1,0:T(8,128)(2,1)S(1)} %passages.1.own_ref, bf16[2048,128]{1,0:T(8,128)(2,1)S(1)} %collective-permute-done.below_ref), custom_call_target="tpu_custom_call" | custom-call | tf_op jit(solution)/shard_map/score_near/pallas_call | solution.py:271
  66.8 0.0 collective-permute-done.2.above_ref
  66.8 0.0 collective-permute-done.1.opposite_ref
  66.8 5.7 %score_far.1 = f32[512,128]{1,0:T(8,128)} custom-call(bf16[8,256,128]{2,1,0:T(8,128)(2,1)S(1)} %get-tuple-element.7.turned_ref, bf16[2048,128]{1,0:T(8,128)(2,1)S(1)} %collective-permute-done.1.opposite_ref, bf16[2048,128]{1,0:T(8,128)(2,1)S(1)} %collective-permute-done.2.above_ref, f32[32,256]{1,0:T(8,128)S(1)} %get-tuple-element.8.near_ref), custom_call_target="tpu_custom_call" | custom-call | tf_op jit(solution)/shard_map/score_far/pallas_call | solution.py:286
  72.5 0.0 copy-start.1
  72.5 10.6 %all-to-all-start.2 = ((f32[512,1,128]{2,1,0:T(1,128)}), f32[512,1,128]{2,1,0:T(1,128)S(1)}, u32[]{:S(2)}, u32[]{:S(2)}) async-start(f32[512,1,128]{2,1,0:T(1,128)} %bitcast.7), calls=%async_computation.2 | async-start | bytes 524288 | tf_op jit(solution)/shard_map/all_to_all | solution.py:298
  83.2 0.1 copy.13
  83.3 0.1 mul.22
  83.4 16.2 %all-to-all-done.2 = f32[512,1,128]{2,1,0:T(1,128)S(1)} async-done(((f32[512,1,128]{2,1,0:T(1,128)}), f32[512,1,128]{2,1,0:T(1,128)S(1)}, u32[]{:S(2)}, u32[]{:S(2)}) %all-to-all-start.2) | async-done | bytes 262176 | tf_op jit(solution)/shard_map/all_to_all | solution.py:298
  99.6 0.0 copy-done.1
  99.6 1.0 %loss.1 = f32[1,32]{1,0:T(1,128)} custom-call(s32[1,128]{1,0:T(1,128)S(1)} %bitcast_add_fusion.slot_ref, f32[512,128]{1,0:T(8,128)S(1)} %bitcast.14, f32[128,64]{1,0:T(8,128)S(1)} %bitcast.17), custom_call_target="tpu_custom_call" | custom-call | tf_op jit(solution)/shard_map/loss/pallas_call | solution.py:302
  (3 shorter events, 0.0 us)
Async XLA Ops:
  0.0 1.0 %copy-start = (bf16[16,128,128]{2,1,0:T(8,128)(2,1)S(1)}, bf16[16,128,128]{2,1,0:T(8,128)(2,1)}, u32[]{:S(2)}) copy-start(bf16[16,128,128]{2,1,0:T(8,128)(2,1)} %param.7) | copy-start | bytes 1572868
  1.4 42.6 %collective-permute-start = (bf16[2048,128]{1,0:T(8,128)(2,1)S(1)}, bf16[2048,128]{1,0:T(8,128)(2,1)S(1)}, u32[]{:S(2)}, u32[]{:S(2)}) collective-permute-start(bf16[2048,128]{1,0:T(8,128)(2,1)S(1)} %passages.1.own_ref), channel_id=1, source_target_pairs={{0,1},{1,2},{2,3},{3,0},{4,5},{5,6},{6,7},{7,4},{8,9},{9,10},{10,1... | collective-permute-start | bytes 1572872 | tf_op jit(solution)/shard_map/ppermute | solution.py:246
  7.9 3.7 %copy-start.2 = (s32[32,4]{0,1:T(4,128)S(1)}, s32[32,4]{0,1:T(4,128)}, u32[]{:S(2)}) copy-start(s32[32,4]{0,1:T(4,128)} %param.9) | copy-start | bytes 1540
  7.9 13.5 %all-to-all-start = ((bf16[4,256,128]{2,1,0:T(8,128)(2,1)}), bf16[4,256,128]{2,1,0:T(8,128)(2,1)S(1)}, u32[]{:S(2)}, u32[]{:S(2)}) async-start(bf16[4,256,128]{2,1,0:T(8,128)(2,1)} %bitcast.18), calls=%async_computation | async-start | bytes 524288 | tf_op jit(solution)/shard_map/all_to_all | solution.py:232
  23.0 38.5 %all-to-all-start.1 = ((bf16[128,16,128]{2,1,0:T(8,128)(2,1)}), bf16[128,16,128]{2,1,0:T(8,128)(2,1)S(1)}, u32[]{:S(2)}, u32[]{:S(2)}) async-start(bf16[128,16,128]{2,1,0:T(8,128)(2,1)} %pack.1), calls=%async_computation.1 | async-start | bytes 1048576 | tf_op jit(solution)/shard_map/all_to_all | solution.py:269
  42.1 24.8 %collective-permute-start.2 = (bf16[2048,128]{1,0:T(8,128)(2,1)S(1)}, bf16[2048,128]{1,0:T(8,128)(2,1)S(1)}, u32[]{:S(2)}, u32[]{:S(2)}) collective-permute-start(bf16[2048,128]{1,0:T(8,128)(2,1)S(1)} %passages.1.own_ref), channel_id=1, source_target_pairs={{0,3},{1,0},{2,1},{3,2},{4,7},{5,4},{6,5},{7,6},{8,11},{9,8},{10,9... | collective-permute-start | bytes 1572872 | tf_op jit(solution)/shard_map/ppermute | solution.py:247
  44.0 22.8 %collective-permute-start.1 = (bf16[2048,128]{1,0:T(8,128)(2,1)S(1)}, bf16[2048,128]{1,0:T(8,128)(2,1)S(1)}, u32[]{:S(2)}, u32[]{:S(2)}) collective-permute-start(bf16[2048,128]{1,0:T(8,128)(2,1)S(1)} %collective-permute-done.below_ref), channel_id=1, source_target_pairs={{0,1},{1,2},{2,3},{3,0},{4,5},{5,6},{6,7},{7,4},{8,9},{9,10},{10,1... | collective-permute-start | bytes 1572872 | tf_op jit(solution)/shard_map/ppermute | solution.py:248
  72.5 27.0 %copy-start.1 = (f32[32,4,64]{2,1,0:T(4,128)S(1)}, f32[32,4,64]{2,1,0:T(4,128)}, u32[]{:S(2)}) copy-start(f32[32,4,64]{2,1,0:T(4,128)} %param.8) | copy-start | bytes 98308
  72.5 27.0 %all-to-all-start.2 = ((f32[512,1,128]{2,1,0:T(1,128)}), f32[512,1,128]{2,1,0:T(1,128)S(1)}, u32[]{:S(2)}, u32[]{:S(2)}) async-start(f32[512,1,128]{2,1,0:T(1,128)} %bitcast.7), calls=%async_computation.2 | async-start | bytes 524288 | tf_op jit(solution)/shard_map/all_to_all | solution.py:298

commit v8 on v6

--- a/solution.py
+++ b/solution.py
@@ -30,11 +30,13 @@
 
 
 def project_kernel(hidden_ref, proj_ref, out_ref):
-    parts, queries, share, embed = out_ref.shape
+    parts, cores, queries, share, embed = out_ref.shape
     projected = jnp.dot(hidden_ref[...], proj_ref[...], preferred_element_type=jnp.float32)
     projected = projected.reshape(queries, parts, share, embed)
     for part in range(parts):
-        out_ref[part] = projected[:, part].astype(out_ref.dtype)
+        block = projected[:, part].astype(out_ref.dtype)
+        for core in range(cores):
+            out_ref[part, core] = block
 
 
 def passage_kernel(passages_ref, out_ref):
@@ -56,7 +58,8 @@
         return carry
 
     lax.fori_loop(0, queries, place, 0, unroll=8)
-    out_ref[...] = slots[...].reshape(out_ref.shape).astype(jnp.bfloat16)
+    sent = slots.shape[0] - 1
+    out_ref[...] = slots[:sent].reshape(out_ref.shape).astype(jnp.bfloat16)
 
 
 def soft_sums(turned, passage_refs, sums):
@@ -164,20 +167,31 @@
     picks = neg_blocks.shape[1]
     rows = queries * picks
     capacity = 2
+    cores = 2
+    chips = dp // cores
     share = tokens // mp
     own_count, passage_tokens, _ = passages.shape
     count = own_count * mp
 
     partial = pl.pallas_call(
         project_kernel,
-        out_shape=jax.ShapeDtypeStruct((mp, queries, share, embed), jnp.bfloat16),
+        out_shape=jax.ShapeDtypeStruct((mp, cores, queries, share, embed), jnp.bfloat16),
         in_specs=[VMEM, VMEM],
         out_specs=VMEM,
         name="project",
     )(query_hidden.reshape(queries * tokens, features), query_proj)
+    peers = [
+        [(chip * cores + core) * mp + part for part in range(mp) for core in range(cores)]
+        for chip in range(chips)
+    ]
     partial = lax.all_to_all(
-        partial.reshape(mp, queries * share, embed), "mp", 0, 0, tiled=True
-    ).reshape(mp, queries, share, embed)
+        partial.reshape(mp * cores, queries * share, embed),
+        ("dp", "mp"),
+        0,
+        0,
+        tiled=True,
+        axis_index_groups=peers,
+    ).reshape(mp, cores * queries, share, embed)
 
     own_vecs = pl.pallas_call(
         passage_kernel,
@@ -193,24 +207,40 @@
     above = lax.ppermute(own_vecs, "mp", down)
     opposite = lax.ppermute(below, "mp", up)
 
-    owners = neg_blocks.reshape(rows)
+    own_blocks = neg_blocks.reshape(rows)
+    other_blocks = lax.ppermute(own_blocks, "dp", [(place, place ^ 1) for place in range(dp)])
+    core = lax.rem(lax.axis_index("dp"), cores)
+    owners = jnp.where(
+        core == 0,
+        jnp.stack([own_blocks, other_blocks]),
+        jnp.stack([other_blocks, own_blocks]),
+    )
     row_ids = jnp.arange(rows, dtype=jnp.int32)
-    earlier = (owners[:, None] == owners[None, :]) & (row_ids[None, :] < row_ids[:, None])
-    ranks = jnp.sum(earlier.astype(jnp.int32), axis=1)
-    slot_ids = owners * capacity + ranks
+    before = row_ids[None, :] < row_ids[:, None]
+    earlier = (owners[:, :, None] == owners[:, None, :]) & before
+    ranks = jnp.sum(earlier.astype(jnp.int32), axis=2)
+    source_core = jnp.arange(cores, dtype=jnp.int32)[:, None]
+    places = (owners // cores * cores + source_core) * capacity + ranks
+    places = jnp.where(owners % cores == core, places, dp * capacity).reshape(cores * rows)
+    own_earlier = (own_blocks[:, None] == own_blocks[None, :]) & before
+    slot_ids = own_blocks * capacity + jnp.sum(own_earlier.astype(jnp.int32), axis=1)
+
     outgoing = pl.pallas_call(
         pack_kernel,
-        out_shape=out_vmem((dp, capacity * share, embed), jnp.bfloat16),
+        out_shape=jax.ShapeDtypeStruct((chips, cores * capacity * share, embed), jnp.bfloat16),
         in_specs=[SMEM, VMEM],
         out_specs=VMEM,
         scratch_shapes=[
-            pltpu.VMEM((queries, share, embed), jnp.float32),
-            pltpu.VMEM((dp * capacity, share, embed), jnp.float32),
+            pltpu.VMEM((cores * queries, share, embed), jnp.float32),
+            pltpu.VMEM((dp * capacity + 1, share, embed), jnp.float32),
         ],
         compiler_params=LIMIT,
         name="pack",
-    )(slot_ids, in_vmem(partial))
-    arrived = lax.all_to_all(outgoing, "dp", 0, 0, tiled=True)
+    )(places, in_vmem(partial))
+    same_core = [[chip * cores + core for chip in range(chips)] for core in range(cores)]
+    arrived = lax.all_to_all(
+        outgoing, "dp", 0, 0, tiled=True, axis_index_groups=same_core
+    )
 
     turned, near = pl.pallas_call(
         functools.partial(near_kernel, capacity),

time: 101 us -> 96.3 us (0.953)
  waiting for transfers between devices: 39.9 us -> 31.8 us
  starting transfers between devices: 42.8 us -> 46 us
    ppermute x0 -> x1, starting transfers between devices: none -> 8.75 us  [scored_loss(): lax.ppermute(own_blocks, 'dp', [(place, place ^ 1) for place in range(dp)])]
    all_to_all x2, waiting for transfers between devices: 23.7 us -> 15.7 us  [the longest x1 10.3 us: scored_loss(): lax.all_to_all(outgoing, 'dp', 0, 0, tiled=True, axis_index_groups=same_c...]
    all_to_all x2, starting transfers between devices: 22.8 us -> 15.5 us  [the longest x1 11.9 us: scored_loss(): lax.all_to_all(outgoing, 'dp', 0, 0, tiled=True, axis_index_groups=same_c...]
    all_to_all x1, starting transfers between devices: 10.6 us -> 13.1 us  [scored_loss(): lax.all_to_all(scores.reshape(dp * mp, 1, capacity * count), ('dp', 'mp')...]
  transfers between devices with their start and end apart: 6 -> 7, of which waited for: 3 -> 3; matrix products, arithmetic and copies ran while one was open for 1% -> 1% of each run, Pallas kernels for 9% -> 10%
where the time goes in v8:
time: 96.3 us; the launch traced here: 95.8 us
  starting transfers between devices  46 us (48%)
  waiting for transfers between devices  31.8 us (33%)
  Pallas kernels  16.4 us (17%)
  local copies, waits for them, and re-layouts  0.97 us (1%)
    all_to_all x1, waiting for transfers between devices, scored_loss(): lax.all_to_all(scores.reshape(dp * mp, 1, capacity * count), ('dp', 'mp')...  16.1 us
    all_to_all x1, starting transfers between devices, scored_loss(): lax.all_to_all(scores.reshape(dp * mp, 1, capacity * count), ('dp', 'mp')...  13.1 us
    all_to_all x1, starting transfers between devices, scored_loss(): lax.all_to_all(outgoing, 'dp', 0, 0, tiled=True, axis_index_groups=same_c...  11.9 us
    all_to_all x1, waiting for transfers between devices, scored_loss(): lax.all_to_all(outgoing, 'dp', 0, 0, tiled=True, axis_index_groups=same_c...  10.3 us
    ppermute x1, starting transfers between devices, scored_loss(): lax.ppermute(own_blocks, 'dp', [(place, place ^ 1) for place in range(dp)])  8.75 us
    pallas_call x1, Pallas kernels, scored_loss(): pl.pallas_call(functools.partial(far_kernel, capacity), out_shape=jax.Sha...  5.68 us
    all_to_all x1, waiting for transfers between devices, scored_loss(): lax.all_to_all(partial.reshape(mp * cores, queries * share, embed), ('dp'...  5.41 us
    pallas_call x1, Pallas kernels, scored_loss(): pl.pallas_call(functools.partial(near_kernel, capacity), out_shape=[out_v...  5.33 us
  transfers between devices with their start and end apart: 7, of which 3 were waited for; matrix products, arithmetic and copies ran while one was open for 1% of the time, Pallas kernels for 10%

profile of v8, /device:TPU:1, one launch (start us, length us, event | category | flops | bytes accessed | tf_op | source)
XLA Modules:
  0.0 95.8 jit_solution(15464932102474822593)
XLA Ops:
  0.0 0.8 copy.13
  0.8 0.1 eq.40
  0.9 8.7 %collective-permute-start = (s32[128]{0:T(128)S(1)}, s32[128]{0:T(128)S(1)}, u32[]{:S(2)}, u32[]{:S(2)}) collective-permute-start(s32[128]{0:T(128)S(1)} %eq.40), channel_id=1, source_target_pairs={{0,4},{4,0},{8,12},{12,8},{16,20},{20,16},{24,28},{28,24},{32,36},... | collective-permute-start | bytes 1544 | tf_op jit(solution)/shard_map/ppermute | solution.py:211
  9.6 2.1 %project.1 = bf16[4,2,32,8,128]{4,3,2,1,0:T(8,128)(2,1)} custom-call(bf16[1024,192]{1,0:T(8,128)(2,1)} %bitcast.44, bf16[192,128]{1,0:T(8,128)(2,1)} %proj_ref.1), custom_call_target="tpu_custom_call" | custom-call | tf_op jit(solution)/shard_map/project/pallas_call | solution.py:176
  11.7 0.0 copy-start
  11.7 3.6 %all-to-all-start = ((bf16[8,256,128]{2,1,0:T(8,128)(2,1)}), bf16[8,256,128]{2,1,0:T(8,128)(2,1)S(1)}, u32[]{:S(2)}, u32[]{:S(2)}) async-start(bf16[8,256,128]{2,1,0:T(8,128)(2,1)} %bitcast.43), calls=%async_computation | async-start | bytes 1048576 | tf_op jit(solution)/shard_map/all_to_all | solution.py:187
  15.3 0.0 copy-done
  15.3 0.4 passages.1.own_ref
  15.7 3.2 %collective-permute-start.1 = (bf16[2048,128]{1,0:T(8,128)(2,1)S(1)}, bf16[2048,128]{1,0:T(8,128)(2,1)S(1)}, u32[]{:S(2)}, u32[]{:S(2)}) collective-permute-start(bf16[2048,128]{1,0:T(8,128)(2,1)S(1)} %passages.1.own_ref), channel_id=1, source_target_pairs={{0,1},{1,2},{2,3},{3,0},{4,5},{5,6},{6,7},{7,4},{8,9},{9,10},{10,1... | collective-permute-start | bytes 1572872 | tf_op jit(solution)/shard_map/ppermute | solution.py:206
  19.0 0.1 reshape.135
  19.1 0.0 collective-permute-done
  19.1 0.2 convert_reduce_fusion
  19.3 5.4 %all-to-all-done = bf16[8,256,128]{2,1,0:T(8,128)(2,1)S(1)} async-done(((bf16[8,256,128]{2,1,0:T(8,128)(2,1)}), bf16[8,256,128]{2,1,0:T(8,128)(2,1)S(1)}, u32[]{:S(2)}, u32[]{:S(2)}) %all-to-all-start) | async-done | bytes 524320 | tf_op jit(solution)/shard_map/all_to_all | solution.py:187
  24.7 1.9 %pack.1 = bf16[64,32,128]{2,1,0:T(8,128)(2,1)} custom-call(s32[256]{0:T(256)S(1)} %compare_select_fusion.slot_ref, bf16[4,64,8,128]{3,2,1,0:T(8,128)(2,1)S(1)} %bitcast.39), custom_call_target="tpu_custom_call" | custom-call | tf_op jit(solution)/shard_map/pack/pallas_call | solution.py:228
  26.6 11.9 %all-to-all-start.1 = ((bf16[64,32,128]{2,1,0:T(8,128)(2,1)}), bf16[64,32,128]{2,1,0:T(8,128)(2,1)S(1)}, u32[]{:S(2)}, u32[]{:S(2)}) async-start(bf16[64,32,128]{2,1,0:T(8,128)(2,1)} %pack.1), calls=%async_computation.1 | async-start | bytes 1048576 | tf_op jit(solution)/shard_map/all_to_all | solution.py:241
  38.6 2.7 %collective-permute-start.3 = (bf16[2048,128]{1,0:T(8,128)(2,1)S(1)}, bf16[2048,128]{1,0:T(8,128)(2,1)S(1)}, u32[]{:S(2)}, u32[]{:S(2)}) collective-permute-start(bf16[2048,128]{1,0:T(8,128)(2,1)S(1)} %passages.1.own_ref), channel_id=1, source_target_pairs={{0,3},{1,0},{2,1},{3,2},{4,7},{5,4},{6,5},{7,6},{8,11},{9,8},{10,9... | collective-permute-start | bytes 1572872 | tf_op jit(solution)/shard_map/ppermute | solution.py:207
  41.3 0.0 collective-permute-done.1.below_ref
  41.3 2.7 %collective-permute-start.2 = (bf16[2048,128]{1,0:T(8,128)(2,1)S(1)}, bf16[2048,128]{1,0:T(8,128)(2,1)S(1)}, u32[]{:S(2)}, u32[]{:S(2)}) collective-permute-start(bf16[2048,128]{1,0:T(8,128)(2,1)S(1)} %collective-permute-done.1.below_ref), channel_id=1, source_target_pairs={{0,1},{1,2},{2,3},{3,0},{4,5},{5,6},{6,7},{7,4},{8,9},{9,10},{10,1... | collective-permute-start | bytes 1572872 | tf_op jit(solution)/shard_map/ppermute | solution.py:208
  44.1 10.3 %all-to-all-done.1 = bf16[64,32,128]{2,1,0:T(8,128)(2,1)S(1)} async-done(((bf16[64,32,128]{2,1,0:T(8,128)(2,1)}), bf16[64,32,128]{2,1,0:T(8,128)(2,1)S(1)}, u32[]{:S(2)}, u32[]{:S(2)}) %all-to-all-start.1) | async-done | bytes 524320 | tf_op jit(solution)/shard_map/all_to_all | solution.py:241
  54.4 5.3 %score_near.1 = (bf16[8,256,128]{2,1,0:T(8,128)(2,1)S(1)}, f32[32,256]{1,0:T(8,128)S(1)}) custom-call(bf16[2048,128]{1,0:T(8,128)(2,1)S(1)} %bitcast.38, bf16[2048,128]{1,0:T(8,128)(2,1)S(1)} %passages.1.own_ref, bf16[2048,128]{1,0:T(8,128)(2,1)S(1)} %collective-permute-done.1.below_ref), custom_call_target="tpu_custom_call" | custom-call | tf_op jit(solution)/shard_map/score_near/pallas_call | solution.py:245
  59.7 0.0 collective-permute-done.3.above_ref
  59.7 0.0 collective-permute-done.2.opposite_ref
  59.7 5.7 %score_far.1 = f32[512,128]{1,0:T(8,128)} custom-call(bf16[8,256,128]{2,1,0:T(8,128)(2,1)S(1)} %get-tuple-element.7.turned_ref, bf16[2048,128]{1,0:T(8,128)(2,1)S(1)} %collective-permute-done.2.opposite_ref, bf16[2048,128]{1,0:T(8,128)(2,1)S(1)} %collective-permute-done.3.above_ref, f32[32,256]{1,0:T(8,128)S(1)} %get-tuple-element.8.near_ref), custom_call_target="tpu_custom_call" | custom-call | tf_op jit(solution)/shard_map/score_far/pallas_call | solution.py:260
  65.4 0.0 copy-start.1
  65.4 13.1 %all-to-all-start.2 = ((f32[512,1,128]{2,1,0:T(1,128)}), f32[512,1,128]{2,1,0:T(1,128)S(1)}, u32[]{:S(2)}, u32[]{:S(2)}) async-start(f32[512,1,128]{2,1,0:T(1,128)} %bitcast.11), calls=%async_computation.2 | async-start | bytes 524288 | tf_op jit(solution)/shard_map/all_to_all | solution.py:272
  78.5 0.2 convert_reduce_fusion.1
  78.7 16.1 %all-to-all-done.2 = f32[512,1,128]{2,1,0:T(1,128)S(1)} async-done(((f32[512,1,128]{2,1,0:T(1,128)}), f32[512,1,128]{2,1,0:T(1,128)S(1)}, u32[]{:S(2)}, u32[]{:S(2)}) %all-to-all-start.2) | async-done | bytes 262176 | tf_op jit(solution)/shard_map/all_to_all | solution.py:272
  94.8 0.0 copy-done.1
  94.8 1.0 %loss.1 = f32[1,32]{1,0:T(1,128)} custom-call(s32[1,128]{1,0:T(1,128)S(1)} %bitcast_add_fusion.2.slot_ref, f32[512,128]{1,0:T(8,128)S(1)} %bitcast.40, f32[128,64]{1,0:T(8,128)S(1)} %bitcast.42), custom_call_target="tpu_custom_call" | custom-call | tf_op jit(solution)/shard_map/loss/pallas_call | solution.py:276
  (4 shorter events, 0.1 us)
Async XLA Ops:
  0.9 18.2 %collective-permute-start = (s32[128]{0:T(128)S(1)}, s32[128]{0:T(128)S(1)}, u32[]{:S(2)}, u32[]{:S(2)}) collective-permute-start(s32[128]{0:T(128)S(1)} %eq.40), channel_id=1, source_target_pairs={{0,4},{4,0},{8,12},{12,8},{16,20},{20,16},{24,28},{28,24},{32,36},... | collective-permute-start | bytes 1544 | tf_op jit(solution)/shard_map/ppermute | solution.py:211
  11.7 3.6 %copy-start = (bf16[16,128,128]{2,1,0:T(8,128)(2,1)S(1)}, bf16[16,128,128]{2,1,0:T(8,128)(2,1)}, u32[]{:S(2)}) copy-start(bf16[16,128,128]{2,1,0:T(8,128)(2,1)} %param.7) | copy-start | bytes 1572868
  11.7 13.0 %all-to-all-start = ((bf16[8,256,128]{2,1,0:T(8,128)(2,1)}), bf16[8,256,128]{2,1,0:T(8,128)(2,1)S(1)}, u32[]{:S(2)}, u32[]{:S(2)}) async-start(bf16[8,256,128]{2,1,0:T(8,128)(2,1)} %bitcast.43), calls=%async_computation | async-start | bytes 1048576 | tf_op jit(solution)/shard_map/all_to_all | solution.py:187
  15.7 25.6 %collective-permute-start.1 = (bf16[2048,128]{1,0:T(8,128)(2,1)S(1)}, bf16[2048,128]{1,0:T(8,128)(2,1)S(1)}, u32[]{:S(2)}, u32[]{:S(2)}) collective-permute-start(bf16[2048,128]{1,0:T(8,128)(2,1)S(1)} %passages.1.own_ref), channel_id=1, source_target_pairs={{0,1},{1,2},{2,3},{3,0},{4,5},{5,6},{6,7},{7,4},{8,9},{9,10},{10,1... | collective-permute-start | bytes 1572872 | tf_op jit(solution)/shard_map/ppermute | solution.py:206
  26.6 27.8 %all-to-all-start.1 = ((bf16[64,32,128]{2,1,0:T(8,128)(2,1)}), bf16[64,32,128]{2,1,0:T(8,128)(2,1)S(1)}, u32[]{:S(2)}, u32[]{:S(2)}) async-start(bf16[64,32,128]{2,1,0:T(8,128)(2,1)} %pack.1), calls=%async_computation.1 | async-start | bytes 1048576 | tf_op jit(solution)/shard_map/all_to_all | solution.py:241
  38.6 21.2 %collective-permute-start.3 = (bf16[2048,128]{1,0:T(8,128)(2,1)S(1)}, bf16[2048,128]{1,0:T(8,128)(2,1)S(1)}, u32[]{:S(2)}, u32[]{:S(2)}) collective-permute-start(bf16[2048,128]{1,0:T(8,128)(2,1)S(1)} %passages.1.own_ref), channel_id=1, source_target_pairs={{0,3},{1,0},{2,1},{3,2},{4,7},{5,4},{6,5},{7,6},{8,11},{9,8},{10,9... | collective-permute-start | bytes 1572872 | tf_op jit(solution)/shard_map/ppermute | solution.py:207
  41.3 18.4 %collective-permute-start.2 = (bf16[2048,128]{1,0:T(8,128)(2,1)S(1)}, bf16[2048,128]{1,0:T(8,128)(2,1)S(1)}, u32[]{:S(2)}, u32[]{:S(2)}) collective-permute-start(bf16[2048,128]{1,0:T(8,128)(2,1)S(1)} %collective-permute-done.1.below_ref), channel_id=1, source_target_pairs={{0,1},{1,2},{2,3},{3,0},{4,5},{5,6},{6,7},{7,4},{8,9},{9,10},{10,1... | collective-permute-start | bytes 1572872 | tf_op jit(solution)/shard_map/ppermute | solution.py:208
  65.4 29.3 %copy-start.1 = (f32[32,4,64]{2,1,0:T(4,128)S(1)}, f32[32,4,64]{2,1,0:T(4,128)}, u32[]{:S(2)}) copy-start(f32[32,4,64]{2,1,0:T(4,128)} %param.8) | copy-start | bytes 98308
  65.4 29.3 %all-to-all-start.2 = ((f32[512,1,128]{2,1,0:T(1,128)}), f32[512,1,128]{2,1,0:T(1,128)S(1)}, u32[]{:S(2)}, u32[]{:S(2)}) async-start(f32[512,1,128]{2,1,0:T(1,128)} %bitcast.11), calls=%async_computation.2 | async-start | bytes 524288 | tf_op jit(solution)/shard_map/all_to_all | solution.py:272

commit v9 on v6

--- a/solution.py
+++ b/solution.py
@@ -63,7 +63,7 @@
     share, count, _, width = sums.shape
     own = count // len(passage_refs)
     tokens = passage_refs[0].shape[0] // own
-    group = 8
+    group = 16
 
     def one_token(token, carry):
         vecs = turned[token]
@@ -239,6 +239,9 @@
         compiler_params=LIMIT,
         name="score_far",
     )(in_vmem(turned), in_vmem(opposite), in_vmem(above), in_vmem(near))
+    scores, slot_row, teacher_rows = lax.optimization_barrier(
+        (scores, slot_ids.reshape(1, rows), teacher.reshape(rows, count))
+    )
     returned = lax.all_to_all(
         scores.reshape(dp * mp, 1, capacity * count), ("dp", "mp"), 0, 0, tiled=True
     ).reshape(dp * mp, capacity * count)
@@ -251,7 +254,7 @@
         scratch_shapes=[pltpu.VMEM((rows, count), jnp.float32)],
         compiler_params=LIMIT,
         name="loss",
-    )(slot_ids.reshape(1, rows), in_vmem(returned), teacher.reshape(rows, count))
+    )(slot_row, in_vmem(returned), teacher_rows)
     return loss.reshape(queries)
 
 

time: 101 us -> 101 us (level)
  blocking collectives: 0 us -> 27.4 us
  waiting for transfers between devices: 39.9 us -> 23.5 us
  starting transfers between devices: 42.8 us -> 32.2 us
    all_to_all x0 -> x1, blocking collectives: none -> 27.4 us  [scored_loss(): lax.all_to_all(scores.reshape(dp * mp, 1, capacity * count), ('dp', 'mp')...]
    all_to_all x1 -> x0, waiting for transfers between devices: 16.2 us -> none  [scored_loss(): lax.all_to_all(scores.reshape(dp * mp, 1, capacity * count), ('dp', 'mp')...]
    all_to_all x1 -> x0, starting transfers between devices: 10.6 us -> none  [scored_loss(): lax.all_to_all(scores.reshape(dp * mp, 1, capacity * count), ('dp', 'mp')...]
  transfers between devices with their start and end apart: 6 -> 5, of which waited for: 3 -> 2; matrix products, arithmetic and copies ran while one was open for 1% -> 1% of each run, Pallas kernels for 9% -> 9%
where the time goes in v9:
time: 101 us; the launch traced here: 100 us
  starting transfers between devices  32.2 us (32%)
  blocking collectives  27.4 us (27%)
  waiting for transfers between devices  23.5 us (23%)
  Pallas kernels  15.4 us (15%)
  local copies, waits for them, and re-layouts  1.43 us (1%)
    all_to_all x1, blocking collectives, scored_loss(): lax.all_to_all(scores.reshape(dp * mp, 1, capacity * count), ('dp', 'mp')...  27.4 us
    all_to_all x1, starting transfers between devices, scored_loss(): arrived = lax.all_to_all(outgoing, 'dp', 0, 0, tiled=True)  19 us
    all_to_all x1, waiting for transfers between devices, scored_loss(): arrived = lax.all_to_all(outgoing, 'dp', 0, 0, tiled=True)  13.7 us
    all_to_all x1, waiting for transfers between devices, scored_loss(): lax.all_to_all(partial.reshape(mp, queries * share, embed), 'mp', 0, 0, t...  9.76 us
    pallas_call x1, Pallas kernels, scored_loss(): pl.pallas_call(functools.partial(near_kernel, capacity), out_shape=[out_v...  5.31 us
    pallas_call x1, Pallas kernels, scored_loss(): pl.pallas_call(functools.partial(far_kernel, capacity), out_shape=jax.Sha...  5.04 us
    ppermute x1, starting transfers between devices, scored_loss(): below = lax.ppermute(own_vecs, 'mp', up)  3.94 us
    all_to_all x1, starting transfers between devices, scored_loss(): lax.all_to_all(partial.reshape(mp, queries * share, embed), 'mp', 0, 0, t...  3.86 us
  transfers between devices with their start and end apart: 5, of which 2 were waited for; matrix products, arithmetic and copies ran while one was open for 1% of the time, Pallas kernels for 9%

profile of v9, /device:TPU:1, one launch (start us, length us, event | category | flops | bytes accessed | tf_op | source)
XLA Modules:
  0.0 100.3 jit_solution(10784989915591195706)
XLA Ops:
  0.0 0.0 copy-start
  0.0 1.0 %copy-done = bf16[16,128,128]{2,1,0:T(8,128)(2,1)S(1)} copy-done((bf16[16,128,128]{2,1,0:T(8,128)(2,1)S(1)}, bf16[16,128,128]{2,1,0:T(8,128)(2,1)}, u32[]{:S(2)}) %copy-start) | copy-done | bytes 524312
  1.0 0.4 passages.1.own_ref
  1.4 3.9 %collective-permute-start = (bf16[2048,128]{1,0:T(8,128)(2,1)S(1)}, bf16[2048,128]{1,0:T(8,128)(2,1)S(1)}, u32[]{:S(2)}, u32[]{:S(2)}) collective-permute-start(bf16[2048,128]{1,0:T(8,128)(2,1)S(1)} %passages.1.own_ref), channel_id=1, source_target_pairs={{0,1},{1,2},{2,3},{3,0},{4,5},{5,6},{6,7},{7,4},{8,9},{9,10},{10,1... | collective-permute-start | bytes 1572872 | tf_op jit(solution)/shard_map/ppermute | solution.py:192
  5.3 2.0 %project.1 = bf16[4,32,8,128]{3,2,1,0:T(8,128)(2,1)} custom-call(bf16[1024,192]{1,0:T(8,128)(2,1)} %bitcast.20, bf16[192,128]{1,0:T(8,128)(2,1)} %proj_ref.1), custom_call_target="tpu_custom_call" | custom-call | tf_op jit(solution)/shard_map/project/pallas_call | solution.py:171
  7.4 0.0 copy-start.2
  7.4 3.9 %all-to-all-start = ((bf16[4,256,128]{2,1,0:T(8,128)(2,1)}), bf16[4,256,128]{2,1,0:T(8,128)(2,1)S(1)}, u32[]{:S(2)}, u32[]{:S(2)}) async-start(bf16[4,256,128]{2,1,0:T(8,128)(2,1)} %bitcast.19), calls=%async_computation | async-start | bytes 524288 | tf_op jit(solution)/shard_map/all_to_all | solution.py:178
  11.2 0.0 copy-done.2
  11.2 0.1 copy.13
  11.3 0.1 reshape.52
  11.4 0.2 convert_reduce_fusion
  11.6 9.8 %all-to-all-done = bf16[4,256,128]{2,1,0:T(8,128)(2,1)S(1)} async-done(((bf16[4,256,128]{2,1,0:T(8,128)(2,1)}), bf16[4,256,128]{2,1,0:T(8,128)(2,1)S(1)}, u32[]{:S(2)}, u32[]{:S(2)}) %all-to-all-start) | async-done | bytes 262176 | tf_op jit(solution)/shard_map/all_to_all | solution.py:178
  21.4 1.7 %pack.1 = bf16[128,16,128]{2,1,0:T(8,128)(2,1)} custom-call(s32[128]{0:T(128)S(1)} %multiply_add_fusion.slot_ref, bf16[4,32,8,128]{3,2,1,0:T(8,128)(2,1)S(1)} %bitcast.16), custom_call_target="tpu_custom_call" | custom-call | tf_op jit(solution)/shard_map/pack/pallas_call | solution.py:201
  23.1 19.0 %all-to-all-start.1 = ((bf16[128,16,128]{2,1,0:T(8,128)(2,1)}), bf16[128,16,128]{2,1,0:T(8,128)(2,1)S(1)}, u32[]{:S(2)}, u32[]{:S(2)}) async-start(bf16[128,16,128]{2,1,0:T(8,128)(2,1)} %pack.1), calls=%async_computation.1 | async-start | bytes 1048576 | tf_op jit(solution)/shard_map/all_to_all | solution.py:213
  42.1 1.9 %collective-permute-start.2 = (bf16[2048,128]{1,0:T(8,128)(2,1)S(1)}, bf16[2048,128]{1,0:T(8,128)(2,1)S(1)}, u32[]{:S(2)}, u32[]{:S(2)}) collective-permute-start(bf16[2048,128]{1,0:T(8,128)(2,1)S(1)} %passages.1.own_ref), channel_id=1, source_target_pairs={{0,3},{1,0},{2,1},{3,2},{4,7},{5,4},{6,5},{7,6},{8,11},{9,8},{10,9... | collective-permute-start | bytes 1572872 | tf_op jit(solution)/shard_map/ppermute | solution.py:193
  44.0 0.0 collective-permute-done.below_ref
  44.0 3.5 %collective-permute-start.1 = (bf16[2048,128]{1,0:T(8,128)(2,1)S(1)}, bf16[2048,128]{1,0:T(8,128)(2,1)S(1)}, u32[]{:S(2)}, u32[]{:S(2)}) collective-permute-start(bf16[2048,128]{1,0:T(8,128)(2,1)S(1)} %collective-permute-done.below_ref), channel_id=1, source_target_pairs={{0,1},{1,2},{2,3},{3,0},{4,5},{5,6},{6,7},{7,4},{8,9},{9,10},{10,1... | collective-permute-start | bytes 1572872 | tf_op jit(solution)/shard_map/ppermute | solution.py:194
  47.6 0.1 copy.14
  47.6 0.1 mul.24
  47.8 13.7 %all-to-all-done.1 = bf16[128,16,128]{2,1,0:T(8,128)(2,1)S(1)} async-done(((bf16[128,16,128]{2,1,0:T(8,128)(2,1)}), bf16[128,16,128]{2,1,0:T(8,128)(2,1)S(1)}, u32[]{:S(2)}, u32[]{:S(2)}) %all-to-all-start.1) | async-done | bytes 524320 | tf_op jit(solution)/shard_map/all_to_all | solution.py:213
  61.5 5.3 %score_near.1 = (bf16[8,256,128]{2,1,0:T(8,128)(2,1)S(1)}, f32[32,256]{1,0:T(8,128)S(1)}) custom-call(bf16[2048,128]{1,0:T(8,128)(2,1)S(1)} %bitcast.13, bf16[2048,128]{1,0:T(8,128)(2,1)S(1)} %passages.1.own_ref, bf16[2048,128]{1,0:T(8,128)(2,1)S(1)} %collective-permute-done.below_ref), custom_call_target="tpu_custom_call" | custom-call | tf_op jit(solution)/shard_map/score_near/pallas_call | solution.py:215
  66.8 0.0 collective-permute-done.2.above_ref
  66.8 0.0 collective-permute-done.1.opposite_ref
  66.8 5.0 %score_far.1 = f32[512,128]{1,0:T(8,128)S(1)} custom-call(bf16[8,256,128]{2,1,0:T(8,128)(2,1)S(1)} %get-tuple-element.10.turned_ref, bf16[2048,128]{1,0:T(8,128)(2,1)S(1)} %collective-permute-done.1.opposite_ref, bf16[2048,128]{1,0:T(8,128)(2,1)S(1)} %collective-permute-done.2.above_ref, f32[32,256]{1,0:T(8,128)S(1)} %get-tuple-element.11.near_ref), custom_call_target="tpu_custom_call" | custom-call | tf_op jit(solution)/shard_map/score_far/pallas_call | solution.py:230
  71.9 0.0 copy-start.1
  71.9 27.4 %all_to_all.15 = f32[512,1,128]{2,1,0:T(1,128)S(1)} all-to-all(f32[512,1,128]{2,1,0:T(1,128)S(1)} %bitcast.14), channel_id=1, replica_groups=mesh['dp'=128,'mp'=4] {'dp','mp'}, dimensions={0} | all-to-all | bytes 524288 | tf_op jit(solution)/shard_map/all_to_all | solution.py:245
  99.3 0.0 copy-done.1
  99.3 1.0 %loss.1 = f32[1,32]{1,0:T(1,128)} custom-call(s32[1,128]{1,0:T(1,128)S(1)} %bitcast_add_fusion.slot_ref, f32[512,128]{1,0:T(8,128)S(1)} %bitcast.15, f32[128,64]{1,0:T(8,128)S(1)} %bitcast.18), custom_call_target="tpu_custom_call" | custom-call | tf_op jit(solution)/shard_map/loss/pallas_call | solution.py:249
  (3 shorter events, 0.0 us)
Async XLA Ops:
  0.0 1.0 %copy-start = (bf16[16,128,128]{2,1,0:T(8,128)(2,1)S(1)}, bf16[16,128,128]{2,1,0:T(8,128)(2,1)}, u32[]{:S(2)}) copy-start(bf16[16,128,128]{2,1,0:T(8,128)(2,1)} %param.7) | copy-start | bytes 1572868
  1.4 42.6 %collective-permute-start = (bf16[2048,128]{1,0:T(8,128)(2,1)S(1)}, bf16[2048,128]{1,0:T(8,128)(2,1)S(1)}, u32[]{:S(2)}, u32[]{:S(2)}) collective-permute-start(bf16[2048,128]{1,0:T(8,128)(2,1)S(1)} %passages.1.own_ref), channel_id=1, source_target_pairs={{0,1},{1,2},{2,3},{3,0},{4,5},{5,6},{6,7},{7,4},{8,9},{9,10},{10,1... | collective-permute-start | bytes 1572872 | tf_op jit(solution)/shard_map/ppermute | solution.py:192
  7.4 3.9 %copy-start.2 = (s32[32,4]{0,1:T(4,128)S(1)}, s32[32,4]{0,1:T(4,128)}, u32[]{:S(2)}) copy-start(s32[32,4]{0,1:T(4,128)} %param.9) | copy-start | bytes 1540
  7.4 14.0 %all-to-all-start = ((bf16[4,256,128]{2,1,0:T(8,128)(2,1)}), bf16[4,256,128]{2,1,0:T(8,128)(2,1)S(1)}, u32[]{:S(2)}, u32[]{:S(2)}) async-start(bf16[4,256,128]{2,1,0:T(8,128)(2,1)} %bitcast.19), calls=%async_computation | async-start | bytes 524288 | tf_op jit(solution)/shard_map/all_to_all | solution.py:178
  23.1 38.4 %all-to-all-start.1 = ((bf16[128,16,128]{2,1,0:T(8,128)(2,1)}), bf16[128,16,128]{2,1,0:T(8,128)(2,1)S(1)}, u32[]{:S(2)}, u32[]{:S(2)}) async-start(bf16[128,16,128]{2,1,0:T(8,128)(2,1)} %pack.1), calls=%async_computation.1 | async-start | bytes 1048576 | tf_op jit(solution)/shard_map/all_to_all | solution.py:213
  42.1 24.7 %collective-permute-start.2 = (bf16[2048,128]{1,0:T(8,128)(2,1)S(1)}, bf16[2048,128]{1,0:T(8,128)(2,1)S(1)}, u32[]{:S(2)}, u32[]{:S(2)}) collective-permute-start(bf16[2048,128]{1,0:T(8,128)(2,1)S(1)} %passages.1.own_ref), channel_id=1, source_target_pairs={{0,3},{1,0},{2,1},{3,2},{4,7},{5,4},{6,5},{7,6},{8,11},{9,8},{10,9... | collective-permute-start | bytes 1572872 | tf_op jit(solution)/shard_map/ppermute | solution.py:193
  44.0 22.8 %collective-permute-start.1 = (bf16[2048,128]{1,0:T(8,128)(2,1)S(1)}, bf16[2048,128]{1,0:T(8,128)(2,1)S(1)}, u32[]{:S(2)}, u32[]{:S(2)}) collective-permute-start(bf16[2048,128]{1,0:T(8,128)(2,1)S(1)} %collective-permute-done.below_ref), channel_id=1, source_target_pairs={{0,1},{1,2},{2,3},{3,0},{4,5},{5,6},{6,7},{7,4},{8,9},{9,10},{10,1... | collective-permute-start | bytes 1572872 | tf_op jit(solution)/shard_map/ppermute | solution.py:194
  71.9 27.4 %copy-start.1 = (f32[32,4,64]{2,1,0:T(4,128)S(1)}, f32[32,4,64]{2,1,0:T(4,128)}, u32[]{:S(2)}) copy-start(f32[32,4,64]{2,1,0:T(4,128)} %param.8) | copy-start | bytes 98308
